TPU v7x, 32 devices: a whole 2x2x4 slice. The times are simulated.
32 devices in a mesh: cfg: 2 (over y), slab: 4 (over z), tile: 2 (over x), spin: 2 (over core).
Axes of the slice: x: 2, y: 2, z: 4, core: 2. Of those that a mesh axis runs over, the one named last changes fastest.
Arguments:
- eigenvectors: bfloat16 [4, 2, 3, 8, 1024, 256], P(('cfg', 'tile'), None, None, 'slab', 'spin'), parts along dimension 0, may hold values from -6 to 6
- gauge_links: float32 [4, 2, 3, 3, 8, 1024], P(('cfg', 'tile'), None, None, None, 'slab', 'spin'), parts along dimension 0, may hold values from -2.5 to 2.5
- momenta: int32 [2, 3], replicated, may hold values from -2 to 2
- displacement: int32 [2], replicated, may hold values from 1 to 2, as said below
- slice_pairs: int32 [4, 2], P('tile'), may hold values from 0 to 1, as said below
- perambulators: bfloat16 [8, 2, 1024, 1024], P(('cfg', 'tile'), None, 'spin', 'slab'), parts along dimension 0, may hold values from -6 to 6
Outputs:
- meson_blocks: bfloat16 [8, 2, 1024, 1024], P(('cfg', 'tile'), None, 'spin', 'slab'), parts along dimension 0
There are 2 independent parts, one for each index of `cfg`. A program takes and returns all parts, laid end to end along the dimension named above; an argument that names none is the same for every part. Nothing has to cross between parts.
Inputs may be any that keep to these rules, and one draw needn't show every extreme that they name: `displacement`: the entries are 1 and 2 in some order, so one elemental is displaced forward and the other backward. `slice_pairs`: column 0 is the sink slice and column 1 the source slice; every pair of slices in 0 to 1 appears exactly once.
All inputs are finite; a program needn't handle non-finite values.
Results may differ from a plain program's by a relative error of at most 0.008.
Values may be sent and summed in bfloat16 or wider, within the bound.
No kernel may reach another device: no remote copies, remote signals or barrier semaphores. Data moves between devices by JAX's collectives and lax.ppermute only.
A program may use at most 64 MiB of HBM per device.

v0:
```python
import functools
import math

import jax
import jax.numpy as jnp
from jax import lax
from jax.experimental import pallas as pl
from jax.experimental.pallas import tpu as pltpu
from jax.sharding import PartitionSpec as P


NS = 4
LY = 32
LZ = 32
COLORS = 3
COEFS = 24


def shift(x, axis, by):
    count = lax.axis_size(axis)
    return lax.ppermute(x, axis, [(i, (i + by) % count) for i in range(count)])


def swap(x, axis, distance):
    count = lax.axis_size(axis)
    return lax.ppermute(x, axis, [(i, i ^ distance) for i in range(count)])


def vmem():
    return pl.BlockSpec(memory_space=pltpu.VMEM)


def smem():
    return pl.BlockSpec(memory_space=pltpu.SMEM)


def edge_kernel(fields_ref, edge_ref, held, taken, given):
    spots = [(part, c) for part in range(2) for c in range(COLORS)]

    def take(at, spot):
        return pltpu.make_async_copy(
            fields_ref.at[spot[0], spot[1], 0], held.at[at], taken.at[at]
        )

    def give(at, spot):
        return pltpu.make_async_copy(held.at[at], edge_ref.at[spot[0], spot[1]], given.at[at])

    for at, spot in enumerate(spots):
        take(at, spot).start()
    for at, spot in enumerate(spots):
        take(at, spot).wait()
        give(at, spot).start()
    for at, spot in enumerate(spots):
        give(at, spot).wait()


def field_kernel(meta_ref, fields_ref, coefs_ref, inner_ref, outer_ref, rotated):
    planes, block, vectors = fields_ref.shape[2:]
    tile = 16

    @pl.when(pl.program_id(0) == 0)
    def _():
        inner_ref[...] = jnp.zeros_like(inner_ref)

    for plane in range(planes):

        def rows_step(step, carry):
            rows = pl.ds(pl.multiple_of(step * tile, tile), tile)
            coefs = coefs_ref[plane, rows, :]

            def coef(which):
                return coefs[:, which : which + 1]

            real = [fields_ref[0, c, plane, rows, :].astype(jnp.float32) for c in range(COLORS)]
            imag = [fields_ref[1, c, plane, rows, :].astype(jnp.float32) for c in range(COLORS)]
            for out in range(COLORS):
                local_real = None
                for c in range(COLORS):
                    link_real = coef(COLORS * c + out)
                    link_imag = coef(COLORS * COLORS + COLORS * c + out)
                    term_real = link_real * real[c] + link_imag * imag[c]
                    term_imag = link_real * imag[c] - link_imag * real[c]
                    local_real = term_real if local_real is None else local_real + term_real
                    local_imag = term_imag if c == 0 else local_imag + term_imag
                for slot in range(2):
                    turn_real = coef(2 * COLORS * COLORS + 2 * slot)
                    turn_imag = coef(2 * COLORS * COLORS + 2 * slot + 1)
                    at = 2 * slot * vectors
                    rotated[out, rows, at : at + vectors] = (
                        turn_real * local_real - turn_imag * local_imag
                    ).astype(jnp.bfloat16)
                    at += vectors
                    rotated[out, rows, at : at + vectors] = (
                        turn_real * local_imag + turn_imag * local_real
                    ).astype(jnp.bfloat16)
            return carry

        lax.fori_loop(0, block // tile, rows_step, 0)
        for c in range(COLORS):
            if plane + 1 < planes:
                ahead = jnp.concatenate(
                    [fields_ref[0, c, plane + 1], fields_ref[1, c, plane + 1]], axis=1
                )
                inner_ref[...] += lax.dot_general(
                    rotated[c], ahead, (((0,), (0,)), ((), ())), preferred_element_type=jnp.float32
                )
            else:
                outer_ref[c] = rotated[c].T


def rim_kernel(normalize, meta_ref, outer_ref, inner_ref, rim_ref, keep_ref, send_ref):
    vectors = rim_ref.shape[-1]
    for slot, out in ((1, send_ref), (0, keep_ref)):
        at = 2 * slot * vectors
        totals = []
        for part in range(2):
            total = inner_ref[at : at + 2 * vectors, part * vectors : (part + 1) * vectors]
            for c in range(COLORS):
                total = total + jnp.dot(
                    outer_ref[c, at : at + 2 * vectors, :],
                    rim_ref[part, c],
                    preferred_element_type=jnp.float32,
                )
            totals.append(total)
        real = totals[0][:vectors] + totals[1][vectors:]
        imag = totals[0][vectors:] - totals[1][:vectors]
        out[meta_ref[1]] = (real * normalize).astype(out.dtype)
        out[1 - meta_ref[1]] = (imag * normalize).astype(out.dtype)


def deal_kernel(share, meta_ref, perams_ref, move_ref, *outs):
    spin_rows = perams_ref.shape[2]
    for by, out in enumerate(outs):
        item = (meta_ref[4] ^ by) // share
        for part in range(2):
            out[part] = jnp.dot(
                perams_ref[item // spin_rows, part, lax.rem(item, spin_rows)],
                move_ref[...],
                preferred_element_type=jnp.float32,
            ).astype(jnp.bfloat16)


def block_kernel(slab, share, meta_ref, *refs):
    parts = refs[:4]
    chunks = refs[4 : 4 + slab]
    outs = refs[4 + slab : -2]
    table_ref, turned_ref = refs[-2:]
    vectors = parts[0].shape[0]
    per = vectors // slab
    core, parity, place = meta_ref[0], meta_ref[1], meta_ref[4]
    found = [piece[...].astype(jnp.float32) for piece in parts]

    def pick(elem):
        mine = core == elem
        first = jnp.where(mine, found[0], found[2])
        second = jnp.where(mine, found[1], found[3])
        real = jnp.where(parity == 0, first, second)
        imag = jnp.where(parity == 0, second, first)
        forward = meta_ref[5 + elem] == 1
        return (
            jnp.where(forward, real, real.T),
            jnp.where(forward, -imag, imag.T),
        )

    real, imag = pick(0)
    real, imag = real.astype(jnp.bfloat16), imag.astype(jnp.bfloat16)
    matrix = jnp.concatenate(
        [jnp.concatenate([real, -imag], axis=1), jnp.concatenate([imag, real], axis=1)], axis=0
    )
    columns = []
    for spin in range(NS):
        at = spin * per
        columns += [
            chunk[...].reshape(2 * vectors, NS * per)[:, at : at + per] for chunk in chunks
        ]
    spread = jnp.concatenate(columns, axis=1)
    left = jnp.dot(matrix, spread, preferred_element_type=jnp.float32).astype(jnp.bfloat16)
    width = vectors // share
    count = slab // share
    lane = lax.broadcasted_iota(jnp.int32, (per, width), 1) // per
    for part, value in enumerate(pick(1)):
        table_ref[...] = value
        for chunk in range(slab):
            row = pl.multiple_of((place ^ chunk) * per, per)
            rows = table_ref[pl.ds(row, per), :]
            turned = rows[:, :width]
            for group in range(1, share):
                turned = jnp.where(
                    lax.rem(place, share) == group,
                    rows[:, group * width : (group + 1) * width],
                    turned,
                )
            step = 1
            while step < count:
                down = pltpu.roll(turned, step * per, 1)
                up = pltpu.roll(turned, width - step * per, 1)
                moved = jnp.where((lane // step) % 2 == 0, up, down)
                turned = jnp.where((place // (share * step)) % 2 == 1, moved, turned)
                step *= 2
            turned_ref[chunk * per : (chunk + 1) * per, part * width : (part + 1) * width] = (
                turned
            )
    right = turned_ref[...].astype(jnp.bfloat16)
    reals, imags = [], []
    for spin in range(NS):
        both = jnp.dot(
            left[:, spin * vectors : (spin + 1) * vectors],
            right,
            preferred_element_type=jnp.float32,
        )
        reals.append(both[:vectors, :width] - both[vectors:, width:])
        imags.append(both[:vectors, width:] + both[vectors:, :width])
    for which, out in enumerate(outs):
        at = which * per
        for part, values in ((0, reals), (1, imags)):
            out[part] = jnp.concatenate(
                [value[:, at : at + per] for value in values], axis=1
            ).astype(jnp.bfloat16)


def join_kernel(count, place_ref, move_ref, *refs):
    out_ref = refs[-1]
    for which in range(count):

        @pl.when(pl.program_id(0) == which)
        def _():
            for part in range(2):
                out_ref[0, part] = jnp.dot(
                    refs[which][part], move_ref[...], preferred_element_type=jnp.float32
                ).astype(jnp.bfloat16)


def body(eigenvectors, gauge_links, momenta, displacement, slice_pairs, perambulators):
    bf16, f32, i32 = jnp.bfloat16, jnp.float32, jnp.int32
    fields = eigenvectors[0]
    links = gauge_links[0]
    planes, sites, vectors = fields.shape[2:]
    slab, tiles = lax.axis_size("slab"), lax.axis_size("tile")
    z, t, core = lax.axis_index("slab"), lax.axis_index("tile"), lax.axis_index("spin")
    z, t, core = z.astype(i32), t.astype(i32), core.astype(i32)
    lattice_x = planes * slab
    normalize = 1.0 / math.sqrt(3072 * lattice_x * LY * LZ)

    edge = pl.pallas_call(
        edge_kernel,
        in_specs=[pl.BlockSpec(memory_space=pl.ANY)],
        out_specs=pl.BlockSpec(memory_space=pl.ANY),
        out_shape=jax.ShapeDtypeStruct((2, COLORS, sites, vectors), bf16),
        scratch_shapes=[
            pltpu.VMEM((2 * COLORS, sites, vectors), bf16),
            pltpu.SemaphoreType.DMA((2 * COLORS,)),
            pltpu.SemaphoreType.DMA((2 * COLORS,)),
        ],
        compiler_params=pltpu.CompilerParams(vmem_limit_bytes=60 << 20),
        name="edge",
    )(fields)
    rim = shift(edge, "slab", -1)

    elems = jnp.stack([core, 1 - core])
    forward = (displacement[elems] == 1).astype(i32)
    turns = momenta[elems]
    x_site = z * planes + jnp.arange(planes, dtype=i32)[None, :] + (1 - forward)[:, None]
    yz_site = core * sites + jnp.arange(sites, dtype=i32)
    wave_x = jnp.mod(turns[:, 0:1] * x_site, lattice_x)
    wave_y = jnp.mod(turns[:, 1:2] * (yz_site // LZ)[None, :], LY)
    wave_z = jnp.mod(turns[:, 2:3] * (yz_site % LZ)[None, :], LZ)
    number = (
        wave_x[:, :, None] * (LY * LZ)
        + (wave_y * (lattice_x * LZ) + wave_z * (lattice_x * LY))[:, None, :]
    )
    angle = number.astype(f32) * (2.0 * math.pi / (lattice_x * LY * LZ))
    sign = (2 * forward - 1).astype(f32)[:, None, None]
    turn = jnp.stack([jnp.cos(angle), jnp.sin(angle) * sign], axis=1)
    coefs = jnp.concatenate(
        [
            links.reshape(2 * COLORS * COLORS, planes, sites),
            turn.reshape(4, planes, sites),
            jnp.zeros((COEFS - 2 * COLORS * COLORS - 4, planes, sites), f32),
        ]
    ).transpose(1, 2, 0)

    parity = lax.rem(z, 2)
    pairs = perambulators.shape[0]
    spin_rows = perambulators.shape[2] // vectors
    width = perambulators.shape[3]
    items = pairs * spin_rows
    share = slab // items
    assert share * items == slab and (share * spin_rows) % 2 == 0
    chosen = slice_pairs[z // share // spin_rows]
    meta = jnp.stack([core, parity, chosen[0], chosen[1], z, displacement[0], displacement[1]])

    per = width // NS
    column = jnp.arange(width, dtype=i32)
    target = (column % NS) * per + column // NS
    gather_spins = (target[:, None] == column[None, :]).astype(bf16)
    spread_spins = (target[None, :] == column[:, None]).astype(bf16)
    count = slab // share

    def places(first, last):
        found = lax.rem(z, count) ^ jnp.arange(first, last, dtype=i32)
        return jnp.concatenate([found // spin_rows, lax.rem(found, spin_rows)])

    cuts = (0, count // 2, count)
    wanted = lax.rem(t - chosen[core] + tiles, tiles)
    spots = [places(first, last) for first, last in zip(cuts[:-1], cuts[1:])]
    meta, coefs, gather_spins, spread_spins, wanted, spots = lax.optimization_barrier(
        (meta, coefs, gather_spins, spread_spins, wanted, spots)
    )

    block = min(sites, 256)
    inner, outer = pl.pallas_call(
        field_kernel,
        grid=(sites // block,),
        in_specs=[
            smem(),
            pl.BlockSpec((2, COLORS, planes, block, vectors), lambda i: (0, 0, 0, i, 0)),
            pl.BlockSpec((planes, block, COEFS), lambda i: (0, i, 0)),
        ],
        out_specs=[
            pl.BlockSpec((4 * vectors, 2 * vectors), lambda i: (0, 0)),
            pl.BlockSpec((COLORS, 4 * vectors, block), lambda i: (0, 0, i)),
        ],
        out_shape=[
            jax.ShapeDtypeStruct((4 * vectors, 2 * vectors), f32),
            jax.ShapeDtypeStruct((COLORS, 4 * vectors, sites), bf16),
        ],
        scratch_shapes=[pltpu.VMEM((COLORS, block, 4 * vectors), bf16)],
        compiler_params=pltpu.CompilerParams(vmem_limit_bytes=15 << 20),
        name="fields",
    )(meta, fields, coefs)

    blocks = pl.pallas_call(
        functools.partial(deal_kernel, share),
        in_specs=[smem(), vmem(), vmem()],
        out_specs=[vmem()] * slab,
        out_shape=[jax.ShapeDtypeStruct((2, vectors, width), bf16)] * slab,
        compiler_params=pltpu.CompilerParams(vmem_limit_bytes=8 << 20),
        name="deal",
    )(meta, perambulators.reshape(pairs, 2, spin_rows, vectors, width), gather_spins)
    outer, *blocks = lax.optimization_barrier((outer, *blocks))

    keep, send = pl.pallas_call(
        functools.partial(rim_kernel, normalize),
        in_specs=[smem()] + [vmem()] * 3,
        out_specs=[vmem()] * 2,
        out_shape=[
            jax.ShapeDtypeStruct((2, vectors, vectors), f32),
            jax.ShapeDtypeStruct((2, vectors, vectors), bf16),
        ],
        compiler_params=pltpu.CompilerParams(vmem_limit_bytes=14 << 20),
        name="rim",
    )(meta, outer, inner, rim)

    half = keep + swap(send, "spin", 1).astype(f32)
    quarter = half[0] + swap(half[1].astype(bf16), "slab", 1).astype(f32)
    distance = 2
    while distance < slab:
        quarter = quarter + swap(quarter.astype(bf16), "slab", distance).astype(f32)
        distance *= 2
    quarter = quarter.astype(bf16)
    own = quarter
    for by in range(1, tiles):
        own = jnp.where(wanted == by, shift(quarter, "tile", by), own)
    pair = swap(own, "slab", 1)
    own_core = swap(own, "spin", 1)
    pair_core = swap(pair, "spin", 1)

    chunks = [blocks[0]]
    for by in range(1, slab):
        chunks.append(swap(blocks[by], "slab", by))

    pieces = pl.pallas_call(
        functools.partial(block_kernel, slab, share),
        in_specs=[smem()] + [vmem()] * (4 + slab),
        out_specs=[vmem()] * count,
        out_shape=[jax.ShapeDtypeStruct((2, vectors, width), bf16)] * count,
        scratch_shapes=[
            pltpu.VMEM((vectors, vectors), f32),
            pltpu.VMEM((vectors, 2 * vectors // share), f32),
        ],
        compiler_params=pltpu.CompilerParams(vmem_limit_bytes=14 << 20),
        name="blocks",
    )(meta, own, pair, own_core, pair_core, *chunks)

    arrived = []
    for which, piece in enumerate(pieces):
        route = [(s, (s % share) * count + ((s // share) ^ which)) for s in range(slab)]
        if any(a != b for a, b in route):
            piece = lax.ppermute(piece, "slab", route)
        arrived.append(piece)

    result = []
    for first, last, spot in zip(cuts[:-1], cuts[1:], spots):
        span = last - first
        result = [
            pl.pallas_call(
                functools.partial(join_kernel, span),
                grid_spec=pltpu.PrefetchScalarGridSpec(
                    num_scalar_prefetch=1,
                    grid=(span,),
                    in_specs=[vmem()] * (1 + span)
                    + [pl.BlockSpec(memory_space=pl.ANY)] * len(result),
                    out_specs=pl.BlockSpec(
                        (1, 2, vectors, width),
                        lambda i, at, span=span: (at[i], 0, at[span + i], 0),
                    ),
                ),
                out_shape=jax.ShapeDtypeStruct(perambulators.shape, bf16),
                input_output_aliases={2 + span: 0} if result else {},
                compiler_params=pltpu.CompilerParams(vmem_limit_bytes=6 << 20),
                name="join",
            )(spot, spread_spins, *arrived[first:last], *result)
        ]
    return result[0]


def solution(mesh):
    return jax.shard_map(
        body,
        mesh=mesh,
        in_specs=(
            P(("cfg", "tile"), None, None, "slab", "spin", None),
            P(("cfg", "tile"), None, None, None, "slab", "spin"),
            P(),
            P(),
            P("tile", None),
            P(("cfg", "tile"), None, "spin", "slab"),
        ),
        out_specs=P(("cfg", "tile"), None, "spin", "slab"),
        check_vma=False,
    )
```

profile of v0, /device:TPU:0, one launch (start us, length us, event | category | flops | bytes accessed | tf_op | source)
XLA Modules:
  0.0 115.7 jit_solution(18111736599862790916)
XLA Ops:
  0.0 0.0 copy-start
  0.0 0.0 copy-start.5
  0.0 0.0 copy-start.3
  0.0 2.3 %edge.1 = bf16[2,3,512,256]{3,2,1,0:T(8,128)(2,1)} custom-call(bf16[2,3,2,512,256]{4,3,2,1,0:T(8,128)(2,1)} %bitcast.26), custom_call_target="tpu_custom_call" | custom-call | tf_op jit(solution)/shard_map/edge/pallas_call | solution.py:244
  2.3 0.0 copy-start.1
  2.3 5.1 %collective-permute-start = (bf16[2,3,512,256]{3,2,1,0:T(8,128)(2,1)}, bf16[2,3,512,256]{3,2,1,0:T(8,128)(2,1)}, u32[]{:S(2)}, u32[]{:S(2)}) collective-permute-start(bf16[2,3,512,256]{3,2,1,0:T(8,128)(2,1)} %edge.1), channel_id=1, source_target_pairs={{0,12},{4,0},{8,4},{12,8},{1,13},{5,1},{9,5},{13,9},{2,14},{6,2},{... | collective-permute-start | bytes 4718600 | tf_op jit(solution)/shard_map/ppermute | solution.py:21
  7.4 0.0 copy-done.5
  7.4 0.6 dynamic_slice.7
  8.6 0.1 fusion.22
  8.7 0.0 copy-done.3
  8.7 0.6 gather_fusion.1
  9.3 0.0 copy-done
  9.3 0.6 gather_fusion
  9.9 0.2 slice_reduce_fusion.2
  10.1 0.1 fusion.17
  10.2 0.1 fusion.8
  10.3 0.2 fusion.5
  10.5 1.0 copy.15
  11.5 0.0 copy-done.4
  11.5 1.0 copy.14
  12.5 0.1 pad.6.clone
  12.6 0.6 fusion.23
  13.3 1.4 %stack.30.meta_ref = s32[7]{0:T(128)S(1)} concatenate(s32[1]{0:T(128)} %bitcast, s32[1]{0:T(128)} %bitcast.1, s32[1]{0:T(128)} %bitcast.2, s32[1]{0:T(128)} %bitcast.3, s32[1]{0:T(128)} %bitcast.4, s32[2]{0:T(128)S(1)} %copy-done.3), dimensions={0} | concatenate | bytes 56 | tf_op jit(solution)/shard_map/stack | solution.py:290
  14.7 0.1 pad_add_fusion.1.place_ref
  14.7 0.1 pad_add_fusion.place_ref
  14.8 0.1 fusion.2
  14.9 1.4 %maximum_bitcast_fusion.coefs_ref = f32[2,512,24]{2,1,0:T(8,128)S(1)} fusion(f32[4,2,512]{0,2,1:T(8,128)} %copy.15, f32[18,2,512]{0,2,1:T(8,128)} %copy.14, f32[24]{0:T(128)S(1)} %pad.6.clone), kind=kLoop, calls=%fused_computation.2 | loop fusion | flops 49152 | bytes 188512 | tf_op jit(solution)/shard_map/transpose | solution.py:280
  16.3 0.0 copy-start.2
  16.4 0.0 copy-done.1
  16.4 13.9 %fields.1 = (f32[1024,512]{1,0:T(8,128)S(1)}, bf16[3,1024,512]{2,1,0:T(8,128)(2,1)S(1)}) custom-call(s32[7]{0:T(128)S(1)} %stack.30.meta_ref, bf16[2,3,2,512,256]{4,3,2,1,0:T(8,128)(2,1)S(1)} %bitcast.27, f32[2,512,24]{2,1,0:T(8,128)S(1)} %maximum_bitcast_fusion.coefs_ref), custom_call_target="tpu_custom_call" | custom-call | tf_op jit(solution)/shard_map/fields/pallas_call | solution.py:311
  30.3 0.0 copy-done.2
  30.3 1.0 deal.1
  31.3 10.1 %collective-permute-done.rim_ref = bf16[2,3,512,256]{3,2,1,0:T(8,128)(2,1)} collective-permute-done((bf16[2,3,512,256]{3,2,1,0:T(8,128)(2,1)}, bf16[2,3,512,256]{3,2,1,0:T(8,128)(2,1)}, u32[]{:S(2)}, u32[]{:S(2)}) %collective-permute-start) | collective-permute-done | bytes 1572896 | tf_op jit(solution)/shard_map/ppermute | solution.py:21
  41.4 3.3 %rim.1 = (f32[2,256,256]{2,1,0:T(8,128)S(1)}, bf16[2,256,256]{2,1,0:T(8,128)(2,1)S(1)}) custom-call(s32[7]{0:T(128)S(1)} %stack.30.meta_ref, bf16[3,1024,512]{2,1,0:T(8,128)(2,1)S(1)} %get-tuple-element.40.outer_ref, f32[1024,512]{1,0:T(8,128)S(1)} %get-tuple-element.41.inner_ref, bf16[2,3,512,256]{3,2,1,0:T(8,128)(2,1)} %collective-permute-done.rim_ref), custom_call_target="tpu_custom_call" | custom-call | tf_op jit(solution)/shard_map/rim/pallas_call | solution.py:342
  44.7 0.1 collective-permute-start.1
  44.8 1.5 %collective-permute-done.1 = bf16[2,256,256]{2,1,0:T(8,128)(2,1)S(1)} collective-permute-done((bf16[2,256,256]{2,1,0:T(8,128)(2,1)S(1)}, bf16[2,256,256]{2,1,0:T(8,128)(2,1)S(1)}, u32[]{:S(2)}, u32[]{:S(2)}) %collective-permute-start.1) | collective-permute-done | bytes 262176 | tf_op jit(solution)/shard_map/ppermute | solution.py:26
  46.3 0.1 convert_add_fusion
  46.4 0.5 collective-permute-start.2
  46.9 5.1 %collective-permute-done.2 = bf16[256,256]{1,0:T(8,128)(2,1)S(1)} collective-permute-done((bf16[256,256]{1,0:T(8,128)(2,1)S(1)}, bf16[256,256]{1,0:T(8,128)(2,1)S(1)}, u32[]{:S(2)}, u32[]{:S(2)}) %collective-permute-start.2) | collective-permute-done | bytes 131104 | tf_op jit(solution)/shard_map/ppermute | solution.py:26
  52.0 3.2 %collective-permute-start.3 = (bf16[256,256]{1,0:T(8,128)(2,1)S(1)}, bf16[256,256]{1,0:T(8,128)(2,1)S(1)}, u32[]{:S(2)}, u32[]{:S(2)}) collective-permute-start(bf16[256,256]{1,0:T(8,128)(2,1)S(1)} %fusion.3), channel_id=1, source_target_pairs={{0,8},{4,12},{8,0},{12,4},{1,9},{5,13},{9,1},{13,5},{2,10},{6,14},... | collective-permute-start | bytes 393224 | tf_op jit(solution)/shard_map/ppermute | solution.py:26
  55.2 6.0 %collective-permute-done.3 = bf16[256,256]{1,0:T(8,128)(2,1)S(1)} collective-permute-done((bf16[256,256]{1,0:T(8,128)(2,1)S(1)}, bf16[256,256]{1,0:T(8,128)(2,1)S(1)}, u32[]{:S(2)}, u32[]{:S(2)}) %collective-permute-start.3) | collective-permute-done | bytes 131104 | tf_op jit(solution)/shard_map/ppermute | solution.py:26
  61.3 1.6 %collective-permute-start.4 = (bf16[256,256]{1,0:T(8,128)(2,1)S(1)}, bf16[256,256]{1,0:T(8,128)(2,1)S(1)}, u32[]{:S(2)}, u32[]{:S(2)}) collective-permute-start(bf16[256,256]{1,0:T(8,128)(2,1)S(1)} %add_convert_fusion), channel_id=1, source_target_pairs={{0,2},{2,0},{1,3},{3,1},{4,6},{6,4},{5,7},{7,5},{8,10},{10,8},{9,1... | collective-permute-start | bytes 393224 | tf_op jit(solution)/shard_map/ppermute | solution.py:21
  62.8 0.7 collective-permute-start.8
  63.5 3.4 %collective-permute-start.9 = (bf16[2,256,256]{2,1,0:T(8,128)(2,1)S(1)}, bf16[2,256,256]{2,1,0:T(8,128)(2,1)S(1)}, u32[]{:S(2)}, u32[]{:S(2)}) collective-permute-start(bf16[2,256,256]{2,1,0:T(8,128)(2,1)S(1)} %get-tuple-element.46), channel_id=1, source_target_pairs={{0,8},{4,12},{8,0},{12,4},{1,9},{5,13},{9,1},{13,5},{2,10},{6,14},... | collective-permute-start | bytes 786440 | tf_op jit(solution)/shard_map/ppermute | solution.py:26
  66.9 0.3 collective-permute-start.10
  67.2 0.0 collective-permute-done.4
  67.2 0.3 collective-permute-start.5
  67.6 0.0 collective-permute-start.6
  67.6 15.6 %collective-permute-done.5.refs_1_ = bf16[256,256]{1,0:T(8,128)(2,1)S(1)} collective-permute-done((bf16[256,256]{1,0:T(8,128)(2,1)S(1)}, bf16[256,256]{1,0:T(8,128)(2,1)S(1)}, u32[]{:S(2)}, u32[]{:S(2)}) %collective-permute-start.5) | collective-permute-done | bytes 131104 | tf_op jit(solution)/shard_map/ppermute | solution.py:26
  83.1 0.0 collective-permute-start.7
  83.1 0.0 collective-permute-done.8.refs_5_
  83.1 2.2 %collective-permute-done.9.refs_6_ = bf16[2,256,256]{2,1,0:T(8,128)(2,1)S(1)} collective-permute-done((bf16[2,256,256]{2,1,0:T(8,128)(2,1)S(1)}, bf16[2,256,256]{2,1,0:T(8,128)(2,1)S(1)}, u32[]{:S(2)}, u32[]{:S(2)}) %collective-permute-start.9) | collective-permute-done | bytes 262176 | tf_op jit(solution)/shard_map/ppermute | solution.py:26
  85.3 0.0 collective-permute-done.10.refs_7_
  85.3 0.0 collective-permute-done.6.refs_2_
  85.3 0.0 collective-permute-done.7.refs_3_
  85.3 2.2 %blocks.1 = (bf16[2,256,256]{2,1,0:T(8,128)(2,1)S(1)}, bf16[2,256,256]{2,1,0:T(8,128)(2,1)S(1)}, bf16[2,256,256]{2,1,0:T(8,128)(2,1)S(1)}, bf16[2,256,256]{2,1,0:T(8,128)(2,1)S(1)}) custom-call(s32[7]{0:T(128)S(1)} %stack.30.meta_ref, bf16[256,256]{1,0:T(8,128)(2,1)S(1)} %broadcast_select_fusion.refs_0_, ...), custom_call_target="tpu_custom_call" | custom-call | tf_op jit(solution)/shard_map/blocks/pallas_call | solution.py:372
  87.5 5.1 %collective-permute-start.13 = (bf16[2,256,256]{2,1,0:T(8,128)(2,1)S(1)}, bf16[2,256,256]{2,1,0:T(8,128)(2,1)S(1)}, u32[]{:S(2)}, u32[]{:S(2)}) collective-permute-start(bf16[2,256,256]{2,1,0:T(8,128)(2,1)S(1)} %get-tuple-element.52), channel_id=1, source_target_pairs={{0,4},{4,0},{8,12},{12,8},{1,5},{5,1},{9,13},{13,9},{2,6},{6,2},{1... | collective-permute-start | bytes 786440 | tf_op jit(solution)/shard_map/ppermute | solution.py:389
  92.6 1.0 collective-permute-start.11
  93.6 1.4 %collective-permute-start.12 = (bf16[2,256,256]{2,1,0:T(8,128)(2,1)S(1)}, bf16[2,256,256]{2,1,0:T(8,128)(2,1)S(1)}, u32[]{:S(2)}, u32[]{:S(2)}) collective-permute-start(bf16[2,256,256]{2,1,0:T(8,128)(2,1)S(1)} %get-tuple-element.49), channel_id=1, source_target_pairs={{0,12},{4,8},{8,4},{12,0},{1,13},{5,9},{9,5},{13,1},{2,14},{6,10},... | collective-permute-start | bytes 786440 | tf_op jit(solution)/shard_map/ppermute | solution.py:389
  95.0 7.3 %collective-permute-done.13.refs_1_ = bf16[2,256,256]{2,1,0:T(8,128)(2,1)S(1)} collective-permute-done((bf16[2,256,256]{2,1,0:T(8,128)(2,1)S(1)}, bf16[2,256,256]{2,1,0:T(8,128)(2,1)S(1)}, u32[]{:S(2)}, u32[]{:S(2)}) %collective-permute-start.13) | collective-permute-done | bytes 262176 | tf_op jit(solution)/shard_map/ppermute | solution.py:389
  102.4 1.8 %join.2.refs_2_ = bf16[2,2,512,256]{3,2,1,0:T(8,128)(2,1)} custom-call(s32[4]{0:T(128)S(1)} %pad_add_fusion.place_ref, bf16[256,256]{1,0:T(8,128)(2,1)S(1)} %get-tuple-element.30.move_ref, bf16[2,256,256]{2,1,0:T(8,128)(2,1)S(1)} %get-tuple-element.51.refs_0_, bf16[2,256,256]{2,1,0:T(8,128)(2,1)S(1)} %collective-permute-done.13.refs_1_), custom_call_target="tpu_custom_call" | custom-call | tf_op jit(solution)/shard_map/join/pallas_call | solution.py:396
  104.1 9.8 %collective-permute-done.11.refs_0_ = bf16[2,256,256]{2,1,0:T(8,128)(2,1)S(1)} collective-permute-done((bf16[2,256,256]{2,1,0:T(8,128)(2,1)S(1)}, bf16[2,256,256]{2,1,0:T(8,128)(2,1)S(1)}, u32[]{:S(2)}, u32[]{:S(2)}) %collective-permute-start.11) | collective-permute-done | bytes 262176 | tf_op jit(solution)/shard_map/ppermute | solution.py:389
  113.9 0.0 collective-permute-done.12.refs_1_
  113.9 1.8 %join.3 = bf16[2,2,512,256]{3,2,1,0:T(8,128)(2,1)} custom-call(s32[4]{0:T(128)S(1)} %pad_add_fusion.1.place_ref, bf16[256,256]{1,0:T(8,128)(2,1)S(1)} %get-tuple-element.30.move_ref, bf16[2,256,256]{2,1,0:T(8,128)(2,1)S(1)} %collective-permute-done.11.refs_0_, ...), custom_call_target="tpu_custom_call", output_to_operand_aliasing={{}: (4, {})} | custom-call | tf_op jit(solution)/shard_map/join/pallas_call | solution.py:396
  (14 shorter events, 0.2 us)
Async XLA Ops:
  0.0 9.3 %copy-start = (s32[2,3]{1,0:T(2,128)S(1)}, s32[2,3]{1,0:T(2,128)}, u32[]{:S(2)}) copy-start(s32[2,3]{1,0:T(2,128)} %param.8) | copy-start | bytes 76
  0.0 7.4 %copy-start.5 = (s32[2,2]{1,0:T(2,128)S(1)}, s32[2,2]{1,0:T(2,128)}, u32[]{:S(2)}) copy-start(s32[2,2]{1,0:T(2,128)} %param.10) | copy-start | bytes 52
  0.0 8.7 %copy-start.3 = (s32[2]{0:T(128)S(1)}, s32[2]{0:T(128)}, u32[]{:S(2)}) copy-start(s32[2]{0:T(128)} %param.9) | copy-start | bytes 28
  0.0 11.5 %copy-start.4 = (f32[1,2,3,3,2,512]{5,4,3,2,1,0:T(2,128)S(1)}, f32[1,2,3,3,2,512]{5,4,3,2,1,0:T(2,128)}, u32[]{:S(2)}) copy-start(f32[1,2,3,3,2,512]{5,4,3,2,1,0:T(2,128)} %param.7) | copy-start | bytes 221188
  2.3 14.1 %copy-start.1 = (bf16[1,2,3,2,512,256]{5,4,3,2,1,0:T(8,128)(2,1)S(1)}, bf16[1,2,3,2,512,256]{5,4,3,2,1,0:T(8,128)(2,1)}, u32[]{:S(2)}) copy-start(bf16[1,2,3,2,512,256]{5,4,3,2,1,0:T(8,128)(2,1)} %param.6) | copy-start | bytes 9437188
  2.3 39.1 %collective-permute-start = (bf16[2,3,512,256]{3,2,1,0:T(8,128)(2,1)}, bf16[2,3,512,256]{3,2,1,0:T(8,128)(2,1)}, u32[]{:S(2)}, u32[]{:S(2)}) collective-permute-start(bf16[2,3,512,256]{3,2,1,0:T(8,128)(2,1)} %edge.1), channel_id=1, source_target_pairs={{0,12},{4,0},{8,4},{12,8},{1,13},{5,1},{9,5},{13,9},{2,14},{6,2},{... | collective-permute-start | bytes 4718600 | tf_op jit(solution)/shard_map/ppermute | solution.py:21
  16.3 14.0 %copy-start.2 = (bf16[2,2,512,256]{3,2,1,0:T(8,128)(2,1)S(1)}, bf16[2,2,512,256]{3,2,1,0:T(8,128)(2,1)}, u32[]{:S(2)}) copy-start(bf16[2,2,512,256]{3,2,1,0:T(8,128)(2,1)} %param.11) | copy-start | bytes 3145732
  44.7 1.6 %collective-permute-start.1 = (bf16[2,256,256]{2,1,0:T(8,128)(2,1)S(1)}, bf16[2,256,256]{2,1,0:T(8,128)(2,1)S(1)}, u32[]{:S(2)}, u32[]{:S(2)}) collective-permute-start(bf16[2,256,256]{2,1,0:T(8,128)(2,1)S(1)} %get-tuple-element.43), channel_id=1, source_target_pairs={{0,1},{1,0},{2,3},{3,2},{4,5},{5,4},{6,7},{7,6},{8,9},{9,8},{10,11... | collective-permute-start | bytes 786440 | tf_op jit(solution)/shard_map/ppermute | solution.py:26
  46.4 5.6 %collective-permute-start.2 = (bf16[256,256]{1,0:T(8,128)(2,1)S(1)}, bf16[256,256]{1,0:T(8,128)(2,1)S(1)}, u32[]{:S(2)}, u32[]{:S(2)}) collective-permute-start(bf16[256,256]{1,0:T(8,128)(2,1)S(1)} %fusion.4), channel_id=1, source_target_pairs={{0,4},{4,0},{8,12},{12,8},{1,5},{5,1},{9,13},{13,9},{2,6},{6,2},{1... | collective-permute-start | bytes 393224 | tf_op jit(solution)/shard_map/ppermute | solution.py:26
  52.0 9.2 %collective-permute-start.3 = (bf16[256,256]{1,0:T(8,128)(2,1)S(1)}, bf16[256,256]{1,0:T(8,128)(2,1)S(1)}, u32[]{:S(2)}, u32[]{:S(2)}) collective-permute-start(bf16[256,256]{1,0:T(8,128)(2,1)S(1)} %fusion.3), channel_id=1, source_target_pairs={{0,8},{4,12},{8,0},{12,4},{1,9},{5,13},{9,1},{13,5},{2,10},{6,14},... | collective-permute-start | bytes 393224 | tf_op jit(solution)/shard_map/ppermute | solution.py:26
  61.3 5.9 %collective-permute-start.4 = (bf16[256,256]{1,0:T(8,128)(2,1)S(1)}, bf16[256,256]{1,0:T(8,128)(2,1)S(1)}, u32[]{:S(2)}, u32[]{:S(2)}) collective-permute-start(bf16[256,256]{1,0:T(8,128)(2,1)S(1)} %add_convert_fusion), channel_id=1, source_target_pairs={{0,2},{2,0},{1,3},{3,1},{4,6},{6,4},{5,7},{7,5},{8,10},{10,8},{9,1... | collective-permute-start | bytes 393224 | tf_op jit(solution)/shard_map/ppermute | solution.py:21
  62.8 20.3 %collective-permute-start.8 = (bf16[2,256,256]{2,1,0:T(8,128)(2,1)S(1)}, bf16[2,256,256]{2,1,0:T(8,128)(2,1)S(1)}, u32[]{:S(2)}, u32[]{:S(2)}) collective-permute-start(bf16[2,256,256]{2,1,0:T(8,128)(2,1)S(1)} %get-tuple-element.45), channel_id=1, source_target_pairs={{0,4},{4,0},{8,12},{12,8},{1,5},{5,1},{9,13},{13,9},{2,6},{6,2},{1... | collective-permute-start | bytes 786440 | tf_op jit(solution)/shard_map/ppermute | solution.py:26
  63.5 21.8 %collective-permute-start.9 = (bf16[2,256,256]{2,1,0:T(8,128)(2,1)S(1)}, bf16[2,256,256]{2,1,0:T(8,128)(2,1)S(1)}, u32[]{:S(2)}, u32[]{:S(2)}) collective-permute-start(bf16[2,256,256]{2,1,0:T(8,128)(2,1)S(1)} %get-tuple-element.46), channel_id=1, source_target_pairs={{0,8},{4,12},{8,0},{12,4},{1,9},{5,13},{9,1},{13,5},{2,10},{6,14},... | collective-permute-start | bytes 786440 | tf_op jit(solution)/shard_map/ppermute | solution.py:26
  66.9 18.4 %collective-permute-start.10 = (bf16[2,256,256]{2,1,0:T(8,128)(2,1)S(1)}, bf16[2,256,256]{2,1,0:T(8,128)(2,1)S(1)}, u32[]{:S(2)}, u32[]{:S(2)}) collective-permute-start(bf16[2,256,256]{2,1,0:T(8,128)(2,1)S(1)} %get-tuple-element.47), channel_id=1, source_target_pairs={{0,12},{4,8},{8,4},{12,0},{1,13},{5,9},{9,5},{13,1},{2,14},{6,10},... | collective-permute-start | bytes 786440 | tf_op jit(solution)/shard_map/ppermute | solution.py:26
  67.2 15.9 %collective-permute-start.5 = (bf16[256,256]{1,0:T(8,128)(2,1)S(1)}, bf16[256,256]{1,0:T(8,128)(2,1)S(1)}, u32[]{:S(2)}, u32[]{:S(2)}) collective-permute-start(bf16[256,256]{1,0:T(8,128)(2,1)S(1)} %broadcast_select_fusion.refs_0_), channel_id=1, source_target_pairs={{0,4},{4,0},{8,12},{12,8},{1,5},{5,1},{9,13},{13,9},{2,6},{6,2},{1... | collective-permute-start | bytes 393224 | tf_op jit(solution)/shard_map/ppermute | solution.py:26
  67.6 17.7 %collective-permute-start.6 = (bf16[256,256]{1,0:T(8,128)(2,1)S(1)}, bf16[256,256]{1,0:T(8,128)(2,1)S(1)}, u32[]{:S(2)}, u32[]{:S(2)}) collective-permute-start(bf16[256,256]{1,0:T(8,128)(2,1)S(1)} %broadcast_select_fusion.refs_0_), channel_id=1, source_target_pairs={{0,1},{1,0},{2,3},{3,2},{4,5},{5,4},{6,7},{7,6},{8,9},{9,8},{10,11... | collective-permute-start | bytes 393224 | tf_op jit(solution)/shard_map/ppermute | solution.py:26
  83.1 2.2 %collective-permute-start.7 = (bf16[256,256]{1,0:T(8,128)(2,1)S(1)}, bf16[256,256]{1,0:T(8,128)(2,1)S(1)}, u32[]{:S(2)}, u32[]{:S(2)}) collective-permute-start(bf16[256,256]{1,0:T(8,128)(2,1)S(1)} %collective-permute-done.5.refs_1_), channel_id=1, source_target_pairs={{0,1},{1,0},{2,3},{3,2},{4,5},{5,4},{6,7},{7,6},{8,9},{9,8},{10,11... | collective-permute-start | bytes 393224 | tf_op jit(solution)/shard_map/ppermute | solution.py:26
  87.5 14.8 %collective-permute-start.13 = (bf16[2,256,256]{2,1,0:T(8,128)(2,1)S(1)}, bf16[2,256,256]{2,1,0:T(8,128)(2,1)S(1)}, u32[]{:S(2)}, u32[]{:S(2)}) collective-permute-start(bf16[2,256,256]{2,1,0:T(8,128)(2,1)S(1)} %get-tuple-element.52), channel_id=1, source_target_pairs={{0,4},{4,0},{8,12},{12,8},{1,5},{5,1},{9,13},{13,9},{2,6},{6,2},{1... | collective-permute-start | bytes 786440 | tf_op jit(solution)/shard_map/ppermute | solution.py:389
  92.6 21.3 %collective-permute-start.11 = (bf16[2,256,256]{2,1,0:T(8,128)(2,1)S(1)}, bf16[2,256,256]{2,1,0:T(8,128)(2,1)S(1)}, u32[]{:S(2)}, u32[]{:S(2)}) collective-permute-start(bf16[2,256,256]{2,1,0:T(8,128)(2,1)S(1)} %get-tuple-element.48), channel_id=1, source_target_pairs={{0,8},{4,12},{8,0},{12,4},{1,9},{5,13},{9,1},{13,5},{2,10},{6,14},... | collective-permute-start | bytes 786440 | tf_op jit(solution)/shard_map/ppermute | solution.py:389
  93.6 20.3 %collective-permute-start.12 = (bf16[2,256,256]{2,1,0:T(8,128)(2,1)S(1)}, bf16[2,256,256]{2,1,0:T(8,128)(2,1)S(1)}, u32[]{:S(2)}, u32[]{:S(2)}) collective-permute-start(bf16[2,256,256]{2,1,0:T(8,128)(2,1)S(1)} %get-tuple-element.49), channel_id=1, source_target_pairs={{0,12},{4,8},{8,4},{12,0},{1,13},{5,9},{9,5},{13,1},{2,14},{6,10},... | collective-permute-start | bytes 786440 | tf_op jit(solution)/shard_map/ppermute | solution.py:389
where the time goes:
time: 117 us; the launch traced here: 116 us
  waiting for transfers between devices  57.6 us (49%)
  Pallas kernels  26.2 us (22%)
  starting transfers between devices  22.7 us (19%)
  local copies, waits for them, and re-layouts  6.15 us (5%)
  other arithmetic  2.32 us (2%)
    ppermute x9, waiting for transfers between devices, swap(): return lax.ppermute(x, axis, [(i, i ^ distance) for i in range(count)])  30.4 us
    ppermute x3, waiting for transfers between devices, body(): piece = lax.ppermute(piece, 'slab', route)  17.1 us
    pallas_call x1, Pallas kernels, body(): pl.pallas_call(field_kernel, grid=(sites // block,), in_specs=[smem(), pl...  13.9 us
    ppermute x2, waiting for transfers between devices, shift(): return lax.ppermute(x, axis, [(i, (i + by) % count) for i in range(count)])  10.1 us
    ppermute x9, starting transfers between devices, swap(): return lax.ppermute(x, axis, [(i, i ^ distance) for i in range(count)])  8.5 us
    ppermute x3, starting transfers between devices, body(): piece = lax.ppermute(piece, 'slab', route)  7.5 us
    ppermute x2, starting transfers between devices, shift(): return lax.ppermute(x, axis, [(i, (i + by) % count) for i in range(count)])  6.67 us
    pallas_call x2, Pallas kernels, body(): pl.pallas_call(functools.partial(join_kernel, span), grid_spec=pltpu.Pref...  3.52 us
  transfers between devices with their start and end apart: 14, of which 8 were waited for; matrix products, arithmetic and copies ran while one was open for 7% of the time, Pallas kernels for 14%

commit v1 on v0

--- a/solution.py
+++ b/solution.py
@@ -34,24 +34,20 @@
     return pl.BlockSpec(memory_space=pltpu.SMEM)
 
 
-def edge_kernel(fields_ref, edge_ref, held, taken, given):
+def edge_kernel(fields_ref, most_ref, last_ref, taken):
     spots = [(part, c) for part in range(2) for c in range(COLORS)]
-
-    def take(at, spot):
-        return pltpu.make_async_copy(
-            fields_ref.at[spot[0], spot[1], 0], held.at[at], taken.at[at]
+    copies = [
+        pltpu.make_async_copy(
+            fields_ref.at[part, c, 0],
+            most_ref.at[at] if at + 1 < len(spots) else last_ref,
+            taken.at[at],
         )
-
-    def give(at, spot):
-        return pltpu.make_async_copy(held.at[at], edge_ref.at[spot[0], spot[1]], given.at[at])
-
-    for at, spot in enumerate(spots):
-        take(at, spot).start()
-    for at, spot in enumerate(spots):
-        take(at, spot).wait()
-        give(at, spot).start()
-    for at, spot in enumerate(spots):
-        give(at, spot).wait()
+        for at, (part, c) in enumerate(spots)
+    ]
+    for copy in copies:
+        copy.start()
+    for copy in copies:
+        copy.wait()
 
 
 def field_kernel(meta_ref, fields_ref, coefs_ref, inner_ref, outer_ref, rotated):
@@ -108,22 +104,35 @@
                 outer_ref[c] = rotated[c].T
 
 
-def rim_kernel(normalize, meta_ref, outer_ref, inner_ref, rim_ref, keep_ref, send_ref):
-    vectors = rim_ref.shape[-1]
-    for slot, out in ((1, send_ref), (0, keep_ref)):
+def most_kernel(outer_ref, inner_ref, most_ref, total_ref):
+    vectors = most_ref.shape[-1]
+    for slot in range(2):
         at = 2 * slot * vectors
         totals = []
         for part in range(2):
             total = inner_ref[at : at + 2 * vectors, part * vectors : (part + 1) * vectors]
-            for c in range(COLORS):
+            for c in range(COLORS - part):
                 total = total + jnp.dot(
                     outer_ref[c, at : at + 2 * vectors, :],
-                    rim_ref[part, c],
+                    most_ref[COLORS * part + c],
                     preferred_element_type=jnp.float32,
                 )
             totals.append(total)
-        real = totals[0][:vectors] + totals[1][vectors:]
-        imag = totals[0][vectors:] - totals[1][:vectors]
+        total_ref[slot, 0] = totals[0][:vectors] + totals[1][vectors:]
+        total_ref[slot, 1] = totals[0][vectors:] - totals[1][:vectors]
+
+
+def last_kernel(normalize, meta_ref, outer_ref, total_ref, last_ref, keep_ref, send_ref):
+    vectors = last_ref.shape[-1]
+    for slot, out in ((1, send_ref), (0, keep_ref)):
+        at = 2 * slot * vectors
+        both = jnp.dot(
+            outer_ref[0, at : at + 2 * vectors, :],
+            last_ref[...],
+            preferred_element_type=jnp.float32,
+        )
+        real = total_ref[slot, 0] + both[vectors:]
+        imag = total_ref[slot, 1] - both[:vectors]
         out[meta_ref[1]] = (real * normalize).astype(out.dtype)
         out[1 - meta_ref[1]] = (imag * normalize).astype(out.dtype)
 
@@ -241,20 +250,20 @@
     lattice_x = planes * slab
     normalize = 1.0 / math.sqrt(3072 * lattice_x * LY * LZ)
 
-    edge = pl.pallas_call(
+    most, last = pl.pallas_call(
         edge_kernel,
         in_specs=[pl.BlockSpec(memory_space=pl.ANY)],
-        out_specs=pl.BlockSpec(memory_space=pl.ANY),
-        out_shape=jax.ShapeDtypeStruct((2, COLORS, sites, vectors), bf16),
-        scratch_shapes=[
-            pltpu.VMEM((2 * COLORS, sites, vectors), bf16),
-            pltpu.SemaphoreType.DMA((2 * COLORS,)),
-            pltpu.SemaphoreType.DMA((2 * COLORS,)),
-        ],
-        compiler_params=pltpu.CompilerParams(vmem_limit_bytes=60 << 20),
+        out_specs=[vmem()] * 2,
+        out_shape=[
+            jax.ShapeDtypeStruct((2 * COLORS - 1, sites, vectors), bf16),
+            jax.ShapeDtypeStruct((sites, vectors), bf16),
+        ],
+        scratch_shapes=[pltpu.SemaphoreType.DMA((2 * COLORS,))],
+        compiler_params=pltpu.CompilerParams(vmem_limit_bytes=62 << 20),
         name="edge",
     )(fields)
-    rim = shift(edge, "slab", -1)
+    most = shift(most, "slab", -1)
+    last = shift(last, "slab", -1)
 
     elems = jnp.stack([core, 1 - core])
     forward = (displacement[elems] == 1).astype(i32)
@@ -301,7 +310,10 @@
         return jnp.concatenate([found // spin_rows, lax.rem(found, spin_rows)])
 
     cuts = (0, count // 2, count)
-    wanted = lax.rem(t - chosen[core] + tiles, tiles)
+    wanted = [
+        lax.rem(t - slice_pairs[place // share // spin_rows, core] + tiles, tiles)
+        for place in (z, z ^ 2)
+    ]
     spots = [places(first, last) for first, last in zip(cuts[:-1], cuts[1:])]
     meta, coefs, gather_spins, spread_spins, wanted, spots = lax.optimization_barrier(
         (meta, coefs, gather_spins, spread_spins, wanted, spots)
@@ -339,28 +351,44 @@
     )(meta, perambulators.reshape(pairs, 2, spin_rows, vectors, width), gather_spins)
     outer, *blocks = lax.optimization_barrier((outer, *blocks))
 
+    total = pl.pallas_call(
+        most_kernel,
+        in_specs=[vmem()] * 3,
+        out_specs=vmem(),
+        out_shape=jax.ShapeDtypeStruct((2, 2, vectors, vectors), f32),
+        compiler_params=pltpu.CompilerParams(vmem_limit_bytes=14 << 20),
+        name="most",
+    )(outer, inner, most)
     keep, send = pl.pallas_call(
-        functools.partial(rim_kernel, normalize),
-        in_specs=[smem()] + [vmem()] * 3,
+        functools.partial(last_kernel, normalize),
+        grid=(1,),
+        in_specs=[
+            smem(),
+            pl.BlockSpec((1, 4 * vectors, sites), lambda i: (COLORS - 1, 0, 0)),
+            vmem(),
+            vmem(),
+        ],
         out_specs=[vmem()] * 2,
         out_shape=[
             jax.ShapeDtypeStruct((2, vectors, vectors), f32),
             jax.ShapeDtypeStruct((2, vectors, vectors), bf16),
         ],
-        compiler_params=pltpu.CompilerParams(vmem_limit_bytes=14 << 20),
-        name="rim",
-    )(meta, outer, inner, rim)
+        compiler_params=pltpu.CompilerParams(vmem_limit_bytes=10 << 20),
+        name="last",
+    )(meta, outer, total, last)
 
     half = keep + swap(send, "spin", 1).astype(f32)
     quarter = half[0] + swap(half[1].astype(bf16), "slab", 1).astype(f32)
-    distance = 2
+    distance = 4
     while distance < slab:
         quarter = quarter + swap(quarter.astype(bf16), "slab", distance).astype(f32)
         distance *= 2
-    quarter = quarter.astype(bf16)
-    own = quarter
+    own, theirs = quarter, quarter.astype(bf16)
     for by in range(1, tiles):
-        own = jnp.where(wanted == by, shift(quarter, "tile", by), own)
+        moved = shift(quarter.astype(bf16), "tile", by)
+        own = jnp.where(wanted[0] == by, moved.astype(f32), own)
+        theirs = jnp.where(wanted[1] == by, moved, theirs)
+    own = (own + swap(theirs, "slab", 2).astype(f32)).astype(bf16)
     pair = swap(own, "slab", 1)
     own_core = swap(own, "spin", 1)
     pair_core = swap(pair, "spin", 1)

time: 117 us -> 115 us (0.983)
  waiting for transfers between devices: 57.6 us -> 52.9 us
  starting transfers between devices: 22.7 us -> 25.3 us
  other arithmetic: 2.32 us -> 1.14 us
    ppermute x9, waiting for transfers between devices: 30.4 us -> 23.6 us  [swap(): return lax.ppermute(x, axis, [(i, i ^ distance) for i in range(count)])]
    ppermute x2 -> x3, waiting for transfers between devices: 10.1 us -> 13.1 us  [shift(): return lax.ppermute(x, axis, [(i, (i + by) % count) for i in range(count)])]
    unnamed x12, local copies, waits for them, and re-layouts: 0.03 us -> 2.01 us
    transpose x1, other arithmetic: 1.41 us -> 0.21 us  [body(): coefs = jnp.concatenate([links.reshape(2 * COLORS * COLORS, planes, sites...]
    pallas_call x1 -> x2, Pallas kernels: 3.28 us -> 2.55 us  [the longest x1 1.53 us: body(): pl.pallas_call(most_kernel, in_specs=[vmem()] * 3, out_specs=vmem(), out_...]
    ppermute x2 -> x3, starting transfers between devices: 6.67 us -> 7.14 us  [shift(): return lax.ppermute(x, axis, [(i, (i + by) % count) for i in range(count)])]
  transfers between devices with their start and end apart: 14 -> 15, of which waited for: 8 -> 9; matrix products, arithmetic and copies ran while one was open for 7% -> 5% of each run, Pallas kernels for 14% -> 16%
where the time goes in v1:
time: 115 us; the launch traced here: 113 us
  waiting for transfers between devices  52.9 us (46%)
  Pallas kernels  25.8 us (22%)
  starting transfers between devices  25.3 us (22%)
  local copies, waits for them, and re-layouts  6.6 us (6%)
  between operations  1.51 us (1%)
    ppermute x9, waiting for transfers between devices, swap(): return lax.ppermute(x, axis, [(i, i ^ distance) for i in range(count)])  23.6 us
    ppermute x3, waiting for transfers between devices, body(): piece = lax.ppermute(piece, 'slab', route)  16.2 us
    pallas_call x1, Pallas kernels, body(): pl.pallas_call(field_kernel, grid=(sites // block,), in_specs=[smem(), pl...  13.9 us
    ppermute x3, waiting for transfers between devices, shift(): return lax.ppermute(x, axis, [(i, (i + by) % count) for i in range(count)])  13.1 us
    ppermute x9, starting transfers between devices, swap(): return lax.ppermute(x, axis, [(i, i ^ distance) for i in range(count)])  9.66 us
    ppermute x3, starting transfers between devices, body(): piece = lax.ppermute(piece, 'slab', route)  8.5 us
    ppermute x3, starting transfers between devices, shift(): return lax.ppermute(x, axis, [(i, (i + by) % count) for i in range(count)])  7.14 us
    pallas_call x2, Pallas kernels, body(): pl.pallas_call(functools.partial(join_kernel, span), grid_spec=pltpu.Pref...  3.52 us
  transfers between devices with their start and end apart: 15, of which 9 were waited for; matrix products, arithmetic and copies ran while one was open for 5% of the time, Pallas kernels for 16%

profile of v1, /device:TPU:0, one launch (start us, length us, event | category | flops | bytes accessed | tf_op | source)
XLA Modules:
  0.0 113.2 jit_solution(4848499532597766979)
XLA Ops:
  0.0 0.0 copy-start
  0.0 2.6 %edge.1 = (bf16[5,512,256]{2,1,0:T(8,128)(2,1)}, bf16[512,256]{1,0:T(8,128)(2,1)}) custom-call(bf16[2,3,2,512,256]{4,3,2,1,0:T(8,128)(2,1)} %bitcast.27), custom_call_target="tpu_custom_call" | custom-call | tf_op jit(solution)/shard_map/edge/pallas_call | solution.py:253
  2.6 5.1 %collective-permute-start.1 = (bf16[512,256]{1,0:T(8,128)(2,1)}, bf16[512,256]{1,0:T(8,128)(2,1)S(1)}, u32[]{:S(2)}, u32[]{:S(2)}) collective-permute-start(bf16[512,256]{1,0:T(8,128)(2,1)} %get-tuple-element.46), channel_id=1, source_target_pairs={{0,12},{4,0},{8,4},{12,8},{1,13},{5,1},{9,5},{13,9},{2,14},{6,2},{... | collective-permute-start | bytes 786440 | tf_op jit(solution)/shard_map/ppermute | solution.py:21
  7.7 0.4 collective-permute-start
  8.2 0.1 fusion.22
  8.3 0.0 copy-done.3
  8.3 0.6 gather_fusion.1
  9.0 0.0 copy-done
  9.0 0.6 gather_fusion
  9.5 0.2 slice_reduce_fusion.2
  9.7 0.0 copy-done.5
  9.8 0.1 fusion.17
  9.9 0.1 pad_add_fusion.1.place_ref
  9.9 0.7 fusion.24
  10.6 0.1 fusion.8
  10.7 0.2 fusion.5
  10.9 0.1 fusion.2
  11.0 0.1 pad_add_fusion.place_ref
  11.1 0.7 fusion.23
  13.0 0.2 copy.15
  13.3 0.0 copy-done.4
  13.3 0.2 copy.14
  13.5 0.1 pad.6.clone
  13.6 1.3 %stack.30.meta_ref = s32[7]{0:T(128)S(1)} concatenate(s32[1]{0:T(128)} %bitcast, s32[1]{0:T(128)} %bitcast.1, s32[1]{0:T(128)} %bitcast.2, s32[1]{0:T(128)} %bitcast.3, s32[1]{0:T(128)} %bitcast.4, s32[2]{0:T(128)S(1)} %copy-done.3), dimensions={0} | concatenate | bytes 56 | tf_op jit(solution)/shard_map/stack | solution.py:299
  14.9 0.2 maximum_bitcast_fusion.coefs_ref
  15.1 0.0 copy-start.1
  15.2 2.0 %copy-done.1 = bf16[1,2,3,2,512,256]{5,4,3,2,1,0:T(8,128)(2,1)S(1)} copy-done((bf16[1,2,3,2,512,256]{5,4,3,2,1,0:T(8,128)(2,1)S(1)}, bf16[1,2,3,2,512,256]{5,4,3,2,1,0:T(8,128)(2,1)}, u32[]{:S(2)}) %copy-start.1) | copy-done | bytes 3145752
  17.1 13.9 %fields.1 = (f32[1024,512]{1,0:T(8,128)S(1)}, bf16[3,1024,512]{2,1,0:T(8,128)(2,1)S(1)}) custom-call(s32[7]{0:T(128)S(1)} %stack.30.meta_ref, bf16[2,3,2,512,256]{4,3,2,1,0:T(8,128)(2,1)S(1)} %bitcast.28, f32[2,512,24]{2,1,0:T(8,128)S(1)} %maximum_bitcast_fusion.coefs_ref), custom_call_target="tpu_custom_call" | custom-call | tf_op jit(solution)/shard_map/fields/pallas_call | solution.py:323
  31.1 1.0 deal.1
  32.0 9.7 %collective-permute-done.most_ref = bf16[5,512,256]{2,1,0:T(8,128)(2,1)S(1)} collective-permute-done((bf16[5,512,256]{2,1,0:T(8,128)(2,1)}, bf16[5,512,256]{2,1,0:T(8,128)(2,1)S(1)}, u32[]{:S(2)}, u32[]{:S(2)}) %collective-permute-start) | collective-permute-done | bytes 1310752 | tf_op jit(solution)/shard_map/ppermute | solution.py:21
  41.7 1.5 %most.1.total_ref = f32[2,2,256,256]{3,2,1,0:T(8,128)S(1)} custom-call(bf16[3,1024,512]{2,1,0:T(8,128)(2,1)S(1)} %get-tuple-element.43.outer_ref, f32[1024,512]{1,0:T(8,128)S(1)} %get-tuple-element.44.inner_ref, bf16[5,512,256]{2,1,0:T(8,128)(2,1)S(1)} %collective-permute-done.most_ref), custom_call_target="tpu_custom_call" | custom-call | tf_op jit(solution)/shard_map/most/pallas_call | solution.py:354
  43.3 0.0 collective-permute-done.1.last_ref
  43.3 1.0 last.1
  44.3 0.1 collective-permute-start.2
  44.4 1.5 %collective-permute-done.2 = bf16[2,256,256]{2,1,0:T(8,128)(2,1)S(1)} collective-permute-done((bf16[2,256,256]{2,1,0:T(8,128)(2,1)S(1)}, bf16[2,256,256]{2,1,0:T(8,128)(2,1)S(1)}, u32[]{:S(2)}, u32[]{:S(2)}) %collective-permute-start.2) | collective-permute-done | bytes 262176 | tf_op jit(solution)/shard_map/ppermute | solution.py:26
  45.9 0.1 convert_add_fusion
  46.0 0.4 collective-permute-start.3
  46.4 5.2 %collective-permute-done.3 = bf16[256,256]{1,0:T(8,128)(2,1)S(1)} collective-permute-done((bf16[256,256]{1,0:T(8,128)(2,1)S(1)}, bf16[256,256]{1,0:T(8,128)(2,1)S(1)}, u32[]{:S(2)}, u32[]{:S(2)}) %collective-permute-start.3) | collective-permute-done | bytes 131104 | tf_op jit(solution)/shard_map/ppermute | solution.py:26
  51.6 1.6 %collective-permute-start.4 = (bf16[256,256]{1,0:T(8,128)(2,1)S(1)}, bf16[256,256]{1,0:T(8,128)(2,1)S(1)}, u32[]{:S(2)}, u32[]{:S(2)}) collective-permute-start(bf16[256,256]{1,0:T(8,128)(2,1)S(1)} %fusion.3), channel_id=1, source_target_pairs={{0,2},{2,0},{1,3},{3,1},{4,6},{6,4},{5,7},{7,5},{8,10},{10,8},{9,1... | collective-permute-start | bytes 393224 | tf_op jit(solution)/shard_map/ppermute | solution.py:21
  53.2 3.5 %collective-permute-done.4 = bf16[256,256]{1,0:T(8,128)(2,1)S(1)} collective-permute-done((bf16[256,256]{1,0:T(8,128)(2,1)S(1)}, bf16[256,256]{1,0:T(8,128)(2,1)S(1)}, u32[]{:S(2)}, u32[]{:S(2)}) %collective-permute-start.4) | collective-permute-done | bytes 131104 | tf_op jit(solution)/shard_map/ppermute | solution.py:21
  56.7 3.1 %collective-permute-start.5 = (bf16[256,256]{1,0:T(8,128)(2,1)S(1)}, bf16[256,256]{1,0:T(8,128)(2,1)S(1)}, u32[]{:S(2)}, u32[]{:S(2)}) collective-permute-start(bf16[256,256]{1,0:T(8,128)(2,1)S(1)} %broadcast_select_fusion), channel_id=1, source_target_pairs={{0,8},{4,12},{8,0},{12,4},{1,9},{5,13},{9,1},{13,5},{2,10},{6,14},... | collective-permute-start | bytes 393224 | tf_op jit(solution)/shard_map/ppermute | solution.py:26
  59.7 1.7 %collective-permute-start.9 = (bf16[2,256,256]{2,1,0:T(8,128)(2,1)S(1)}, bf16[2,256,256]{2,1,0:T(8,128)(2,1)S(1)}, u32[]{:S(2)}, u32[]{:S(2)}) collective-permute-start(bf16[2,256,256]{2,1,0:T(8,128)(2,1)S(1)} %get-tuple-element.51), channel_id=1, source_target_pairs={{0,4},{4,0},{8,12},{12,8},{1,5},{5,1},{9,13},{13,9},{2,6},{6,2},{1... | collective-permute-start | bytes 786440 | tf_op jit(solution)/shard_map/ppermute | solution.py:26
  61.5 0.1 collective-permute-start.10
  61.5 2.6 %collective-permute-start.11 = (bf16[2,256,256]{2,1,0:T(8,128)(2,1)S(1)}, bf16[2,256,256]{2,1,0:T(8,128)(2,1)S(1)}, u32[]{:S(2)}, u32[]{:S(2)}) collective-permute-start(bf16[2,256,256]{2,1,0:T(8,128)(2,1)S(1)} %get-tuple-element.53), channel_id=1, source_target_pairs={{0,12},{4,8},{8,4},{12,0},{1,13},{5,9},{9,5},{13,1},{2,14},{6,10},... | collective-permute-start | bytes 786440 | tf_op jit(solution)/shard_map/ppermute | solution.py:26
  64.1 1.3 %collective-permute-done.5 = bf16[256,256]{1,0:T(8,128)(2,1)S(1)} collective-permute-done((bf16[256,256]{1,0:T(8,128)(2,1)S(1)}, bf16[256,256]{1,0:T(8,128)(2,1)S(1)}, u32[]{:S(2)}, u32[]{:S(2)}) %collective-permute-start.5) | collective-permute-done | bytes 131104 | tf_op jit(solution)/shard_map/ppermute | solution.py:26
  65.4 0.1 add_convert_fusion.refs_0_
  65.5 1.7 %collective-permute-start.6 = (bf16[256,256]{1,0:T(8,128)(2,1)S(1)}, bf16[256,256]{1,0:T(8,128)(2,1)S(1)}, u32[]{:S(2)}, u32[]{:S(2)}) collective-permute-start(bf16[256,256]{1,0:T(8,128)(2,1)S(1)} %add_convert_fusion.refs_0_), channel_id=1, source_target_pairs={{0,4},{4,0},{8,12},{12,8},{1,5},{5,1},{9,13},{13,9},{2,6},{6,2},{1... | collective-permute-start | bytes 393224 | tf_op jit(solution)/shard_map/ppermute | solution.py:26
  67.2 0.0 collective-permute-start.7
  67.2 13.9 %collective-permute-done.6.refs_1_ = bf16[256,256]{1,0:T(8,128)(2,1)S(1)} collective-permute-done((bf16[256,256]{1,0:T(8,128)(2,1)S(1)}, bf16[256,256]{1,0:T(8,128)(2,1)S(1)}, u32[]{:S(2)}, u32[]{:S(2)}) %collective-permute-start.6) | collective-permute-done | bytes 131104 | tf_op jit(solution)/shard_map/ppermute | solution.py:26
  81.1 0.0 collective-permute-start.8
  81.1 0.0 collective-permute-done.9.refs_5_
  81.1 1.7 %collective-permute-done.10.refs_6_ = bf16[2,256,256]{2,1,0:T(8,128)(2,1)S(1)} collective-permute-done((bf16[2,256,256]{2,1,0:T(8,128)(2,1)S(1)}, bf16[2,256,256]{2,1,0:T(8,128)(2,1)S(1)}, u32[]{:S(2)}, u32[]{:S(2)}) %collective-permute-start.10) | collective-permute-done | bytes 262176 | tf_op jit(solution)/shard_map/ppermute | solution.py:26
  82.8 0.0 collective-permute-done.11.refs_7_
  82.8 0.0 collective-permute-done.7.refs_2_
  82.8 0.0 collective-permute-done.8.refs_3_
  82.8 2.2 %blocks.1 = (bf16[2,256,256]{2,1,0:T(8,128)(2,1)S(1)}, bf16[2,256,256]{2,1,0:T(8,128)(2,1)S(1)}, bf16[2,256,256]{2,1,0:T(8,128)(2,1)S(1)}, bf16[2,256,256]{2,1,0:T(8,128)(2,1)S(1)}) custom-call(s32[7]{0:T(128)S(1)} %stack.30.meta_ref, bf16[256,256]{1,0:T(8,128)(2,1)S(1)} %add_convert_fusion.refs_0_, bf16[256,256]{1,0:T(8,128)(2,1)S(1)} %collective-permute-done.6.refs_1_, ...), custom_call_target="tpu_custom_call" | custom-call | tf_op jit(solution)/shard_map/blocks/pallas_call | solution.py:400
  85.0 5.1 %collective-permute-start.14 = (bf16[2,256,256]{2,1,0:T(8,128)(2,1)S(1)}, bf16[2,256,256]{2,1,0:T(8,128)(2,1)S(1)}, u32[]{:S(2)}, u32[]{:S(2)}) collective-permute-start(bf16[2,256,256]{2,1,0:T(8,128)(2,1)S(1)} %get-tuple-element.58), channel_id=1, source_target_pairs={{0,4},{4,0},{8,12},{12,8},{1,5},{5,1},{9,13},{13,9},{2,6},{6,2},{1... | collective-permute-start | bytes 786440 | tf_op jit(solution)/shard_map/ppermute | solution.py:417
  90.1 2.0 %collective-permute-start.12 = (bf16[2,256,256]{2,1,0:T(8,128)(2,1)S(1)}, bf16[2,256,256]{2,1,0:T(8,128)(2,1)S(1)}, u32[]{:S(2)}, u32[]{:S(2)}) collective-permute-start(bf16[2,256,256]{2,1,0:T(8,128)(2,1)S(1)} %get-tuple-element.54), channel_id=1, source_target_pairs={{0,8},{4,12},{8,0},{12,4},{1,9},{5,13},{9,1},{13,5},{2,10},{6,14},... | collective-permute-start | bytes 786440 | tf_op jit(solution)/shard_map/ppermute | solution.py:417
  92.1 1.4 %collective-permute-start.13 = (bf16[2,256,256]{2,1,0:T(8,128)(2,1)S(1)}, bf16[2,256,256]{2,1,0:T(8,128)(2,1)S(1)}, u32[]{:S(2)}, u32[]{:S(2)}) collective-permute-start(bf16[2,256,256]{2,1,0:T(8,128)(2,1)S(1)} %get-tuple-element.55), channel_id=1, source_target_pairs={{0,12},{4,8},{8,4},{12,0},{1,13},{5,9},{9,5},{13,1},{2,14},{6,10},... | collective-permute-start | bytes 786440 | tf_op jit(solution)/shard_map/ppermute | solution.py:417
  93.5 6.6 %collective-permute-done.14.refs_1_ = bf16[2,256,256]{2,1,0:T(8,128)(2,1)S(1)} collective-permute-done((bf16[2,256,256]{2,1,0:T(8,128)(2,1)S(1)}, bf16[2,256,256]{2,1,0:T(8,128)(2,1)S(1)}, u32[]{:S(2)}, u32[]{:S(2)}) %collective-permute-start.14) | collective-permute-done | bytes 262176 | tf_op jit(solution)/shard_map/ppermute | solution.py:417
  100.1 1.8 %join.2.refs_2_ = bf16[2,2,512,256]{3,2,1,0:T(8,128)(2,1)} custom-call(s32[4]{0:T(128)S(1)} %pad_add_fusion.place_ref, bf16[256,256]{1,0:T(8,128)(2,1)S(1)} %get-tuple-element.33.move_ref, bf16[2,256,256]{2,1,0:T(8,128)(2,1)S(1)} %get-tuple-element.57.refs_0_, bf16[2,256,256]{2,1,0:T(8,128)(2,1)S(1)} %collective-permute-done.14.refs_1_), custom_call_target="tpu_custom_call" | custom-call | tf_op jit(solution)/shard_map/join/pallas_call | solution.py:424
  101.9 9.6 %collective-permute-done.12.refs_0_ = bf16[2,256,256]{2,1,0:T(8,128)(2,1)S(1)} collective-permute-done((bf16[2,256,256]{2,1,0:T(8,128)(2,1)S(1)}, bf16[2,256,256]{2,1,0:T(8,128)(2,1)S(1)}, u32[]{:S(2)}, u32[]{:S(2)}) %collective-permute-start.12) | collective-permute-done | bytes 262176 | tf_op jit(solution)/shard_map/ppermute | solution.py:417
  111.5 0.0 collective-permute-done.13.refs_1_
  111.5 1.8 %join.3 = bf16[2,2,512,256]{3,2,1,0:T(8,128)(2,1)} custom-call(s32[4]{0:T(128)S(1)} %pad_add_fusion.1.place_ref, bf16[256,256]{1,0:T(8,128)(2,1)S(1)} %get-tuple-element.33.move_ref, bf16[2,256,256]{2,1,0:T(8,128)(2,1)S(1)} %collective-permute-done.12.refs_0_, ...), custom_call_target="tpu_custom_call", output_to_operand_aliasing={{}: (4, {})} | custom-call | tf_op jit(solution)/shard_map/join/pallas_call | solution.py:424
  (17 shorter events, 0.1 us)
Async XLA Ops:
  0.0 9.0 %copy-start = (s32[2,3]{1,0:T(2,128)S(1)}, s32[2,3]{1,0:T(2,128)}, u32[]{:S(2)}) copy-start(s32[2,3]{1,0:T(2,128)} %param.8) | copy-start | bytes 76
  0.0 8.3 %copy-start.3 = (s32[2]{0:T(128)S(1)}, s32[2]{0:T(128)}, u32[]{:S(2)}) copy-start(s32[2]{0:T(128)} %param.9) | copy-start | bytes 28
  0.0 9.7 %copy-start.5 = (s32[2,2]{1,0:T(2,128)S(1)}, s32[2,2]{1,0:T(2,128)}, u32[]{:S(2)}) copy-start(s32[2,2]{1,0:T(2,128)} %param.10) | copy-start | bytes 52
  0.0 13.3 %copy-start.4 = (f32[1,2,3,3,2,512]{5,4,3,2,1,0:T(2,128)S(1)}, f32[1,2,3,3,2,512]{5,4,3,2,1,0:T(2,128)}, u32[]{:S(2)}) copy-start(f32[1,2,3,3,2,512]{5,4,3,2,1,0:T(2,128)} %param.7) | copy-start | bytes 221188
  2.6 40.6 %collective-permute-start.1 = (bf16[512,256]{1,0:T(8,128)(2,1)}, bf16[512,256]{1,0:T(8,128)(2,1)S(1)}, u32[]{:S(2)}, u32[]{:S(2)}) collective-permute-start(bf16[512,256]{1,0:T(8,128)(2,1)} %get-tuple-element.46), channel_id=1, source_target_pairs={{0,12},{4,0},{8,4},{12,8},{1,13},{5,1},{9,5},{13,9},{2,14},{6,2},{... | collective-permute-start | bytes 786440 | tf_op jit(solution)/shard_map/ppermute | solution.py:21
  7.7 34.0 %collective-permute-start = (bf16[5,512,256]{2,1,0:T(8,128)(2,1)}, bf16[5,512,256]{2,1,0:T(8,128)(2,1)S(1)}, u32[]{:S(2)}, u32[]{:S(2)}) collective-permute-start(bf16[5,512,256]{2,1,0:T(8,128)(2,1)} %get-tuple-element.45), channel_id=1, source_target_pairs={{0,12},{4,0},{8,4},{12,8},{1,13},{5,1},{9,5},{13,9},{2,14},{6,2},{... | collective-permute-start | bytes 3932168 | tf_op jit(solution)/shard_map/ppermute | solution.py:21
  14.9 16.1 %copy-start.2 = (bf16[2,2,512,256]{3,2,1,0:T(8,128)(2,1)S(1)}, bf16[2,2,512,256]{3,2,1,0:T(8,128)(2,1)}, u32[]{:S(2)}) copy-start(bf16[2,2,512,256]{3,2,1,0:T(8,128)(2,1)} %param.11) | copy-start | bytes 3145732
  15.1 2.0 %copy-start.1 = (bf16[1,2,3,2,512,256]{5,4,3,2,1,0:T(8,128)(2,1)S(1)}, bf16[1,2,3,2,512,256]{5,4,3,2,1,0:T(8,128)(2,1)}, u32[]{:S(2)}) copy-start(bf16[1,2,3,2,512,256]{5,4,3,2,1,0:T(8,128)(2,1)} %param.6) | copy-start | bytes 9437188
  44.3 1.6 %collective-permute-start.2 = (bf16[2,256,256]{2,1,0:T(8,128)(2,1)S(1)}, bf16[2,256,256]{2,1,0:T(8,128)(2,1)S(1)}, u32[]{:S(2)}, u32[]{:S(2)}) collective-permute-start(bf16[2,256,256]{2,1,0:T(8,128)(2,1)S(1)} %get-tuple-element.48), channel_id=1, source_target_pairs={{0,1},{1,0},{2,3},{3,2},{4,5},{5,4},{6,7},{7,6},{8,9},{9,8},{10,11... | collective-permute-start | bytes 786440 | tf_op jit(solution)/shard_map/ppermute | solution.py:26
  46.0 5.6 %collective-permute-start.3 = (bf16[256,256]{1,0:T(8,128)(2,1)S(1)}, bf16[256,256]{1,0:T(8,128)(2,1)S(1)}, u32[]{:S(2)}, u32[]{:S(2)}) collective-permute-start(bf16[256,256]{1,0:T(8,128)(2,1)S(1)} %fusion.4), channel_id=1, source_target_pairs={{0,4},{4,0},{8,12},{12,8},{1,5},{5,1},{9,13},{13,9},{2,6},{6,2},{1... | collective-permute-start | bytes 393224 | tf_op jit(solution)/shard_map/ppermute | solution.py:26
  51.6 5.0 %collective-permute-start.4 = (bf16[256,256]{1,0:T(8,128)(2,1)S(1)}, bf16[256,256]{1,0:T(8,128)(2,1)S(1)}, u32[]{:S(2)}, u32[]{:S(2)}) collective-permute-start(bf16[256,256]{1,0:T(8,128)(2,1)S(1)} %fusion.3), channel_id=1, source_target_pairs={{0,2},{2,0},{1,3},{3,1},{4,6},{6,4},{5,7},{7,5},{8,10},{10,8},{9,1... | collective-permute-start | bytes 393224 | tf_op jit(solution)/shard_map/ppermute | solution.py:21
  56.7 8.7 %collective-permute-start.5 = (bf16[256,256]{1,0:T(8,128)(2,1)S(1)}, bf16[256,256]{1,0:T(8,128)(2,1)S(1)}, u32[]{:S(2)}, u32[]{:S(2)}) collective-permute-start(bf16[256,256]{1,0:T(8,128)(2,1)S(1)} %broadcast_select_fusion), channel_id=1, source_target_pairs={{0,8},{4,12},{8,0},{12,4},{1,9},{5,13},{9,1},{13,5},{2,10},{6,14},... | collective-permute-start | bytes 393224 | tf_op jit(solution)/shard_map/ppermute | solution.py:26
  59.7 21.3 %collective-permute-start.9 = (bf16[2,256,256]{2,1,0:T(8,128)(2,1)S(1)}, bf16[2,256,256]{2,1,0:T(8,128)(2,1)S(1)}, u32[]{:S(2)}, u32[]{:S(2)}) collective-permute-start(bf16[2,256,256]{2,1,0:T(8,128)(2,1)S(1)} %get-tuple-element.51), channel_id=1, source_target_pairs={{0,4},{4,0},{8,12},{12,8},{1,5},{5,1},{9,13},{13,9},{2,6},{6,2},{1... | collective-permute-start | bytes 786440 | tf_op jit(solution)/shard_map/ppermute | solution.py:26
  61.5 21.3 %collective-permute-start.10 = (bf16[2,256,256]{2,1,0:T(8,128)(2,1)S(1)}, bf16[2,256,256]{2,1,0:T(8,128)(2,1)S(1)}, u32[]{:S(2)}, u32[]{:S(2)}) collective-permute-start(bf16[2,256,256]{2,1,0:T(8,128)(2,1)S(1)} %get-tuple-element.52), channel_id=1, source_target_pairs={{0,8},{4,12},{8,0},{12,4},{1,9},{5,13},{9,1},{13,5},{2,10},{6,14},... | collective-permute-start | bytes 786440 | tf_op jit(solution)/shard_map/ppermute | solution.py:26
  61.5 21.2 %collective-permute-start.11 = (bf16[2,256,256]{2,1,0:T(8,128)(2,1)S(1)}, bf16[2,256,256]{2,1,0:T(8,128)(2,1)S(1)}, u32[]{:S(2)}, u32[]{:S(2)}) collective-permute-start(bf16[2,256,256]{2,1,0:T(8,128)(2,1)S(1)} %get-tuple-element.53), channel_id=1, source_target_pairs={{0,12},{4,8},{8,4},{12,0},{1,13},{5,9},{9,5},{13,1},{2,14},{6,10},... | collective-permute-start | bytes 786440 | tf_op jit(solution)/shard_map/ppermute | solution.py:26
  65.5 15.6 %collective-permute-start.6 = (bf16[256,256]{1,0:T(8,128)(2,1)S(1)}, bf16[256,256]{1,0:T(8,128)(2,1)S(1)}, u32[]{:S(2)}, u32[]{:S(2)}) collective-permute-start(bf16[256,256]{1,0:T(8,128)(2,1)S(1)} %add_convert_fusion.refs_0_), channel_id=1, source_target_pairs={{0,4},{4,0},{8,12},{12,8},{1,5},{5,1},{9,13},{13,9},{2,6},{6,2},{1... | collective-permute-start | bytes 393224 | tf_op jit(solution)/shard_map/ppermute | solution.py:26
  67.2 15.6 %collective-permute-start.7 = (bf16[256,256]{1,0:T(8,128)(2,1)S(1)}, bf16[256,256]{1,0:T(8,128)(2,1)S(1)}, u32[]{:S(2)}, u32[]{:S(2)}) collective-permute-start(bf16[256,256]{1,0:T(8,128)(2,1)S(1)} %add_convert_fusion.refs_0_), channel_id=1, source_target_pairs={{0,1},{1,0},{2,3},{3,2},{4,5},{5,4},{6,7},{7,6},{8,9},{9,8},{10,11... | collective-permute-start | bytes 393224 | tf_op jit(solution)/shard_map/ppermute | solution.py:26
  81.1 1.7 %collective-permute-start.8 = (bf16[256,256]{1,0:T(8,128)(2,1)S(1)}, bf16[256,256]{1,0:T(8,128)(2,1)S(1)}, u32[]{:S(2)}, u32[]{:S(2)}) collective-permute-start(bf16[256,256]{1,0:T(8,128)(2,1)S(1)} %collective-permute-done.6.refs_1_), channel_id=1, source_target_pairs={{0,1},{1,0},{2,3},{3,2},{4,5},{5,4},{6,7},{7,6},{8,9},{9,8},{10,11... | collective-permute-start | bytes 393224 | tf_op jit(solution)/shard_map/ppermute | solution.py:26
  85.0 15.1 %collective-permute-start.14 = (bf16[2,256,256]{2,1,0:T(8,128)(2,1)S(1)}, bf16[2,256,256]{2,1,0:T(8,128)(2,1)S(1)}, u32[]{:S(2)}, u32[]{:S(2)}) collective-permute-start(bf16[2,256,256]{2,1,0:T(8,128)(2,1)S(1)} %get-tuple-element.58), channel_id=1, source_target_pairs={{0,4},{4,0},{8,12},{12,8},{1,5},{5,1},{9,13},{13,9},{2,6},{6,2},{1... | collective-permute-start | bytes 786440 | tf_op jit(solution)/shard_map/ppermute | solution.py:417
  90.1 21.3 %collective-permute-start.12 = (bf16[2,256,256]{2,1,0:T(8,128)(2,1)S(1)}, bf16[2,256,256]{2,1,0:T(8,128)(2,1)S(1)}, u32[]{:S(2)}, u32[]{:S(2)}) collective-permute-start(bf16[2,256,256]{2,1,0:T(8,128)(2,1)S(1)} %get-tuple-element.54), channel_id=1, source_target_pairs={{0,8},{4,12},{8,0},{12,4},{1,9},{5,13},{9,1},{13,5},{2,10},{6,14},... | collective-permute-start | bytes 786440 | tf_op jit(solution)/shard_map/ppermute | solution.py:417
  92.1 19.3 %collective-permute-start.13 = (bf16[2,256,256]{2,1,0:T(8,128)(2,1)S(1)}, bf16[2,256,256]{2,1,0:T(8,128)(2,1)S(1)}, u32[]{:S(2)}, u32[]{:S(2)}) collective-permute-start(bf16[2,256,256]{2,1,0:T(8,128)(2,1)S(1)} %get-tuple-element.55), channel_id=1, source_target_pairs={{0,12},{4,8},{8,4},{12,0},{1,13},{5,9},{9,5},{13,1},{2,14},{6,10},... | collective-permute-start | bytes 786440 | tf_op jit(solution)/shard_map/ppermute | solution.py:417

commit v2 on v1

--- a/solution.py
+++ b/solution.py
@@ -14,6 +14,7 @@
 LZ = 32
 COLORS = 3
 COEFS = 24
+CUTS = 2
 
 
 def shift(x, axis, by):
@@ -34,23 +35,23 @@
     return pl.BlockSpec(memory_space=pltpu.SMEM)
 
 
-def edge_kernel(fields_ref, most_ref, last_ref, taken):
-    spots = [(part, c) for part in range(2) for c in range(COLORS)]
-    copies = [
-        pltpu.make_async_copy(
-            fields_ref.at[part, c, 0],
-            most_ref.at[at] if at + 1 < len(spots) else last_ref,
-            taken.at[at],
-        )
-        for at, (part, c) in enumerate(spots)
-    ]
+def edge_kernel(spots, fields_ref, *refs):
+    *outs, taken = refs
+    copies = []
+    for out, chunk in zip(outs, spots):
+        for at, (part, c) in enumerate(chunk):
+            copies.append(
+                pltpu.make_async_copy(
+                    fields_ref.at[part, c, 0], out.at[at], taken.at[len(copies)]
+                )
+            )
     for copy in copies:
         copy.start()
     for copy in copies:
         copy.wait()
 
 
-def field_kernel(meta_ref, fields_ref, coefs_ref, inner_ref, outer_ref, rotated):
+def field_kernel(meta_ref, fields_ref, links_ref, turns_ref, inner_ref, outer_ref, rotated, coefs_ref):
     planes, block, vectors = fields_ref.shape[2:]
     tile = 16
 
@@ -59,6 +60,9 @@
         inner_ref[...] = jnp.zeros_like(inner_ref)
 
     for plane in range(planes):
+        rows = [links_ref[:, plane, :], turns_ref[:, plane, :]]
+        rows.append(jnp.zeros((COEFS - sum(row.shape[0] for row in rows), block), jnp.float32))
+        coefs_ref[plane] = jnp.concatenate(rows, axis=0).T
 
         def rows_step(step, carry):
             rows = pl.ds(pl.multiple_of(step * tile, tile), tile)
@@ -104,7 +108,7 @@
                 outer_ref[c] = rotated[c].T
 
 
-def most_kernel(outer_ref, inner_ref, most_ref, total_ref):
+def most_kernel(outer_ref, inner_ref, first_ref, most_ref, total_ref):
     vectors = most_ref.shape[-1]
     for slot in range(2):
         at = 2 * slot * vectors
@@ -114,7 +118,7 @@
             for c in range(COLORS - part):
                 total = total + jnp.dot(
                     outer_ref[c, at : at + 2 * vectors, :],
-                    most_ref[COLORS * part + c],
+                    most_ref[COLORS * part + c - 1] if part + c else first_ref[0],
                     preferred_element_type=jnp.float32,
                 )
             totals.append(total)
@@ -128,7 +132,7 @@
         at = 2 * slot * vectors
         both = jnp.dot(
             outer_ref[0, at : at + 2 * vectors, :],
-            last_ref[...],
+            last_ref[0],
             preferred_element_type=jnp.float32,
         )
         real = total_ref[slot, 0] + both[vectors:]
@@ -139,12 +143,14 @@
 
 def deal_kernel(share, meta_ref, perams_ref, move_ref, *outs):
     spin_rows = perams_ref.shape[2]
-    for by, out in enumerate(outs):
+    width = outs[0].shape[-1]
+    for which, out in enumerate(outs):
+        by, half = which // CUTS, which % CUTS
         item = (meta_ref[4] ^ by) // share
         for part in range(2):
             out[part] = jnp.dot(
                 perams_ref[item // spin_rows, part, lax.rem(item, spin_rows)],
-                move_ref[...],
+                move_ref[:, half * width : (half + 1) * width],
                 preferred_element_type=jnp.float32,
             ).astype(jnp.bfloat16)
 
@@ -176,11 +182,12 @@
     matrix = jnp.concatenate(
         [jnp.concatenate([real, -imag], axis=1), jnp.concatenate([imag, real], axis=1)], axis=0
     )
+    spins = NS // CUTS
     columns = []
-    for spin in range(NS):
+    for spin in range(spins):
         at = spin * per
         columns += [
-            chunk[...].reshape(2 * vectors, NS * per)[:, at : at + per] for chunk in chunks
+            chunk[...].reshape(2 * vectors, spins * per)[:, at : at + per] for chunk in chunks
         ]
     spread = jnp.concatenate(columns, axis=1)
     left = jnp.dot(matrix, spread, preferred_element_type=jnp.float32).astype(jnp.bfloat16)
@@ -211,7 +218,7 @@
             )
     right = turned_ref[...].astype(jnp.bfloat16)
     reals, imags = [], []
-    for spin in range(NS):
+    for spin in range(spins):
         both = jnp.dot(
             left[:, spin * vectors : (spin + 1) * vectors],
             right,
@@ -233,9 +240,11 @@
 
         @pl.when(pl.program_id(0) == which)
         def _():
+            cuts = refs[which * CUTS : (which + 1) * CUTS]
             for part in range(2):
+                piece = jnp.concatenate([cut[part] for cut in cuts], axis=1)
                 out_ref[0, part] = jnp.dot(
-                    refs[which][part], move_ref[...], preferred_element_type=jnp.float32
+                    piece, move_ref[...], preferred_element_type=jnp.float32
                 ).astype(jnp.bfloat16)
 
 
@@ -250,24 +259,29 @@
     lattice_x = planes * slab
     normalize = 1.0 / math.sqrt(3072 * lattice_x * LY * LZ)
 
-    most, last = pl.pallas_call(
-        edge_kernel,
-        in_specs=[pl.BlockSpec(memory_space=pl.ANY)],
-        out_specs=[vmem()] * 2,
-        out_shape=[
-            jax.ShapeDtypeStruct((2 * COLORS - 1, sites, vectors), bf16),
-            jax.ShapeDtypeStruct((sites, vectors), bf16),
-        ],
-        scratch_shapes=[pltpu.SemaphoreType.DMA((2 * COLORS,))],
-        compiler_params=pltpu.CompilerParams(vmem_limit_bytes=62 << 20),
-        name="edge",
-    )(fields)
+    def edge(spots):
+        return pl.pallas_call(
+            functools.partial(edge_kernel, spots),
+            in_specs=[pl.BlockSpec(memory_space=pl.ANY)],
+            out_specs=[vmem()] * len(spots),
+            out_shape=[
+                jax.ShapeDtypeStruct((len(chunk), sites, vectors), bf16) for chunk in spots
+            ],
+            scratch_shapes=[pltpu.SemaphoreType.DMA((sum(map(len, spots)),))],
+            compiler_params=pltpu.CompilerParams(vmem_limit_bytes=62 << 20),
+            name="edge",
+        )(fields)
+
+    spots = [(part, c) for part in range(2) for c in range(COLORS)]
+    (first,) = edge((spots[:1],))
+    first = shift(first, "slab", -1)
+    most, last = edge((spots[1:-1], spots[-1:]))
     most = shift(most, "slab", -1)
     last = shift(last, "slab", -1)
 
-    elems = jnp.stack([core, 1 - core])
-    forward = (displacement[elems] == 1).astype(i32)
-    turns = momenta[elems]
+    forward = (displacement == 1).astype(i32)
+    forward = jnp.where(core == 0, forward, forward[::-1])
+    turns = jnp.where(core == 0, momenta, momenta[::-1])
     x_site = z * planes + jnp.arange(planes, dtype=i32)[None, :] + (1 - forward)[:, None]
     yz_site = core * sites + jnp.arange(sites, dtype=i32)
     wave_x = jnp.mod(turns[:, 0:1] * x_site, lattice_x)
@@ -280,13 +294,8 @@
     angle = number.astype(f32) * (2.0 * math.pi / (lattice_x * LY * LZ))
     sign = (2 * forward - 1).astype(f32)[:, None, None]
     turn = jnp.stack([jnp.cos(angle), jnp.sin(angle) * sign], axis=1)
-    coefs = jnp.concatenate(
-        [
-            links.reshape(2 * COLORS * COLORS, planes, sites),
-            turn.reshape(4, planes, sites),
-            jnp.zeros((COEFS - 2 * COLORS * COLORS - 4, planes, sites), f32),
-        ]
-    ).transpose(1, 2, 0)
+    turn = turn.reshape(4, planes, sites)
+    links = links.reshape(2 * COLORS * COLORS, planes, sites)
 
     parity = lax.rem(z, 2)
     pairs = perambulators.shape[0]
@@ -305,8 +314,8 @@
     spread_spins = (target[None, :] == column[:, None]).astype(bf16)
     count = slab // share
 
-    def places(first, last):
-        found = lax.rem(z, count) ^ jnp.arange(first, last, dtype=i32)
+    def places(low, high):
+        found = lax.rem(z, count) ^ jnp.arange(low, high, dtype=i32)
         return jnp.concatenate([found // spin_rows, lax.rem(found, spin_rows)])
 
     cuts = (0, count // 2, count)
@@ -314,9 +323,9 @@
         lax.rem(t - slice_pairs[place // share // spin_rows, core] + tiles, tiles)
         for place in (z, z ^ 2)
     ]
-    spots = [places(first, last) for first, last in zip(cuts[:-1], cuts[1:])]
-    meta, coefs, gather_spins, spread_spins, wanted, spots = lax.optimization_barrier(
-        (meta, coefs, gather_spins, spread_spins, wanted, spots)
+    spots = [places(low, high) for low, high in zip(cuts[:-1], cuts[1:])]
+    meta, turn, gather_spins, spread_spins, wanted, spots = lax.optimization_barrier(
+        (meta, turn, gather_spins, spread_spins, wanted, spots)
     )
 
     block = min(sites, 256)
@@ -326,7 +335,8 @@
         in_specs=[
             smem(),
             pl.BlockSpec((2, COLORS, planes, block, vectors), lambda i: (0, 0, 0, i, 0)),
-            pl.BlockSpec((planes, block, COEFS), lambda i: (0, i, 0)),
+            pl.BlockSpec((2 * COLORS * COLORS, planes, block), lambda i: (0, 0, i)),
+            pl.BlockSpec((4, planes, block), lambda i: (0, 0, i)),
         ],
         out_specs=[
             pl.BlockSpec((4 * vectors, 2 * vectors), lambda i: (0, 0)),
@@ -336,16 +346,19 @@
             jax.ShapeDtypeStruct((4 * vectors, 2 * vectors), f32),
             jax.ShapeDtypeStruct((COLORS, 4 * vectors, sites), bf16),
         ],
-        scratch_shapes=[pltpu.VMEM((COLORS, block, 4 * vectors), bf16)],
+        scratch_shapes=[
+            pltpu.VMEM((COLORS, block, 4 * vectors), bf16),
+            pltpu.VMEM((planes, block, COEFS), f32),
+        ],
         compiler_params=pltpu.CompilerParams(vmem_limit_bytes=15 << 20),
         name="fields",
-    )(meta, fields, coefs)
+    )(meta, fields, links, turn)
 
     blocks = pl.pallas_call(
         functools.partial(deal_kernel, share),
         in_specs=[smem(), vmem(), vmem()],
-        out_specs=[vmem()] * slab,
-        out_shape=[jax.ShapeDtypeStruct((2, vectors, width), bf16)] * slab,
+        out_specs=[vmem()] * (slab * CUTS),
+        out_shape=[jax.ShapeDtypeStruct((2, vectors, width // CUTS), bf16)] * (slab * CUTS),
         compiler_params=pltpu.CompilerParams(vmem_limit_bytes=8 << 20),
         name="deal",
     )(meta, perambulators.reshape(pairs, 2, spin_rows, vectors, width), gather_spins)
@@ -353,12 +366,12 @@
 
     total = pl.pallas_call(
         most_kernel,
-        in_specs=[vmem()] * 3,
+        in_specs=[vmem()] * 4,
         out_specs=vmem(),
         out_shape=jax.ShapeDtypeStruct((2, 2, vectors, vectors), f32),
         compiler_params=pltpu.CompilerParams(vmem_limit_bytes=14 << 20),
         name="most",
-    )(outer, inner, most)
+    )(outer, inner, first, most)
     keep, send = pl.pallas_call(
         functools.partial(last_kernel, normalize),
         grid=(1,),
@@ -393,40 +406,41 @@
     own_core = swap(own, "spin", 1)
     pair_core = swap(pair, "spin", 1)
 
-    chunks = [blocks[0]]
-    for by in range(1, slab):
-        chunks.append(swap(blocks[by], "slab", by))
-
-    pieces = pl.pallas_call(
-        functools.partial(block_kernel, slab, share),
-        in_specs=[smem()] + [vmem()] * (4 + slab),
-        out_specs=[vmem()] * count,
-        out_shape=[jax.ShapeDtypeStruct((2, vectors, width), bf16)] * count,
-        scratch_shapes=[
-            pltpu.VMEM((vectors, vectors), f32),
-            pltpu.VMEM((vectors, 2 * vectors // share), f32),
-        ],
-        compiler_params=pltpu.CompilerParams(vmem_limit_bytes=14 << 20),
-        name="blocks",
-    )(meta, own, pair, own_core, pair_core, *chunks)
-
-    arrived = []
-    for which, piece in enumerate(pieces):
-        route = [(s, (s % share) * count + ((s // share) ^ which)) for s in range(slab)]
-        if any(a != b for a, b in route):
-            piece = lax.ppermute(piece, "slab", route)
-        arrived.append(piece)
+    pieces = []
+    for cut in range(CUTS):
+        chunks = [blocks[cut]]
+        for by in range(1, slab):
+            chunks.append(swap(blocks[by * CUTS + cut], "slab", by))
+        found = pl.pallas_call(
+            functools.partial(block_kernel, slab, share),
+            in_specs=[smem()] + [vmem()] * (4 + slab),
+            out_specs=[vmem()] * count,
+            out_shape=[jax.ShapeDtypeStruct((2, vectors, width // CUTS), bf16)] * count,
+            scratch_shapes=[
+                pltpu.VMEM((vectors, vectors), f32),
+                pltpu.VMEM((vectors, 2 * vectors // share), f32),
+            ],
+            compiler_params=pltpu.CompilerParams(vmem_limit_bytes=14 << 20),
+            name="blocks",
+        )(meta, own, pair, own_core, pair_core, *chunks)
+        arrived = []
+        for which, piece in enumerate(found):
+            route = [(s, (s % share) * count + ((s // share) ^ which)) for s in range(slab)]
+            if any(a != b for a, b in route):
+                piece = lax.ppermute(piece, "slab", route)
+            arrived.append(piece)
+        pieces.append(arrived)
 
     result = []
-    for first, last, spot in zip(cuts[:-1], cuts[1:], spots):
-        span = last - first
+    for low, high, spot in zip(cuts[:-1], cuts[1:], spots):
+        span = high - low
         result = [
             pl.pallas_call(
                 functools.partial(join_kernel, span),
                 grid_spec=pltpu.PrefetchScalarGridSpec(
                     num_scalar_prefetch=1,
                     grid=(span,),
-                    in_specs=[vmem()] * (1 + span)
+                    in_specs=[vmem()] * (1 + span * CUTS)
                     + [pl.BlockSpec(memory_space=pl.ANY)] * len(result),
                     out_specs=pl.BlockSpec(
                         (1, 2, vectors, width),
@@ -434,10 +448,15 @@
                     ),
                 ),
                 out_shape=jax.ShapeDtypeStruct(perambulators.shape, bf16),
-                input_output_aliases={2 + span: 0} if result else {},
+                input_output_aliases={2 + span * CUTS: 0} if result else {},
                 compiler_params=pltpu.CompilerParams(vmem_limit_bytes=6 << 20),
                 name="join",
-            )(spot, spread_spins, *arrived[first:last], *result)
+            )(
+                spot,
+                spread_spins,
+                *[arrived[at] for at in range(low, high) for arrived in pieces],
+                *result,
+            )
         ]
     return result[0]
 

time: 115 us -> 118 us (1.026); the launches traced: 113 us -> 118 us
  starting transfers between devices: 25.3 us -> 37.7 us
  waiting for transfers between devices: 52.9 us -> 40.9 us
  Pallas kernels: 25.8 us -> 28.9 us
  local copies, waits for them, and re-layouts: 6.6 us -> 8.1 us
    ppermute x3 -> x6, starting transfers between devices: 8.5 us -> 14.9 us  [body(): piece = lax.ppermute(piece, 'slab', route)]
    ppermute x9 -> x12, waiting for transfers between devices: 23.6 us -> 17.5 us  [swap(): return lax.ppermute(x, axis, [(i, i ^ distance) for i in range(count)])]
    ppermute x9 -> x12, starting transfers between devices: 9.66 us -> 15.1 us  [swap(): return lax.ppermute(x, axis, [(i, i ^ distance) for i in range(count)])]
    ppermute x3 -> x4, waiting for transfers between devices: 13.1 us -> 8.55 us  [shift(): return lax.ppermute(x, axis, [(i, (i + by) % count) for i in range(count)])]
    unnamed x12 -> x32, local copies, waits for them, and re-layouts: 2.01 us -> 5.16 us
    pallas_call x2 -> x3, Pallas kernels: 4.12 us -> 5.62 us  [the longest x2 4.1 us: edge(): pl.pallas_call(functools.partial(edge_kernel, spots), in_specs=[pl.BlockS...]
    ppermute x3 -> x6, waiting for transfers between devices: 16.2 us -> 14.8 us  [body(): piece = lax.ppermute(piece, 'slab', route)]
    gather x2 -> x0, local copies, waits for them, and re-layouts: 1.2 us -> none  [the longest x1 0.64 us: body(): forward = (displacement[elems] == 1).astype(i32)]
  transfers between devices with their start and end apart: 15 -> 22, of which waited for: 9 -> 11; matrix products, arithmetic and copies ran while one was open for 5% -> 3% of each run, Pallas kernels for 16% -> 21%
where the time goes in v2:
time: 118 us
  waiting for transfers between devices  40.9 us (35%)
  starting transfers between devices  37.7 us (32%)
  Pallas kernels  28.9 us (24%)
  local copies, waits for them, and re-layouts  8.1 us (7%)
  between operations  1.56 us (1%)
    ppermute x12, waiting for transfers between devices, swap(): return lax.ppermute(x, axis, [(i, i ^ distance) for i in range(count)])  17.5 us
    ppermute x12, starting transfers between devices, swap(): return lax.ppermute(x, axis, [(i, i ^ distance) for i in range(count)])  15.1 us
    ppermute x6, starting transfers between devices, body(): piece = lax.ppermute(piece, 'slab', route)  14.9 us
    ppermute x6, waiting for transfers between devices, body(): piece = lax.ppermute(piece, 'slab', route)  14.8 us
    pallas_call x1, Pallas kernels, body(): pl.pallas_call(field_kernel, grid=(sites // block,), in_specs=[smem(), pl...  14.2 us
    ppermute x4, waiting for transfers between devices, shift(): return lax.ppermute(x, axis, [(i, (i + by) % count) for i in range(count)])  8.55 us
    ppermute x4, starting transfers between devices, shift(): return lax.ppermute(x, axis, [(i, (i + by) % count) for i in range(count)])  7.65 us
    unnamed x32, local copies, waits for them, and re-layouts  5.16 us
  transfers between devices with their start and end apart: 22, of which 11 were waited for; matrix products, arithmetic and copies ran while one was open for 3% of the time, Pallas kernels for 21%

profile of v2, /device:TPU:0, one launch (start us, length us, event | category | flops | bytes accessed | tf_op | source)
XLA Modules:
  0.0 117.9 jit_solution(8885896208842809988)
XLA Ops:
  0.0 1.7 %edge.2 = bf16[1,512,256]{2,1,0:T(8,128)(2,1)} custom-call(bf16[2,3,2,512,256]{4,3,2,1,0:T(8,128)(2,1)} %bitcast.21), custom_call_target="tpu_custom_call" | custom-call | tf_op jit(solution)/shard_map/edge/pallas_call | solution.py:263
  1.8 0.0 copy-start.2
  1.8 5.1 %collective-permute-start = (bf16[1,512,256]{2,1,0:T(8,128)(2,1)}, bf16[1,512,256]{2,1,0:T(8,128)(2,1)S(1)}, u32[]{:S(2)}, u32[]{:S(2)}) collective-permute-start(bf16[1,512,256]{2,1,0:T(8,128)(2,1)} %edge.2), channel_id=1, source_target_pairs={{0,12},{4,0},{8,4},{12,8},{1,13},{5,1},{9,5},{13,9},{2,14},{6,2},{... | collective-permute-start | bytes 786440 | tf_op jit(solution)/shard_map/ppermute | solution.py:22
  6.9 2.4 %edge.3 = (bf16[4,512,256]{2,1,0:T(8,128)(2,1)}, bf16[1,512,256]{2,1,0:T(8,128)(2,1)}) custom-call(bf16[2,3,2,512,256]{4,3,2,1,0:T(8,128)(2,1)} %bitcast.22), custom_call_target="tpu_custom_call" | custom-call | tf_op jit(solution)/shard_map/edge/pallas_call | solution.py:263
  9.3 0.5 collective-permute-start.2
  9.8 0.4 collective-permute-start.1
  10.3 0.1 rev.7
  10.4 0.2 slice_reduce_fusion.2
  10.7 0.1 fusion.17
  10.8 0.1 pad_add_fusion.1.place_ref
  10.8 0.6 fusion.20
  11.5 0.1 fusion.8
  11.5 0.2 fusion.5
  11.8 0.1 pad_add_fusion.place_ref
  11.8 0.7 fusion.19
  13.8 1.3 %stack.21.meta_ref = s32[7]{0:T(128)S(1)} concatenate(s32[1]{0:T(128)} %bitcast, s32[1]{0:T(128)} %bitcast.1, s32[1]{0:T(128)} %bitcast.2, s32[1]{0:T(128)} %bitcast.3, s32[1]{0:T(128)} %bitcast.4, s32[2]{0:T(128)S(1)} %copy-done.14), dimensions={0} | concatenate | bytes 56 | tf_op jit(solution)/shard_map/stack | solution.py:308
  15.1 0.1 fusion.2
  15.2 1.2 %deal.1 = (bf16[2,256,128]{2,1,0:T(8,128)(2,1)S(1)}, bf16[2,256,128]{2,1,0:T(8,128)(2,1)S(1)}, bf16[2,256,128]{2,1,0:T(8,128)(2,1)S(1)}, bf16[2,256,128]{2,1,0:T...) custom-call(s32[7]{0:T(128)S(1)} %stack.21.meta_ref, ...), custom_call_target="tpu_custom_call" | custom-call | tf_op jit(solution)/shard_map/deal/pallas_call | solution.py:357
  16.5 0.6 copy-done.3
  17.1 0.7 copy-done.5
  17.8 0.6 copy-done.7
  18.4 0.7 copy-done.9
  19.1 0.6 copy-done.11
  19.7 1.9 %copy-done = bf16[1,2,3,2,512,256]{5,4,3,2,1,0:T(8,128)(2,1)S(1)} copy-done((bf16[1,2,3,2,512,256]{5,4,3,2,1,0:T(8,128)(2,1)S(1)}, bf16[1,2,3,2,512,256]{5,4,3,2,1,0:T(8,128)(2,1)}, u32[]{:S(2)}) %copy-start) | copy-done | bytes 3145752
  21.6 14.2 %fields.1 = (f32[1024,512]{1,0:T(8,128)S(1)}, bf16[3,1024,512]{2,1,0:T(8,128)(2,1)S(1)}) custom-call(s32[7]{0:T(128)S(1)} %stack.21.meta_ref, bf16[2,3,2,512,256]{4,3,2,1,0:T(8,128)(2,1)S(1)} %bitcast.23, f32[18,2,512]{2,1,0:T(2,128)S(1)} %bitcast.25, f32[4,2,512]{2,1,0:T(2,128)S(1)} %bitcast.26), custom_call_target="tpu_custom_call" | custom-call | tf_op jit(solution)/shard_map/fields/pallas_call | solution.py:332
  35.8 5.1 %collective-permute-done.1.most_ref = bf16[4,512,256]{2,1,0:T(8,128)(2,1)S(1)} collective-permute-done((bf16[4,512,256]{2,1,0:T(8,128)(2,1)}, bf16[4,512,256]{2,1,0:T(8,128)(2,1)S(1)}, u32[]{:S(2)}, u32[]{:S(2)}) %collective-permute-start.1) | collective-permute-done | bytes 1048608 | tf_op jit(solution)/shard_map/ppermute | solution.py:22
  40.9 1.5 %most.1.total_ref = f32[2,2,256,256]{3,2,1,0:T(8,128)S(1)} custom-call(bf16[3,1024,512]{2,1,0:T(8,128)(2,1)S(1)} %get-tuple-element.59.outer_ref, f32[1024,512]{1,0:T(8,128)S(1)} %get-tuple-element.60.inner_ref, bf16[1,512,256]{2,1,0:T(8,128)(2,1)S(1)} %collective-permute-done.first_ref, bf16[4,512,256]{2,1,0:T(8,128)(2,1)S(1)} %collective-permute-done.1.most_ref), custom_call_target="tpu_custom_call" | custom-call | tf_op jit(solution)/shard_map/most/pallas_call | solution.py:367
  42.5 0.0 collective-permute-done.2.last_ref
  42.5 1.0 last.1
  43.5 0.1 collective-permute-start.3
  43.6 1.5 %collective-permute-done.3 = bf16[2,256,256]{2,1,0:T(8,128)(2,1)S(1)} collective-permute-done((bf16[2,256,256]{2,1,0:T(8,128)(2,1)S(1)}, bf16[2,256,256]{2,1,0:T(8,128)(2,1)S(1)}, u32[]{:S(2)}, u32[]{:S(2)}) %collective-permute-start.3) | collective-permute-done | bytes 262176 | tf_op jit(solution)/shard_map/ppermute | solution.py:27
  45.1 0.1 convert_add_fusion
  45.2 0.4 collective-permute-start.4
  45.6 5.2 %collective-permute-done.4 = bf16[256,256]{1,0:T(8,128)(2,1)S(1)} collective-permute-done((bf16[256,256]{1,0:T(8,128)(2,1)S(1)}, bf16[256,256]{1,0:T(8,128)(2,1)S(1)}, u32[]{:S(2)}, u32[]{:S(2)}) %collective-permute-start.4) | collective-permute-done | bytes 131104 | tf_op jit(solution)/shard_map/ppermute | solution.py:27
  50.8 1.6 %collective-permute-start.5 = (bf16[256,256]{1,0:T(8,128)(2,1)S(1)}, bf16[256,256]{1,0:T(8,128)(2,1)S(1)}, u32[]{:S(2)}, u32[]{:S(2)}) collective-permute-start(bf16[256,256]{1,0:T(8,128)(2,1)S(1)} %fusion.3), channel_id=1, source_target_pairs={{0,2},{2,0},{1,3},{3,1},{4,6},{6,4},{5,7},{7,5},{8,10},{10,8},{9,1... | collective-permute-start | bytes 393224 | tf_op jit(solution)/shard_map/ppermute | solution.py:22
  52.4 3.5 %collective-permute-done.5 = bf16[256,256]{1,0:T(8,128)(2,1)S(1)} collective-permute-done((bf16[256,256]{1,0:T(8,128)(2,1)S(1)}, bf16[256,256]{1,0:T(8,128)(2,1)S(1)}, u32[]{:S(2)}, u32[]{:S(2)}) %collective-permute-start.5) | collective-permute-done | bytes 131104 | tf_op jit(solution)/shard_map/ppermute | solution.py:22
  55.9 3.1 %collective-permute-start.6 = (bf16[256,256]{1,0:T(8,128)(2,1)S(1)}, bf16[256,256]{1,0:T(8,128)(2,1)S(1)}, u32[]{:S(2)}, u32[]{:S(2)}) collective-permute-start(bf16[256,256]{1,0:T(8,128)(2,1)S(1)} %broadcast_select_fusion), channel_id=1, source_target_pairs={{0,8},{4,12},{8,0},{12,4},{1,9},{5,13},{9,1},{13,5},{2,10},{6,14},... | collective-permute-start | bytes 393224 | tf_op jit(solution)/shard_map/ppermute | solution.py:27
  58.9 4.9 %collective-permute-done.6 = bf16[256,256]{1,0:T(8,128)(2,1)S(1)} collective-permute-done((bf16[256,256]{1,0:T(8,128)(2,1)S(1)}, bf16[256,256]{1,0:T(8,128)(2,1)S(1)}, u32[]{:S(2)}, u32[]{:S(2)}) %collective-permute-start.6) | collective-permute-done | bytes 131104 | tf_op jit(solution)/shard_map/ppermute | solution.py:27
  63.8 0.1 add_convert_fusion.refs_0_
  63.9 0.8 collective-permute-start.7
  64.7 1.3 %collective-permute-start.14 = (bf16[2,256,128]{2,1,0:T(8,128)(2,1)S(1)}, bf16[2,256,128]{2,1,0:T(8,128)(2,1)S(1)}, u32[]{:S(2)}, u32[]{:S(2)}) collective-permute-start(bf16[2,256,128]{2,1,0:T(8,128)(2,1)S(1)} %copy-done.12), channel_id=1, source_target_pairs={{0,4},{4,0},{8,12},{12,8},{1,5},{5,1},{9,13},{13,9},{2,6},{6,2},{1... | collective-permute-start | bytes 393224 | tf_op jit(solution)/shard_map/ppermute | solution.py:27
  66.0 2.2 %collective-permute-start.15 = (bf16[2,256,128]{2,1,0:T(8,128)(2,1)S(1)}, bf16[2,256,128]{2,1,0:T(8,128)(2,1)S(1)}, u32[]{:S(2)}, u32[]{:S(2)}) collective-permute-start(bf16[2,256,128]{2,1,0:T(8,128)(2,1)S(1)} %copy-done.10), channel_id=1, source_target_pairs={{0,8},{4,12},{8,0},{12,4},{1,9},{5,13},{9,1},{13,5},{2,10},{6,14},... | collective-permute-start | bytes 393224 | tf_op jit(solution)/shard_map/ppermute | solution.py:27
  68.1 1.4 %collective-permute-start.16 = (bf16[2,256,128]{2,1,0:T(8,128)(2,1)S(1)}, bf16[2,256,128]{2,1,0:T(8,128)(2,1)S(1)}, u32[]{:S(2)}, u32[]{:S(2)}) collective-permute-start(bf16[2,256,128]{2,1,0:T(8,128)(2,1)S(1)} %copy-done.8), channel_id=1, source_target_pairs={{0,12},{4,8},{8,4},{12,0},{1,13},{5,9},{9,5},{13,1},{2,14},{6,10},... | collective-permute-start | bytes 393224 | tf_op jit(solution)/shard_map/ppermute | solution.py:27
  69.6 0.7 collective-permute-done.7.refs_1_
  70.3 0.0 collective-permute-start.9
  70.3 2.0 %collective-permute-done.14.refs_5_ = bf16[2,256,128]{2,1,0:T(8,128)(2,1)S(1)} collective-permute-done((bf16[2,256,128]{2,1,0:T(8,128)(2,1)S(1)}, bf16[2,256,128]{2,1,0:T(8,128)(2,1)S(1)}, u32[]{:S(2)}, u32[]{:S(2)}) %collective-permute-start.14) | collective-permute-done | bytes 131104 | tf_op jit(solution)/shard_map/ppermute | solution.py:27
  72.4 0.4 collective-permute-start.10
  72.8 2.0 %collective-permute-done.15.refs_6_ = bf16[2,256,128]{2,1,0:T(8,128)(2,1)S(1)} collective-permute-done((bf16[2,256,128]{2,1,0:T(8,128)(2,1)S(1)}, bf16[2,256,128]{2,1,0:T(8,128)(2,1)S(1)}, u32[]{:S(2)}, u32[]{:S(2)}) %collective-permute-start.15) | collective-permute-done | bytes 131104 | tf_op jit(solution)/shard_map/ppermute | solution.py:27
  74.8 4.3 %collective-permute-start.11 = (bf16[2,256,128]{2,1,0:T(8,128)(2,1)S(1)}, bf16[2,256,128]{2,1,0:T(8,128)(2,1)S(1)}, u32[]{:S(2)}, u32[]{:S(2)}) collective-permute-start(bf16[2,256,128]{2,1,0:T(8,128)(2,1)S(1)} %copy-done.4), channel_id=1, source_target_pairs={{0,8},{4,12},{8,0},{12,4},{1,9},{5,13},{9,1},{13,5},{2,10},{6,14},... | collective-permute-start | bytes 393224 | tf_op jit(solution)/shard_map/ppermute | solution.py:27
  79.1 1.2 collective-permute-done.16.refs_7_
  80.2 1.1 collective-permute-start.12
  81.3 0.0 collective-permute-done.8.refs_2_
  81.3 1.7 %blocks.3 = (bf16[2,256,128]{2,1,0:T(8,128)(2,1)S(1)}, bf16[2,256,128]{2,1,0:T(8,128)(2,1)S(1)}, bf16[2,256,128]{2,1,0:T(8,128)(2,1)S(1)}, bf16[2,256,128]{2,1,0:T(8,128)(2,1)S(1)}) custom-call(s32[7]{0:T(128)S(1)} %stack.21.meta_ref, bf16[256,256]{1,0:T(8,128)(2,1)S(1)} %add_convert_fusion.refs_0_, bf16[256,256]{1,0:T(8,128)(2,1)S(1)} %collective-permute-done.7.refs_1_, ...), custom_call_target="tpu_custom_call" | custom-call | tf_op jit(solution)/shard_map/blocks/pallas_call | solution.py:414
  83.0 7.8 %collective-permute-start.21 = (bf16[2,256,128]{2,1,0:T(8,128)(2,1)S(1)}, bf16[2,256,128]{2,1,0:T(8,128)(2,1)S(1)}, u32[]{:S(2)}, u32[]{:S(2)}) collective-permute-start(bf16[2,256,128]{2,1,0:T(8,128)(2,1)S(1)} %get-tuple-element.82), channel_id=1, source_target_pairs={{0,4},{4,0},{8,12},{12,8},{1,5},{5,1},{9,13},{13,9},{2,6},{6,2},{1... | collective-permute-start | bytes 393224 | tf_op jit(solution)/shard_map/ppermute | solution.py:430
  90.9 1.7 %blocks.2 = (bf16[2,256,128]{2,1,0:T(8,128)(2,1)S(1)}, bf16[2,256,128]{2,1,0:T(8,128)(2,1)S(1)}, bf16[2,256,128]{2,1,0:T(8,128)(2,1)S(1)}, bf16[2,256,128]{2,1,0:T(8,128)(2,1)S(1)}) custom-call(s32[7]{0:T(128)S(1)} %stack.21.meta_ref, bf16[256,256]{1,0:T(8,128)(2,1)S(1)} %add_convert_fusion.refs_0_, bf16[256,256]{1,0:T(8,128)(2,1)S(1)} %collective-permute-done.7.refs_1_, ...), custom_call_target="tpu_custom_call" | custom-call | tf_op jit(solution)/shard_map/blocks/pallas_call | solution.py:414
  92.5 1.3 %collective-permute-start.20 = (bf16[2,256,128]{2,1,0:T(8,128)(2,1)S(1)}, bf16[2,256,128]{2,1,0:T(8,128)(2,1)S(1)}, u32[]{:S(2)}, u32[]{:S(2)}) collective-permute-start(bf16[2,256,128]{2,1,0:T(8,128)(2,1)S(1)} %get-tuple-element.81), channel_id=1, source_target_pairs={{0,4},{4,0},{8,12},{12,8},{1,5},{5,1},{9,13},{13,9},{2,6},{6,2},{1... | collective-permute-start | bytes 393224 | tf_op jit(solution)/shard_map/ppermute | solution.py:430
  93.8 1.5 %collective-permute-start.17 = (bf16[2,256,128]{2,1,0:T(8,128)(2,1)S(1)}, bf16[2,256,128]{2,1,0:T(8,128)(2,1)S(1)}, u32[]{:S(2)}, u32[]{:S(2)}) collective-permute-start(bf16[2,256,128]{2,1,0:T(8,128)(2,1)S(1)} %get-tuple-element.75), channel_id=1, source_target_pairs={{0,8},{4,12},{8,0},{12,4},{1,9},{5,13},{9,1},{13,5},{2,10},{6,14},... | collective-permute-start | bytes 393224 | tf_op jit(solution)/shard_map/ppermute | solution.py:430
  95.3 1.7 %collective-permute-start.19 = (bf16[2,256,128]{2,1,0:T(8,128)(2,1)S(1)}, bf16[2,256,128]{2,1,0:T(8,128)(2,1)S(1)}, u32[]{:S(2)}, u32[]{:S(2)}) collective-permute-start(bf16[2,256,128]{2,1,0:T(8,128)(2,1)S(1)} %get-tuple-element.77), channel_id=1, source_target_pairs={{0,12},{4,8},{8,4},{12,0},{1,13},{5,9},{9,5},{13,1},{2,14},{6,10},... | collective-permute-start | bytes 393224 | tf_op jit(solution)/shard_map/ppermute | solution.py:430
  97.0 1.8 %collective-permute-start.13 = (bf16[2,256,128]{2,1,0:T(8,128)(2,1)S(1)}, bf16[2,256,128]{2,1,0:T(8,128)(2,1)S(1)}, u32[]{:S(2)}, u32[]{:S(2)}) collective-permute-start(bf16[2,256,128]{2,1,0:T(8,128)(2,1)S(1)} %get-tuple-element.70), channel_id=1, source_target_pairs={{0,8},{4,12},{8,0},{12,4},{1,9},{5,13},{9,1},{13,5},{2,10},{6,14},... | collective-permute-start | bytes 393224 | tf_op jit(solution)/shard_map/ppermute | solution.py:430
  98.7 0.9 collective-permute-start.18
  99.6 1.7 %join.2.refs_4_ = bf16[2,2,512,256]{3,2,1,0:T(8,128)(2,1)} custom-call(s32[4]{0:T(128)S(1)} %pad_add_fusion.place_ref, bf16[256,256]{1,0:T(8,128)(2,1)S(1)} %get-tuple-element.45.move_ref, bf16[2,256,128]{2,1,0:T(8,128)(2,1)S(1)} %get-tuple-element.79.refs_0_, bf16[2,256,128]{2,1,0:T(8,128)(2,1)S(1)} %get-tuple-element.80.refs_1_, ...), custom_call_target="tpu_custom_call" | custom-call | tf_op jit(solution)/shard_map/join/pallas_call | solution.py:438
  101.4 9.2 %collective-permute-done.17.refs_1_ = bf16[2,256,128]{2,1,0:T(8,128)(2,1)S(1)} collective-permute-done((bf16[2,256,128]{2,1,0:T(8,128)(2,1)S(1)}, bf16[2,256,128]{2,1,0:T(8,128)(2,1)S(1)}, u32[]{:S(2)}, u32[]{:S(2)}) %collective-permute-start.17) | collective-permute-done | bytes 131104 | tf_op jit(solution)/shard_map/ppermute | solution.py:430
  110.5 5.6 %collective-permute-done.13.refs_0_ = bf16[2,256,128]{2,1,0:T(8,128)(2,1)S(1)} collective-permute-done((bf16[2,256,128]{2,1,0:T(8,128)(2,1)S(1)}, bf16[2,256,128]{2,1,0:T(8,128)(2,1)S(1)}, u32[]{:S(2)}, u32[]{:S(2)}) %collective-permute-start.13) | collective-permute-done | bytes 131104 | tf_op jit(solution)/shard_map/ppermute | solution.py:430
  116.2 1.8 %join.3 = bf16[2,2,512,256]{3,2,1,0:T(8,128)(2,1)} custom-call(s32[4]{0:T(128)S(1)} %pad_add_fusion.1.place_ref, bf16[256,256]{1,0:T(8,128)(2,1)S(1)} %get-tuple-element.45.move_ref, bf16[2,256,128]{2,1,0:T(8,128)(2,1)S(1)} %collective-permute-done.13.refs_0_, ...), custom_call_target="tpu_custom_call", output_to_operand_aliasing={{}: (6, {})} | custom-call | tf_op jit(solution)/shard_map/join/pallas_call | solution.py:438
  (48 shorter events, 0.2 us)
Async XLA Ops:
  0.0 10.3 %copy-start.14 = (s32[2]{0:T(128)S(1)}, s32[2]{0:T(128)}, u32[]{:S(2)}) copy-start(s32[2]{0:T(128)} %param.9) | copy-start | bytes 28
  0.0 10.4 %copy-start.13 = (s32[2,3]{1,0:T(2,128)S(1)}, s32[2,3]{1,0:T(2,128)}, u32[]{:S(2)}) copy-start(s32[2,3]{1,0:T(2,128)} %param.8) | copy-start | bytes 76
  0.0 10.6 %copy-start.15 = (s32[2,2]{1,0:T(2,128)S(1)}, s32[2,2]{1,0:T(2,128)}, u32[]{:S(2)}) copy-start(s32[2,2]{1,0:T(2,128)} %param.10) | copy-start | bytes 52
  0.0 15.2 %copy-start.1 = (bf16[2,2,512,256]{3,2,1,0:T(8,128)(2,1)S(1)}, bf16[2,2,512,256]{3,2,1,0:T(8,128)(2,1)}, u32[]{:S(2)}) copy-start(bf16[2,2,512,256]{3,2,1,0:T(8,128)(2,1)} %param.11) | copy-start | bytes 3145732
  1.8 18.0 %copy-start.2 = (f32[1,2,3,3,2,512]{5,4,3,2,1,0:T(2,128)S(1)}, f32[1,2,3,3,2,512]{5,4,3,2,1,0:T(2,128)}, u32[]{:S(2)}) copy-start(f32[1,2,3,3,2,512]{5,4,3,2,1,0:T(2,128)} %param.7) | copy-start | bytes 221188
  1.8 34.0 %collective-permute-start = (bf16[1,512,256]{2,1,0:T(8,128)(2,1)}, bf16[1,512,256]{2,1,0:T(8,128)(2,1)S(1)}, u32[]{:S(2)}, u32[]{:S(2)}) collective-permute-start(bf16[1,512,256]{2,1,0:T(8,128)(2,1)} %edge.2), channel_id=1, source_target_pairs={{0,12},{4,0},{8,4},{12,8},{1,13},{5,1},{9,5},{13,9},{2,14},{6,2},{... | collective-permute-start | bytes 786440 | tf_op jit(solution)/shard_map/ppermute | solution.py:22
  9.3 33.2 %collective-permute-start.2 = (bf16[1,512,256]{2,1,0:T(8,128)(2,1)}, bf16[1,512,256]{2,1,0:T(8,128)(2,1)S(1)}, u32[]{:S(2)}, u32[]{:S(2)}) collective-permute-start(bf16[1,512,256]{2,1,0:T(8,128)(2,1)} %get-tuple-element.62), channel_id=1, source_target_pairs={{0,12},{4,0},{8,4},{12,8},{1,13},{5,1},{9,5},{13,9},{2,14},{6,2},{... | collective-permute-start | bytes 786440 | tf_op jit(solution)/shard_map/ppermute | solution.py:22
  9.8 31.1 %collective-permute-start.1 = (bf16[4,512,256]{2,1,0:T(8,128)(2,1)}, bf16[4,512,256]{2,1,0:T(8,128)(2,1)S(1)}, u32[]{:S(2)}, u32[]{:S(2)}) collective-permute-start(bf16[4,512,256]{2,1,0:T(8,128)(2,1)} %get-tuple-element.61), channel_id=1, source_target_pairs={{0,12},{4,0},{8,4},{12,8},{1,13},{5,1},{9,5},{13,9},{2,14},{6,2},{... | collective-permute-start | bytes 3145736 | tf_op jit(solution)/shard_map/ppermute | solution.py:22
  16.5 0.6 copy-start.3
  17.1 0.7 copy-start.5
  17.8 0.6 copy-start.7
  18.4 0.7 copy-start.9
  19.1 0.6 copy-start.11
  19.7 1.9 %copy-start = (bf16[1,2,3,2,512,256]{5,4,3,2,1,0:T(8,128)(2,1)S(1)}, bf16[1,2,3,2,512,256]{5,4,3,2,1,0:T(8,128)(2,1)}, u32[]{:S(2)}) copy-start(bf16[1,2,3,2,512,256]{5,4,3,2,1,0:T(8,128)(2,1)} %param.6) | copy-start | bytes 9437188
  42.4 22.3 %copy-start.12 = (bf16[2,256,128]{2,1,0:T(8,128)(2,1)S(1)}, bf16[2,256,128]{2,1,0:T(8,128)(2,1)}, u32[]{:S(2)}) copy-start(bf16[2,256,128]{2,1,0:T(8,128)(2,1)} %copy-done.11) | copy-start | bytes 393220
  42.4 23.6 %copy-start.10 = (bf16[2,256,128]{2,1,0:T(8,128)(2,1)S(1)}, bf16[2,256,128]{2,1,0:T(8,128)(2,1)}, u32[]{:S(2)}) copy-start(bf16[2,256,128]{2,1,0:T(8,128)(2,1)} %copy-done.9) | copy-start | bytes 393220
  42.4 25.7 %copy-start.8 = (bf16[2,256,128]{2,1,0:T(8,128)(2,1)S(1)}, bf16[2,256,128]{2,1,0:T(8,128)(2,1)}, u32[]{:S(2)}) copy-start(bf16[2,256,128]{2,1,0:T(8,128)(2,1)} %copy-done.7) | copy-start | bytes 393220
  42.4 29.9 %copy-start.6 = (bf16[2,256,128]{2,1,0:T(8,128)(2,1)S(1)}, bf16[2,256,128]{2,1,0:T(8,128)(2,1)}, u32[]{:S(2)}) copy-start(bf16[2,256,128]{2,1,0:T(8,128)(2,1)} %copy-done.5) | copy-start | bytes 393220
  42.4 32.3 %copy-start.4 = (bf16[2,256,128]{2,1,0:T(8,128)(2,1)S(1)}, bf16[2,256,128]{2,1,0:T(8,128)(2,1)}, u32[]{:S(2)}) copy-start(bf16[2,256,128]{2,1,0:T(8,128)(2,1)} %copy-done.3) | copy-start | bytes 393220
  43.5 1.6 %collective-permute-start.3 = (bf16[2,256,256]{2,1,0:T(8,128)(2,1)S(1)}, bf16[2,256,256]{2,1,0:T(8,128)(2,1)S(1)}, u32[]{:S(2)}, u32[]{:S(2)}) collective-permute-start(bf16[2,256,256]{2,1,0:T(8,128)(2,1)S(1)} %get-tuple-element.64), channel_id=1, source_target_pairs={{0,1},{1,0},{2,3},{3,2},{4,5},{5,4},{6,7},{7,6},{8,9},{9,8},{10,11... | collective-permute-start | bytes 786440 | tf_op jit(solution)/shard_map/ppermute | solution.py:27
  45.2 5.6 %collective-permute-start.4 = (bf16[256,256]{1,0:T(8,128)(2,1)S(1)}, bf16[256,256]{1,0:T(8,128)(2,1)S(1)}, u32[]{:S(2)}, u32[]{:S(2)}) collective-permute-start(bf16[256,256]{1,0:T(8,128)(2,1)S(1)} %fusion.4), channel_id=1, source_target_pairs={{0,4},{4,0},{8,12},{12,8},{1,5},{5,1},{9,13},{13,9},{2,6},{6,2},{1... | collective-permute-start | bytes 393224 | tf_op jit(solution)/shard_map/ppermute | solution.py:27
  50.8 5.0 %collective-permute-start.5 = (bf16[256,256]{1,0:T(8,128)(2,1)S(1)}, bf16[256,256]{1,0:T(8,128)(2,1)S(1)}, u32[]{:S(2)}, u32[]{:S(2)}) collective-permute-start(bf16[256,256]{1,0:T(8,128)(2,1)S(1)} %fusion.3), channel_id=1, source_target_pairs={{0,2},{2,0},{1,3},{3,1},{4,6},{6,4},{5,7},{7,5},{8,10},{10,8},{9,1... | collective-permute-start | bytes 393224 | tf_op jit(solution)/shard_map/ppermute | solution.py:22
  55.9 7.9 %collective-permute-start.6 = (bf16[256,256]{1,0:T(8,128)(2,1)S(1)}, bf16[256,256]{1,0:T(8,128)(2,1)S(1)}, u32[]{:S(2)}, u32[]{:S(2)}) collective-permute-start(bf16[256,256]{1,0:T(8,128)(2,1)S(1)} %broadcast_select_fusion), channel_id=1, source_target_pairs={{0,8},{4,12},{8,0},{12,4},{1,9},{5,13},{9,1},{13,5},{2,10},{6,14},... | collective-permute-start | bytes 393224 | tf_op jit(solution)/shard_map/ppermute | solution.py:27
  63.9 6.4 %collective-permute-start.7 = (bf16[256,256]{1,0:T(8,128)(2,1)S(1)}, bf16[256,256]{1,0:T(8,128)(2,1)S(1)}, u32[]{:S(2)}, u32[]{:S(2)}) collective-permute-start(bf16[256,256]{1,0:T(8,128)(2,1)S(1)} %add_convert_fusion.refs_0_), channel_id=1, source_target_pairs={{0,4},{4,0},{8,12},{12,8},{1,5},{5,1},{9,13},{13,9},{2,6},{6,2},{1... | collective-permute-start | bytes 393224 | tf_op jit(solution)/shard_map/ppermute | solution.py:27
  64.7 7.7 %collective-permute-start.14 = (bf16[2,256,128]{2,1,0:T(8,128)(2,1)S(1)}, bf16[2,256,128]{2,1,0:T(8,128)(2,1)S(1)}, u32[]{:S(2)}, u32[]{:S(2)}) collective-permute-start(bf16[2,256,128]{2,1,0:T(8,128)(2,1)S(1)} %copy-done.12), channel_id=1, source_target_pairs={{0,4},{4,0},{8,12},{12,8},{1,5},{5,1},{9,13},{13,9},{2,6},{6,2},{1... | collective-permute-start | bytes 393224 | tf_op jit(solution)/shard_map/ppermute | solution.py:27
  66.0 8.8 %collective-permute-start.15 = (bf16[2,256,128]{2,1,0:T(8,128)(2,1)S(1)}, bf16[2,256,128]{2,1,0:T(8,128)(2,1)S(1)}, u32[]{:S(2)}, u32[]{:S(2)}) collective-permute-start(bf16[2,256,128]{2,1,0:T(8,128)(2,1)S(1)} %copy-done.10), channel_id=1, source_target_pairs={{0,8},{4,12},{8,0},{12,4},{1,9},{5,13},{9,1},{13,5},{2,10},{6,14},... | collective-permute-start | bytes 393224 | tf_op jit(solution)/shard_map/ppermute | solution.py:27
  68.1 12.1 %collective-permute-start.16 = (bf16[2,256,128]{2,1,0:T(8,128)(2,1)S(1)}, bf16[2,256,128]{2,1,0:T(8,128)(2,1)S(1)}, u32[]{:S(2)}, u32[]{:S(2)}) collective-permute-start(bf16[2,256,128]{2,1,0:T(8,128)(2,1)S(1)} %copy-done.8), channel_id=1, source_target_pairs={{0,12},{4,8},{8,4},{12,0},{1,13},{5,9},{9,5},{13,1},{2,14},{6,10},... | collective-permute-start | bytes 393224 | tf_op jit(solution)/shard_map/ppermute | solution.py:27
  69.6 11.8 %collective-permute-start.8 = (bf16[256,256]{1,0:T(8,128)(2,1)S(1)}, bf16[256,256]{1,0:T(8,128)(2,1)S(1)}, u32[]{:S(2)}, u32[]{:S(2)}) collective-permute-start(bf16[256,256]{1,0:T(8,128)(2,1)S(1)} %add_convert_fusion.refs_0_), channel_id=1, source_target_pairs={{0,1},{1,0},{2,3},{3,2},{4,5},{5,4},{6,7},{7,6},{8,9},{9,8},{10,11... | collective-permute-start | bytes 393224 | tf_op jit(solution)/shard_map/ppermute | solution.py:27
  70.3 11.0 %collective-permute-start.9 = (bf16[256,256]{1,0:T(8,128)(2,1)S(1)}, bf16[256,256]{1,0:T(8,128)(2,1)S(1)}, u32[]{:S(2)}, u32[]{:S(2)}) collective-permute-start(bf16[256,256]{1,0:T(8,128)(2,1)S(1)} %collective-permute-done.7.refs_1_), channel_id=1, source_target_pairs={{0,1},{1,0},{2,3},{3,2},{4,5},{5,4},{6,7},{7,6},{8,9},{9,8},{10,11... | collective-permute-start | bytes 393224 | tf_op jit(solution)/shard_map/ppermute | solution.py:27
  72.4 18.5 %collective-permute-start.10 = (bf16[2,256,128]{2,1,0:T(8,128)(2,1)S(1)}, bf16[2,256,128]{2,1,0:T(8,128)(2,1)S(1)}, u32[]{:S(2)}, u32[]{:S(2)}) collective-permute-start(bf16[2,256,128]{2,1,0:T(8,128)(2,1)S(1)} %copy-done.6), channel_id=1, source_target_pairs={{0,4},{4,0},{8,12},{12,8},{1,5},{5,1},{9,13},{13,9},{2,6},{6,2},{1... | collective-permute-start | bytes 393224 | tf_op jit(solution)/shard_map/ppermute | solution.py:27
  74.8 16.1 %collective-permute-start.11 = (bf16[2,256,128]{2,1,0:T(8,128)(2,1)S(1)}, bf16[2,256,128]{2,1,0:T(8,128)(2,1)S(1)}, u32[]{:S(2)}, u32[]{:S(2)}) collective-permute-start(bf16[2,256,128]{2,1,0:T(8,128)(2,1)S(1)} %copy-done.4), channel_id=1, source_target_pairs={{0,8},{4,12},{8,0},{12,4},{1,9},{5,13},{9,1},{13,5},{2,10},{6,14},... | collective-permute-start | bytes 393224 | tf_op jit(solution)/shard_map/ppermute | solution.py:27
  80.2 10.6 %collective-permute-start.12 = (bf16[2,256,128]{2,1,0:T(8,128)(2,1)S(1)}, bf16[2,256,128]{2,1,0:T(8,128)(2,1)S(1)}, u32[]{:S(2)}, u32[]{:S(2)}) collective-permute-start(bf16[2,256,128]{2,1,0:T(8,128)(2,1)S(1)} %get-tuple-element.69), channel_id=1, source_target_pairs={{0,12},{4,8},{8,4},{12,0},{1,13},{5,9},{9,5},{13,1},{2,14},{6,10},... | collective-permute-start | bytes 393224 | tf_op jit(solution)/shard_map/ppermute | solution.py:27
  83.0 15.7 %collective-permute-start.21 = (bf16[2,256,128]{2,1,0:T(8,128)(2,1)S(1)}, bf16[2,256,128]{2,1,0:T(8,128)(2,1)S(1)}, u32[]{:S(2)}, u32[]{:S(2)}) collective-permute-start(bf16[2,256,128]{2,1,0:T(8,128)(2,1)S(1)} %get-tuple-element.82), channel_id=1, source_target_pairs={{0,4},{4,0},{8,12},{12,8},{1,5},{5,1},{9,13},{13,9},{2,6},{6,2},{1... | collective-permute-start | bytes 393224 | tf_op jit(solution)/shard_map/ppermute | solution.py:430
  92.5 7.1 %collective-permute-start.20 = (bf16[2,256,128]{2,1,0:T(8,128)(2,1)S(1)}, bf16[2,256,128]{2,1,0:T(8,128)(2,1)S(1)}, u32[]{:S(2)}, u32[]{:S(2)}) collective-permute-start(bf16[2,256,128]{2,1,0:T(8,128)(2,1)S(1)} %get-tuple-element.81), channel_id=1, source_target_pairs={{0,4},{4,0},{8,12},{12,8},{1,5},{5,1},{9,13},{13,9},{2,6},{6,2},{1... | collective-permute-start | bytes 393224 | tf_op jit(solution)/shard_map/ppermute | solution.py:430
  93.8 16.8 %collective-permute-start.17 = (bf16[2,256,128]{2,1,0:T(8,128)(2,1)S(1)}, bf16[2,256,128]{2,1,0:T(8,128)(2,1)S(1)}, u32[]{:S(2)}, u32[]{:S(2)}) collective-permute-start(bf16[2,256,128]{2,1,0:T(8,128)(2,1)S(1)} %get-tuple-element.75), channel_id=1, source_target_pairs={{0,8},{4,12},{8,0},{12,4},{1,9},{5,13},{9,1},{13,5},{2,10},{6,14},... | collective-permute-start | bytes 393224 | tf_op jit(solution)/shard_map/ppermute | solution.py:430
  95.3 15.2 %collective-permute-start.19 = (bf16[2,256,128]{2,1,0:T(8,128)(2,1)S(1)}, bf16[2,256,128]{2,1,0:T(8,128)(2,1)S(1)}, u32[]{:S(2)}, u32[]{:S(2)}) collective-permute-start(bf16[2,256,128]{2,1,0:T(8,128)(2,1)S(1)} %get-tuple-element.77), channel_id=1, source_target_pairs={{0,12},{4,8},{8,4},{12,0},{1,13},{5,9},{9,5},{13,1},{2,14},{6,10},... | collective-permute-start | bytes 393224 | tf_op jit(solution)/shard_map/ppermute | solution.py:430
  97.0 19.2 %collective-permute-start.13 = (bf16[2,256,128]{2,1,0:T(8,128)(2,1)S(1)}, bf16[2,256,128]{2,1,0:T(8,128)(2,1)S(1)}, u32[]{:S(2)}, u32[]{:S(2)}) collective-permute-start(bf16[2,256,128]{2,1,0:T(8,128)(2,1)S(1)} %get-tuple-element.70), channel_id=1, source_target_pairs={{0,8},{4,12},{8,0},{12,4},{1,9},{5,13},{9,1},{13,5},{2,10},{6,14},... | collective-permute-start | bytes 393224 | tf_op jit(solution)/shard_map/ppermute | solution.py:430
  98.7 17.4 %collective-permute-start.18 = (bf16[2,256,128]{2,1,0:T(8,128)(2,1)S(1)}, bf16[2,256,128]{2,1,0:T(8,128)(2,1)S(1)}, u32[]{:S(2)}, u32[]{:S(2)}) collective-permute-start(bf16[2,256,128]{2,1,0:T(8,128)(2,1)S(1)} %get-tuple-element.76), channel_id=1, source_target_pairs={{0,12},{4,8},{8,4},{12,0},{1,13},{5,9},{9,5},{13,1},{2,14},{6,10},... | collective-permute-start | bytes 393224 | tf_op jit(solution)/shard_map/ppermute | solution.py:430

commit v3 on v2

--- a/solution.py
+++ b/solution.py
@@ -235,17 +235,27 @@
 
 
 def join_kernel(count, place_ref, move_ref, *refs):
-    out_ref = refs[-1]
+    out_ref, joined, given = refs[-3:]
+    vectors = joined.shape[2]
+    copies = []
     for which in range(count):
-
-        @pl.when(pl.program_id(0) == which)
-        def _():
-            cuts = refs[which * CUTS : (which + 1) * CUTS]
-            for part in range(2):
-                piece = jnp.concatenate([cut[part] for cut in cuts], axis=1)
-                out_ref[0, part] = jnp.dot(
-                    piece, move_ref[...], preferred_element_type=jnp.float32
-                ).astype(jnp.bfloat16)
+        cuts = refs[which * CUTS : (which + 1) * CUTS]
+        for part in range(2):
+            piece = jnp.concatenate([cut[part] for cut in cuts], axis=1)
+            joined[which, part] = jnp.dot(
+                piece, move_ref[...], preferred_element_type=jnp.float32
+            ).astype(jnp.bfloat16)
+        row = pl.multiple_of(place_ref[count + which] * vectors, vectors)
+        copies.append(
+            pltpu.make_async_copy(
+                joined.at[which],
+                out_ref.at[place_ref[which], :, pl.ds(row, vectors), :],
+                given.at[which],
+            )
+        )
+        copies[-1].start()
+    for copy in copies:
+        copy.wait()
 
 
 def body(eigenvectors, gauge_links, momenta, displacement, slice_pairs, perambulators):
@@ -437,17 +447,15 @@
         result = [
             pl.pallas_call(
                 functools.partial(join_kernel, span),
-                grid_spec=pltpu.PrefetchScalarGridSpec(
-                    num_scalar_prefetch=1,
-                    grid=(span,),
-                    in_specs=[vmem()] * (1 + span * CUTS)
-                    + [pl.BlockSpec(memory_space=pl.ANY)] * len(result),
-                    out_specs=pl.BlockSpec(
-                        (1, 2, vectors, width),
-                        lambda i, at, span=span: (at[i], 0, at[span + i], 0),
-                    ),
-                ),
+                in_specs=[smem()]
+                + [vmem()] * (1 + span * CUTS)
+                + [pl.BlockSpec(memory_space=pl.ANY)] * len(result),
+                out_specs=pl.BlockSpec(memory_space=pl.ANY),
                 out_shape=jax.ShapeDtypeStruct(perambulators.shape, bf16),
+                scratch_shapes=[
+                    pltpu.VMEM((span, 2, vectors, width), bf16),
+                    pltpu.SemaphoreType.DMA((span,)),
+                ],
                 input_output_aliases={2 + span * CUTS: 0} if result else {},
                 compiler_params=pltpu.CompilerParams(vmem_limit_bytes=6 << 20),
                 name="join",

time: 118 us -> 118 us (level)
  no operation moved by 1% of the time
where the time goes in v3:
time: 118 us
  waiting for transfers between devices  41 us (35%)
  starting transfers between devices  37.7 us (32%)
  Pallas kernels  28.5 us (24%)
  local copies, waits for them, and re-layouts  8.1 us (7%)
  between operations  1.57 us (1%)
    ppermute x12, waiting for transfers between devices, swap(): return lax.ppermute(x, axis, [(i, i ^ distance) for i in range(count)])  17.5 us
    ppermute x12, starting transfers between devices, swap(): return lax.ppermute(x, axis, [(i, i ^ distance) for i in range(count)])  15.1 us
    ppermute x6, waiting for transfers between devices, body(): piece = lax.ppermute(piece, 'slab', route)  14.9 us
    ppermute x6, starting transfers between devices, body(): piece = lax.ppermute(piece, 'slab', route)  14.9 us
    pallas_call x1, Pallas kernels, body(): pl.pallas_call(field_kernel, grid=(sites // block,), in_specs=[smem(), pl...  14.2 us
    ppermute x4, waiting for transfers between devices, shift(): return lax.ppermute(x, axis, [(i, (i + by) % count) for i in range(count)])  8.55 us
    ppermute x4, starting transfers between devices, shift(): return lax.ppermute(x, axis, [(i, (i + by) % count) for i in range(count)])  7.65 us
    unnamed x32, local copies, waits for them, and re-layouts  5.16 us
  transfers between devices with their start and end apart: 22, of which 11 were waited for; matrix products, arithmetic and copies ran while one was open for 3% of the time, Pallas kernels for 21%

profile of v3, /device:TPU:0, one launch (start us, length us, event | category | flops | bytes accessed | tf_op | source)
XLA Modules:
  0.0 117.7 jit_solution(18021947523621823975)
XLA Ops:
  0.0 1.7 %edge.2 = bf16[1,512,256]{2,1,0:T(8,128)(2,1)} custom-call(bf16[2,3,2,512,256]{4,3,2,1,0:T(8,128)(2,1)} %bitcast.21), custom_call_target="tpu_custom_call" | custom-call | tf_op jit(solution)/shard_map/edge/pallas_call | solution.py:273
  1.8 0.0 copy-start.2
  1.8 5.1 %collective-permute-start = (bf16[1,512,256]{2,1,0:T(8,128)(2,1)}, bf16[1,512,256]{2,1,0:T(8,128)(2,1)S(1)}, u32[]{:S(2)}, u32[]{:S(2)}) collective-permute-start(bf16[1,512,256]{2,1,0:T(8,128)(2,1)} %edge.2), channel_id=1, source_target_pairs={{0,12},{4,0},{8,4},{12,8},{1,13},{5,1},{9,5},{13,9},{2,14},{6,2},{... | collective-permute-start | bytes 786440 | tf_op jit(solution)/shard_map/ppermute | solution.py:22
  6.9 2.4 %edge.3 = (bf16[4,512,256]{2,1,0:T(8,128)(2,1)}, bf16[1,512,256]{2,1,0:T(8,128)(2,1)}) custom-call(bf16[2,3,2,512,256]{4,3,2,1,0:T(8,128)(2,1)} %bitcast.22), custom_call_target="tpu_custom_call" | custom-call | tf_op jit(solution)/shard_map/edge/pallas_call | solution.py:273
  9.3 0.5 collective-permute-start.2
  9.8 0.4 collective-permute-start.1
  10.3 0.1 rev.7
  10.4 0.2 slice_reduce_fusion.2
  10.7 0.1 fusion.17
  10.8 0.1 pad_add_fusion.1.place_ref
  10.8 0.6 fusion.20
  11.5 0.1 fusion.8
  11.5 0.2 fusion.5
  11.8 0.1 pad_add_fusion.place_ref
  11.8 0.7 fusion.19
  13.8 1.3 %stack.21.meta_ref = s32[7]{0:T(128)S(1)} concatenate(s32[1]{0:T(128)} %bitcast, s32[1]{0:T(128)} %bitcast.1, s32[1]{0:T(128)} %bitcast.2, s32[1]{0:T(128)} %bitcast.3, s32[1]{0:T(128)} %bitcast.4, s32[2]{0:T(128)S(1)} %copy-done.14), dimensions={0} | concatenate | bytes 56 | tf_op jit(solution)/shard_map/stack | solution.py:318
  15.1 0.1 fusion.2
  15.2 1.2 %deal.1 = (bf16[2,256,128]{2,1,0:T(8,128)(2,1)S(1)}, bf16[2,256,128]{2,1,0:T(8,128)(2,1)S(1)}, bf16[2,256,128]{2,1,0:T(8,128)(2,1)S(1)}, bf16[2,256,128]{2,1,0:T...) custom-call(s32[7]{0:T(128)S(1)} %stack.21.meta_ref, ...), custom_call_target="tpu_custom_call" | custom-call | tf_op jit(solution)/shard_map/deal/pallas_call | solution.py:367
  16.5 0.6 copy-done.3
  17.1 0.7 copy-done.5
  17.8 0.6 copy-done.7
  18.4 0.7 copy-done.9
  19.1 0.6 copy-done.11
  19.7 1.9 %copy-done = bf16[1,2,3,2,512,256]{5,4,3,2,1,0:T(8,128)(2,1)S(1)} copy-done((bf16[1,2,3,2,512,256]{5,4,3,2,1,0:T(8,128)(2,1)S(1)}, bf16[1,2,3,2,512,256]{5,4,3,2,1,0:T(8,128)(2,1)}, u32[]{:S(2)}) %copy-start) | copy-done | bytes 3145752
  21.6 14.2 %fields.1 = (f32[1024,512]{1,0:T(8,128)S(1)}, bf16[3,1024,512]{2,1,0:T(8,128)(2,1)S(1)}) custom-call(s32[7]{0:T(128)S(1)} %stack.21.meta_ref, bf16[2,3,2,512,256]{4,3,2,1,0:T(8,128)(2,1)S(1)} %bitcast.23, f32[18,2,512]{2,1,0:T(2,128)S(1)} %bitcast.25, f32[4,2,512]{2,1,0:T(2,128)S(1)} %bitcast.26), custom_call_target="tpu_custom_call" | custom-call | tf_op jit(solution)/shard_map/fields/pallas_call | solution.py:342
  35.8 5.1 %collective-permute-done.1.most_ref = bf16[4,512,256]{2,1,0:T(8,128)(2,1)S(1)} collective-permute-done((bf16[4,512,256]{2,1,0:T(8,128)(2,1)}, bf16[4,512,256]{2,1,0:T(8,128)(2,1)S(1)}, u32[]{:S(2)}, u32[]{:S(2)}) %collective-permute-start.1) | collective-permute-done | bytes 1048608 | tf_op jit(solution)/shard_map/ppermute | solution.py:22
  40.9 1.5 %most.1.total_ref = f32[2,2,256,256]{3,2,1,0:T(8,128)S(1)} custom-call(bf16[3,1024,512]{2,1,0:T(8,128)(2,1)S(1)} %get-tuple-element.59.outer_ref, f32[1024,512]{1,0:T(8,128)S(1)} %get-tuple-element.60.inner_ref, bf16[1,512,256]{2,1,0:T(8,128)(2,1)S(1)} %collective-permute-done.first_ref, bf16[4,512,256]{2,1,0:T(8,128)(2,1)S(1)} %collective-permute-done.1.most_ref), custom_call_target="tpu_custom_call" | custom-call | tf_op jit(solution)/shard_map/most/pallas_call | solution.py:377
  42.5 0.0 collective-permute-done.2.last_ref
  42.5 1.0 last.1
  43.5 0.1 collective-permute-start.3
  43.6 1.5 %collective-permute-done.3 = bf16[2,256,256]{2,1,0:T(8,128)(2,1)S(1)} collective-permute-done((bf16[2,256,256]{2,1,0:T(8,128)(2,1)S(1)}, bf16[2,256,256]{2,1,0:T(8,128)(2,1)S(1)}, u32[]{:S(2)}, u32[]{:S(2)}) %collective-permute-start.3) | collective-permute-done | bytes 262176 | tf_op jit(solution)/shard_map/ppermute | solution.py:27
  45.1 0.1 convert_add_fusion
  45.2 0.4 collective-permute-start.4
  45.6 5.2 %collective-permute-done.4 = bf16[256,256]{1,0:T(8,128)(2,1)S(1)} collective-permute-done((bf16[256,256]{1,0:T(8,128)(2,1)S(1)}, bf16[256,256]{1,0:T(8,128)(2,1)S(1)}, u32[]{:S(2)}, u32[]{:S(2)}) %collective-permute-start.4) | collective-permute-done | bytes 131104 | tf_op jit(solution)/shard_map/ppermute | solution.py:27
  50.8 1.6 %collective-permute-start.5 = (bf16[256,256]{1,0:T(8,128)(2,1)S(1)}, bf16[256,256]{1,0:T(8,128)(2,1)S(1)}, u32[]{:S(2)}, u32[]{:S(2)}) collective-permute-start(bf16[256,256]{1,0:T(8,128)(2,1)S(1)} %fusion.3), channel_id=1, source_target_pairs={{0,2},{2,0},{1,3},{3,1},{4,6},{6,4},{5,7},{7,5},{8,10},{10,8},{9,1... | collective-permute-start | bytes 393224 | tf_op jit(solution)/shard_map/ppermute | solution.py:22
  52.4 3.5 %collective-permute-done.5 = bf16[256,256]{1,0:T(8,128)(2,1)S(1)} collective-permute-done((bf16[256,256]{1,0:T(8,128)(2,1)S(1)}, bf16[256,256]{1,0:T(8,128)(2,1)S(1)}, u32[]{:S(2)}, u32[]{:S(2)}) %collective-permute-start.5) | collective-permute-done | bytes 131104 | tf_op jit(solution)/shard_map/ppermute | solution.py:22
  55.9 3.1 %collective-permute-start.6 = (bf16[256,256]{1,0:T(8,128)(2,1)S(1)}, bf16[256,256]{1,0:T(8,128)(2,1)S(1)}, u32[]{:S(2)}, u32[]{:S(2)}) collective-permute-start(bf16[256,256]{1,0:T(8,128)(2,1)S(1)} %broadcast_select_fusion), channel_id=1, source_target_pairs={{0,8},{4,12},{8,0},{12,4},{1,9},{5,13},{9,1},{13,5},{2,10},{6,14},... | collective-permute-start | bytes 393224 | tf_op jit(solution)/shard_map/ppermute | solution.py:27
  58.9 4.9 %collective-permute-done.6 = bf16[256,256]{1,0:T(8,128)(2,1)S(1)} collective-permute-done((bf16[256,256]{1,0:T(8,128)(2,1)S(1)}, bf16[256,256]{1,0:T(8,128)(2,1)S(1)}, u32[]{:S(2)}, u32[]{:S(2)}) %collective-permute-start.6) | collective-permute-done | bytes 131104 | tf_op jit(solution)/shard_map/ppermute | solution.py:27
  63.8 0.1 add_convert_fusion.refs_0_
  63.9 0.8 collective-permute-start.7
  64.7 1.3 %collective-permute-start.14 = (bf16[2,256,128]{2,1,0:T(8,128)(2,1)S(1)}, bf16[2,256,128]{2,1,0:T(8,128)(2,1)S(1)}, u32[]{:S(2)}, u32[]{:S(2)}) collective-permute-start(bf16[2,256,128]{2,1,0:T(8,128)(2,1)S(1)} %copy-done.12), channel_id=1, source_target_pairs={{0,4},{4,0},{8,12},{12,8},{1,5},{5,1},{9,13},{13,9},{2,6},{6,2},{1... | collective-permute-start | bytes 393224 | tf_op jit(solution)/shard_map/ppermute | solution.py:27
  66.0 2.2 %collective-permute-start.15 = (bf16[2,256,128]{2,1,0:T(8,128)(2,1)S(1)}, bf16[2,256,128]{2,1,0:T(8,128)(2,1)S(1)}, u32[]{:S(2)}, u32[]{:S(2)}) collective-permute-start(bf16[2,256,128]{2,1,0:T(8,128)(2,1)S(1)} %copy-done.10), channel_id=1, source_target_pairs={{0,8},{4,12},{8,0},{12,4},{1,9},{5,13},{9,1},{13,5},{2,10},{6,14},... | collective-permute-start | bytes 393224 | tf_op jit(solution)/shard_map/ppermute | solution.py:27
  68.1 1.4 %collective-permute-start.16 = (bf16[2,256,128]{2,1,0:T(8,128)(2,1)S(1)}, bf16[2,256,128]{2,1,0:T(8,128)(2,1)S(1)}, u32[]{:S(2)}, u32[]{:S(2)}) collective-permute-start(bf16[2,256,128]{2,1,0:T(8,128)(2,1)S(1)} %copy-done.8), channel_id=1, source_target_pairs={{0,12},{4,8},{8,4},{12,0},{1,13},{5,9},{9,5},{13,1},{2,14},{6,10},... | collective-permute-start | bytes 393224 | tf_op jit(solution)/shard_map/ppermute | solution.py:27
  69.6 0.7 collective-permute-done.7.refs_1_
  70.3 0.0 collective-permute-start.9
  70.3 2.0 %collective-permute-done.14.refs_5_ = bf16[2,256,128]{2,1,0:T(8,128)(2,1)S(1)} collective-permute-done((bf16[2,256,128]{2,1,0:T(8,128)(2,1)S(1)}, bf16[2,256,128]{2,1,0:T(8,128)(2,1)S(1)}, u32[]{:S(2)}, u32[]{:S(2)}) %collective-permute-start.14) | collective-permute-done | bytes 131104 | tf_op jit(solution)/shard_map/ppermute | solution.py:27
  72.4 0.4 collective-permute-start.10
  72.8 2.0 %collective-permute-done.15.refs_6_ = bf16[2,256,128]{2,1,0:T(8,128)(2,1)S(1)} collective-permute-done((bf16[2,256,128]{2,1,0:T(8,128)(2,1)S(1)}, bf16[2,256,128]{2,1,0:T(8,128)(2,1)S(1)}, u32[]{:S(2)}, u32[]{:S(2)}) %collective-permute-start.15) | collective-permute-done | bytes 131104 | tf_op jit(solution)/shard_map/ppermute | solution.py:27
  74.8 4.3 %collective-permute-start.11 = (bf16[2,256,128]{2,1,0:T(8,128)(2,1)S(1)}, bf16[2,256,128]{2,1,0:T(8,128)(2,1)S(1)}, u32[]{:S(2)}, u32[]{:S(2)}) collective-permute-start(bf16[2,256,128]{2,1,0:T(8,128)(2,1)S(1)} %copy-done.4), channel_id=1, source_target_pairs={{0,8},{4,12},{8,0},{12,4},{1,9},{5,13},{9,1},{13,5},{2,10},{6,14},... | collective-permute-start | bytes 393224 | tf_op jit(solution)/shard_map/ppermute | solution.py:27
  79.1 1.2 collective-permute-done.16.refs_7_
  80.2 1.1 collective-permute-start.12
  81.3 0.0 collective-permute-done.8.refs_2_
  81.3 1.7 %blocks.3 = (bf16[2,256,128]{2,1,0:T(8,128)(2,1)S(1)}, bf16[2,256,128]{2,1,0:T(8,128)(2,1)S(1)}, bf16[2,256,128]{2,1,0:T(8,128)(2,1)S(1)}, bf16[2,256,128]{2,1,0:T(8,128)(2,1)S(1)}) custom-call(s32[7]{0:T(128)S(1)} %stack.21.meta_ref, bf16[256,256]{1,0:T(8,128)(2,1)S(1)} %add_convert_fusion.refs_0_, bf16[256,256]{1,0:T(8,128)(2,1)S(1)} %collective-permute-done.7.refs_1_, ...), custom_call_target="tpu_custom_call" | custom-call | tf_op jit(solution)/shard_map/blocks/pallas_call | solution.py:424
  83.0 7.8 %collective-permute-start.21 = (bf16[2,256,128]{2,1,0:T(8,128)(2,1)S(1)}, bf16[2,256,128]{2,1,0:T(8,128)(2,1)S(1)}, u32[]{:S(2)}, u32[]{:S(2)}) collective-permute-start(bf16[2,256,128]{2,1,0:T(8,128)(2,1)S(1)} %get-tuple-element.82), channel_id=1, source_target_pairs={{0,4},{4,0},{8,12},{12,8},{1,5},{5,1},{9,13},{13,9},{2,6},{6,2},{1... | collective-permute-start | bytes 393224 | tf_op jit(solution)/shard_map/ppermute | solution.py:440
  90.9 1.7 %blocks.2 = (bf16[2,256,128]{2,1,0:T(8,128)(2,1)S(1)}, bf16[2,256,128]{2,1,0:T(8,128)(2,1)S(1)}, bf16[2,256,128]{2,1,0:T(8,128)(2,1)S(1)}, bf16[2,256,128]{2,1,0:T(8,128)(2,1)S(1)}) custom-call(s32[7]{0:T(128)S(1)} %stack.21.meta_ref, bf16[256,256]{1,0:T(8,128)(2,1)S(1)} %add_convert_fusion.refs_0_, bf16[256,256]{1,0:T(8,128)(2,1)S(1)} %collective-permute-done.7.refs_1_, ...), custom_call_target="tpu_custom_call" | custom-call | tf_op jit(solution)/shard_map/blocks/pallas_call | solution.py:424
  92.5 1.3 %collective-permute-start.20 = (bf16[2,256,128]{2,1,0:T(8,128)(2,1)S(1)}, bf16[2,256,128]{2,1,0:T(8,128)(2,1)S(1)}, u32[]{:S(2)}, u32[]{:S(2)}) collective-permute-start(bf16[2,256,128]{2,1,0:T(8,128)(2,1)S(1)} %get-tuple-element.81), channel_id=1, source_target_pairs={{0,4},{4,0},{8,12},{12,8},{1,5},{5,1},{9,13},{13,9},{2,6},{6,2},{1... | collective-permute-start | bytes 393224 | tf_op jit(solution)/shard_map/ppermute | solution.py:440
  93.8 1.5 %collective-permute-start.17 = (bf16[2,256,128]{2,1,0:T(8,128)(2,1)S(1)}, bf16[2,256,128]{2,1,0:T(8,128)(2,1)S(1)}, u32[]{:S(2)}, u32[]{:S(2)}) collective-permute-start(bf16[2,256,128]{2,1,0:T(8,128)(2,1)S(1)} %get-tuple-element.75), channel_id=1, source_target_pairs={{0,8},{4,12},{8,0},{12,4},{1,9},{5,13},{9,1},{13,5},{2,10},{6,14},... | collective-permute-start | bytes 393224 | tf_op jit(solution)/shard_map/ppermute | solution.py:440
  95.3 1.7 %collective-permute-start.19 = (bf16[2,256,128]{2,1,0:T(8,128)(2,1)S(1)}, bf16[2,256,128]{2,1,0:T(8,128)(2,1)S(1)}, u32[]{:S(2)}, u32[]{:S(2)}) collective-permute-start(bf16[2,256,128]{2,1,0:T(8,128)(2,1)S(1)} %get-tuple-element.77), channel_id=1, source_target_pairs={{0,12},{4,8},{8,4},{12,0},{1,13},{5,9},{9,5},{13,1},{2,14},{6,10},... | collective-permute-start | bytes 393224 | tf_op jit(solution)/shard_map/ppermute | solution.py:440
  97.0 1.8 %collective-permute-start.13 = (bf16[2,256,128]{2,1,0:T(8,128)(2,1)S(1)}, bf16[2,256,128]{2,1,0:T(8,128)(2,1)S(1)}, u32[]{:S(2)}, u32[]{:S(2)}) collective-permute-start(bf16[2,256,128]{2,1,0:T(8,128)(2,1)S(1)} %get-tuple-element.70), channel_id=1, source_target_pairs={{0,8},{4,12},{8,0},{12,4},{1,9},{5,13},{9,1},{13,5},{2,10},{6,14},... | collective-permute-start | bytes 393224 | tf_op jit(solution)/shard_map/ppermute | solution.py:440
  98.7 0.9 collective-permute-start.18
  99.6 1.6 %join.2.refs_4_ = bf16[2,2,512,256]{3,2,1,0:T(8,128)(2,1)} custom-call(s32[4]{0:T(128)S(1)} %pad_add_fusion.place_ref, bf16[256,256]{1,0:T(8,128)(2,1)S(1)} %get-tuple-element.45.move_ref, bf16[2,256,128]{2,1,0:T(8,128)(2,1)S(1)} %get-tuple-element.79.refs_0_, bf16[2,256,128]{2,1,0:T(8,128)(2,1)S(1)} %get-tuple-element.80.refs_1_, ...), custom_call_target="tpu_custom_call" | custom-call | tf_op jit(solution)/shard_map/join/pallas_call | solution.py:448
  101.2 9.3 %collective-permute-done.17.refs_1_ = bf16[2,256,128]{2,1,0:T(8,128)(2,1)S(1)} collective-permute-done((bf16[2,256,128]{2,1,0:T(8,128)(2,1)S(1)}, bf16[2,256,128]{2,1,0:T(8,128)(2,1)S(1)}, u32[]{:S(2)}, u32[]{:S(2)}) %collective-permute-start.17) | collective-permute-done | bytes 131104 | tf_op jit(solution)/shard_map/ppermute | solution.py:440
  110.5 5.6 %collective-permute-done.13.refs_0_ = bf16[2,256,128]{2,1,0:T(8,128)(2,1)S(1)} collective-permute-done((bf16[2,256,128]{2,1,0:T(8,128)(2,1)S(1)}, bf16[2,256,128]{2,1,0:T(8,128)(2,1)S(1)}, u32[]{:S(2)}, u32[]{:S(2)}) %collective-permute-start.13) | collective-permute-done | bytes 131104 | tf_op jit(solution)/shard_map/ppermute | solution.py:440
  116.2 1.6 %join.3 = bf16[2,2,512,256]{3,2,1,0:T(8,128)(2,1)} custom-call(s32[4]{0:T(128)S(1)} %pad_add_fusion.1.place_ref, bf16[256,256]{1,0:T(8,128)(2,1)S(1)} %get-tuple-element.45.move_ref, bf16[2,256,128]{2,1,0:T(8,128)(2,1)S(1)} %collective-permute-done.13.refs_0_, ...), custom_call_target="tpu_custom_call", output_to_operand_aliasing={{}: (6, {})} | custom-call | tf_op jit(solution)/shard_map/join/pallas_call | solution.py:448
  (48 shorter events, 0.2 us)
Async XLA Ops:
  0.0 10.3 %copy-start.14 = (s32[2]{0:T(128)S(1)}, s32[2]{0:T(128)}, u32[]{:S(2)}) copy-start(s32[2]{0:T(128)} %param.9) | copy-start | bytes 28
  0.0 10.4 %copy-start.13 = (s32[2,3]{1,0:T(2,128)S(1)}, s32[2,3]{1,0:T(2,128)}, u32[]{:S(2)}) copy-start(s32[2,3]{1,0:T(2,128)} %param.8) | copy-start | bytes 76
  0.0 10.6 %copy-start.15 = (s32[2,2]{1,0:T(2,128)S(1)}, s32[2,2]{1,0:T(2,128)}, u32[]{:S(2)}) copy-start(s32[2,2]{1,0:T(2,128)} %param.10) | copy-start | bytes 52
  0.0 15.2 %copy-start.1 = (bf16[2,2,512,256]{3,2,1,0:T(8,128)(2,1)S(1)}, bf16[2,2,512,256]{3,2,1,0:T(8,128)(2,1)}, u32[]{:S(2)}) copy-start(bf16[2,2,512,256]{3,2,1,0:T(8,128)(2,1)} %param.11) | copy-start | bytes 3145732
  1.8 18.0 %copy-start.2 = (f32[1,2,3,3,2,512]{5,4,3,2,1,0:T(2,128)S(1)}, f32[1,2,3,3,2,512]{5,4,3,2,1,0:T(2,128)}, u32[]{:S(2)}) copy-start(f32[1,2,3,3,2,512]{5,4,3,2,1,0:T(2,128)} %param.7) | copy-start | bytes 221188
  1.8 34.0 %collective-permute-start = (bf16[1,512,256]{2,1,0:T(8,128)(2,1)}, bf16[1,512,256]{2,1,0:T(8,128)(2,1)S(1)}, u32[]{:S(2)}, u32[]{:S(2)}) collective-permute-start(bf16[1,512,256]{2,1,0:T(8,128)(2,1)} %edge.2), channel_id=1, source_target_pairs={{0,12},{4,0},{8,4},{12,8},{1,13},{5,1},{9,5},{13,9},{2,14},{6,2},{... | collective-permute-start | bytes 786440 | tf_op jit(solution)/shard_map/ppermute | solution.py:22
  9.3 33.2 %collective-permute-start.2 = (bf16[1,512,256]{2,1,0:T(8,128)(2,1)}, bf16[1,512,256]{2,1,0:T(8,128)(2,1)S(1)}, u32[]{:S(2)}, u32[]{:S(2)}) collective-permute-start(bf16[1,512,256]{2,1,0:T(8,128)(2,1)} %get-tuple-element.62), channel_id=1, source_target_pairs={{0,12},{4,0},{8,4},{12,8},{1,13},{5,1},{9,5},{13,9},{2,14},{6,2},{... | collective-permute-start | bytes 786440 | tf_op jit(solution)/shard_map/ppermute | solution.py:22
  9.8 31.1 %collective-permute-start.1 = (bf16[4,512,256]{2,1,0:T(8,128)(2,1)}, bf16[4,512,256]{2,1,0:T(8,128)(2,1)S(1)}, u32[]{:S(2)}, u32[]{:S(2)}) collective-permute-start(bf16[4,512,256]{2,1,0:T(8,128)(2,1)} %get-tuple-element.61), channel_id=1, source_target_pairs={{0,12},{4,0},{8,4},{12,8},{1,13},{5,1},{9,5},{13,9},{2,14},{6,2},{... | collective-permute-start | bytes 3145736 | tf_op jit(solution)/shard_map/ppermute | solution.py:22
  16.5 0.6 copy-start.3
  17.1 0.7 copy-start.5
  17.8 0.6 copy-start.7
  18.4 0.7 copy-start.9
  19.1 0.6 copy-start.11
  19.7 1.9 %copy-start = (bf16[1,2,3,2,512,256]{5,4,3,2,1,0:T(8,128)(2,1)S(1)}, bf16[1,2,3,2,512,256]{5,4,3,2,1,0:T(8,128)(2,1)}, u32[]{:S(2)}) copy-start(bf16[1,2,3,2,512,256]{5,4,3,2,1,0:T(8,128)(2,1)} %param.6) | copy-start | bytes 9437188
  42.4 22.3 %copy-start.12 = (bf16[2,256,128]{2,1,0:T(8,128)(2,1)S(1)}, bf16[2,256,128]{2,1,0:T(8,128)(2,1)}, u32[]{:S(2)}) copy-start(bf16[2,256,128]{2,1,0:T(8,128)(2,1)} %copy-done.11) | copy-start | bytes 393220
  42.4 23.6 %copy-start.10 = (bf16[2,256,128]{2,1,0:T(8,128)(2,1)S(1)}, bf16[2,256,128]{2,1,0:T(8,128)(2,1)}, u32[]{:S(2)}) copy-start(bf16[2,256,128]{2,1,0:T(8,128)(2,1)} %copy-done.9) | copy-start | bytes 393220
  42.4 25.7 %copy-start.8 = (bf16[2,256,128]{2,1,0:T(8,128)(2,1)S(1)}, bf16[2,256,128]{2,1,0:T(8,128)(2,1)}, u32[]{:S(2)}) copy-start(bf16[2,256,128]{2,1,0:T(8,128)(2,1)} %copy-done.7) | copy-start | bytes 393220
  42.4 29.9 %copy-start.6 = (bf16[2,256,128]{2,1,0:T(8,128)(2,1)S(1)}, bf16[2,256,128]{2,1,0:T(8,128)(2,1)}, u32[]{:S(2)}) copy-start(bf16[2,256,128]{2,1,0:T(8,128)(2,1)} %copy-done.5) | copy-start | bytes 393220
  42.4 32.3 %copy-start.4 = (bf16[2,256,128]{2,1,0:T(8,128)(2,1)S(1)}, bf16[2,256,128]{2,1,0:T(8,128)(2,1)}, u32[]{:S(2)}) copy-start(bf16[2,256,128]{2,1,0:T(8,128)(2,1)} %copy-done.3) | copy-start | bytes 393220
  43.5 1.6 %collective-permute-start.3 = (bf16[2,256,256]{2,1,0:T(8,128)(2,1)S(1)}, bf16[2,256,256]{2,1,0:T(8,128)(2,1)S(1)}, u32[]{:S(2)}, u32[]{:S(2)}) collective-permute-start(bf16[2,256,256]{2,1,0:T(8,128)(2,1)S(1)} %get-tuple-element.64), channel_id=1, source_target_pairs={{0,1},{1,0},{2,3},{3,2},{4,5},{5,4},{6,7},{7,6},{8,9},{9,8},{10,11... | collective-permute-start | bytes 786440 | tf_op jit(solution)/shard_map/ppermute | solution.py:27
  45.2 5.6 %collective-permute-start.4 = (bf16[256,256]{1,0:T(8,128)(2,1)S(1)}, bf16[256,256]{1,0:T(8,128)(2,1)S(1)}, u32[]{:S(2)}, u32[]{:S(2)}) collective-permute-start(bf16[256,256]{1,0:T(8,128)(2,1)S(1)} %fusion.4), channel_id=1, source_target_pairs={{0,4},{4,0},{8,12},{12,8},{1,5},{5,1},{9,13},{13,9},{2,6},{6,2},{1... | collective-permute-start | bytes 393224 | tf_op jit(solution)/shard_map/ppermute | solution.py:27
  50.8 5.0 %collective-permute-start.5 = (bf16[256,256]{1,0:T(8,128)(2,1)S(1)}, bf16[256,256]{1,0:T(8,128)(2,1)S(1)}, u32[]{:S(2)}, u32[]{:S(2)}) collective-permute-start(bf16[256,256]{1,0:T(8,128)(2,1)S(1)} %fusion.3), channel_id=1, source_target_pairs={{0,2},{2,0},{1,3},{3,1},{4,6},{6,4},{5,7},{7,5},{8,10},{10,8},{9,1... | collective-permute-start | bytes 393224 | tf_op jit(solution)/shard_map/ppermute | solution.py:22
  55.9 7.9 %collective-permute-start.6 = (bf16[256,256]{1,0:T(8,128)(2,1)S(1)}, bf16[256,256]{1,0:T(8,128)(2,1)S(1)}, u32[]{:S(2)}, u32[]{:S(2)}) collective-permute-start(bf16[256,256]{1,0:T(8,128)(2,1)S(1)} %broadcast_select_fusion), channel_id=1, source_target_pairs={{0,8},{4,12},{8,0},{12,4},{1,9},{5,13},{9,1},{13,5},{2,10},{6,14},... | collective-permute-start | bytes 393224 | tf_op jit(solution)/shard_map/ppermute | solution.py:27
  63.9 6.4 %collective-permute-start.7 = (bf16[256,256]{1,0:T(8,128)(2,1)S(1)}, bf16[256,256]{1,0:T(8,128)(2,1)S(1)}, u32[]{:S(2)}, u32[]{:S(2)}) collective-permute-start(bf16[256,256]{1,0:T(8,128)(2,1)S(1)} %add_convert_fusion.refs_0_), channel_id=1, source_target_pairs={{0,4},{4,0},{8,12},{12,8},{1,5},{5,1},{9,13},{13,9},{2,6},{6,2},{1... | collective-permute-start | bytes 393224 | tf_op jit(solution)/shard_map/ppermute | solution.py:27
  64.7 7.7 %collective-permute-start.14 = (bf16[2,256,128]{2,1,0:T(8,128)(2,1)S(1)}, bf16[2,256,128]{2,1,0:T(8,128)(2,1)S(1)}, u32[]{:S(2)}, u32[]{:S(2)}) collective-permute-start(bf16[2,256,128]{2,1,0:T(8,128)(2,1)S(1)} %copy-done.12), channel_id=1, source_target_pairs={{0,4},{4,0},{8,12},{12,8},{1,5},{5,1},{9,13},{13,9},{2,6},{6,2},{1... | collective-permute-start | bytes 393224 | tf_op jit(solution)/shard_map/ppermute | solution.py:27
  66.0 8.8 %collective-permute-start.15 = (bf16[2,256,128]{2,1,0:T(8,128)(2,1)S(1)}, bf16[2,256,128]{2,1,0:T(8,128)(2,1)S(1)}, u32[]{:S(2)}, u32[]{:S(2)}) collective-permute-start(bf16[2,256,128]{2,1,0:T(8,128)(2,1)S(1)} %copy-done.10), channel_id=1, source_target_pairs={{0,8},{4,12},{8,0},{12,4},{1,9},{5,13},{9,1},{13,5},{2,10},{6,14},... | collective-permute-start | bytes 393224 | tf_op jit(solution)/shard_map/ppermute | solution.py:27
  68.1 12.1 %collective-permute-start.16 = (bf16[2,256,128]{2,1,0:T(8,128)(2,1)S(1)}, bf16[2,256,128]{2,1,0:T(8,128)(2,1)S(1)}, u32[]{:S(2)}, u32[]{:S(2)}) collective-permute-start(bf16[2,256,128]{2,1,0:T(8,128)(2,1)S(1)} %copy-done.8), channel_id=1, source_target_pairs={{0,12},{4,8},{8,4},{12,0},{1,13},{5,9},{9,5},{13,1},{2,14},{6,10},... | collective-permute-start | bytes 393224 | tf_op jit(solution)/shard_map/ppermute | solution.py:27
  69.6 11.8 %collective-permute-start.8 = (bf16[256,256]{1,0:T(8,128)(2,1)S(1)}, bf16[256,256]{1,0:T(8,128)(2,1)S(1)}, u32[]{:S(2)}, u32[]{:S(2)}) collective-permute-start(bf16[256,256]{1,0:T(8,128)(2,1)S(1)} %add_convert_fusion.refs_0_), channel_id=1, source_target_pairs={{0,1},{1,0},{2,3},{3,2},{4,5},{5,4},{6,7},{7,6},{8,9},{9,8},{10,11... | collective-permute-start | bytes 393224 | tf_op jit(solution)/shard_map/ppermute | solution.py:27
  70.3 11.0 %collective-permute-start.9 = (bf16[256,256]{1,0:T(8,128)(2,1)S(1)}, bf16[256,256]{1,0:T(8,128)(2,1)S(1)}, u32[]{:S(2)}, u32[]{:S(2)}) collective-permute-start(bf16[256,256]{1,0:T(8,128)(2,1)S(1)} %collective-permute-done.7.refs_1_), channel_id=1, source_target_pairs={{0,1},{1,0},{2,3},{3,2},{4,5},{5,4},{6,7},{7,6},{8,9},{9,8},{10,11... | collective-permute-start | bytes 393224 | tf_op jit(solution)/shard_map/ppermute | solution.py:27
  72.4 18.5 %collective-permute-start.10 = (bf16[2,256,128]{2,1,0:T(8,128)(2,1)S(1)}, bf16[2,256,128]{2,1,0:T(8,128)(2,1)S(1)}, u32[]{:S(2)}, u32[]{:S(2)}) collective-permute-start(bf16[2,256,128]{2,1,0:T(8,128)(2,1)S(1)} %copy-done.6), channel_id=1, source_target_pairs={{0,4},{4,0},{8,12},{12,8},{1,5},{5,1},{9,13},{13,9},{2,6},{6,2},{1... | collective-permute-start | bytes 393224 | tf_op jit(solution)/shard_map/ppermute | solution.py:27
  74.8 16.1 %collective-permute-start.11 = (bf16[2,256,128]{2,1,0:T(8,128)(2,1)S(1)}, bf16[2,256,128]{2,1,0:T(8,128)(2,1)S(1)}, u32[]{:S(2)}, u32[]{:S(2)}) collective-permute-start(bf16[2,256,128]{2,1,0:T(8,128)(2,1)S(1)} %copy-done.4), channel_id=1, source_target_pairs={{0,8},{4,12},{8,0},{12,4},{1,9},{5,13},{9,1},{13,5},{2,10},{6,14},... | collective-permute-start | bytes 393224 | tf_op jit(solution)/shard_map/ppermute | solution.py:27
  80.2 10.6 %collective-permute-start.12 = (bf16[2,256,128]{2,1,0:T(8,128)(2,1)S(1)}, bf16[2,256,128]{2,1,0:T(8,128)(2,1)S(1)}, u32[]{:S(2)}, u32[]{:S(2)}) collective-permute-start(bf16[2,256,128]{2,1,0:T(8,128)(2,1)S(1)} %get-tuple-element.69), channel_id=1, source_target_pairs={{0,12},{4,8},{8,4},{12,0},{1,13},{5,9},{9,5},{13,1},{2,14},{6,10},... | collective-permute-start | bytes 393224 | tf_op jit(solution)/shard_map/ppermute | solution.py:27
  83.0 15.7 %collective-permute-start.21 = (bf16[2,256,128]{2,1,0:T(8,128)(2,1)S(1)}, bf16[2,256,128]{2,1,0:T(8,128)(2,1)S(1)}, u32[]{:S(2)}, u32[]{:S(2)}) collective-permute-start(bf16[2,256,128]{2,1,0:T(8,128)(2,1)S(1)} %get-tuple-element.82), channel_id=1, source_target_pairs={{0,4},{4,0},{8,12},{12,8},{1,5},{5,1},{9,13},{13,9},{2,6},{6,2},{1... | collective-permute-start | bytes 393224 | tf_op jit(solution)/shard_map/ppermute | solution.py:440
  92.5 7.1 %collective-permute-start.20 = (bf16[2,256,128]{2,1,0:T(8,128)(2,1)S(1)}, bf16[2,256,128]{2,1,0:T(8,128)(2,1)S(1)}, u32[]{:S(2)}, u32[]{:S(2)}) collective-permute-start(bf16[2,256,128]{2,1,0:T(8,128)(2,1)S(1)} %get-tuple-element.81), channel_id=1, source_target_pairs={{0,4},{4,0},{8,12},{12,8},{1,5},{5,1},{9,13},{13,9},{2,6},{6,2},{1... | collective-permute-start | bytes 393224 | tf_op jit(solution)/shard_map/ppermute | solution.py:440
  93.8 16.8 %collective-permute-start.17 = (bf16[2,256,128]{2,1,0:T(8,128)(2,1)S(1)}, bf16[2,256,128]{2,1,0:T(8,128)(2,1)S(1)}, u32[]{:S(2)}, u32[]{:S(2)}) collective-permute-start(bf16[2,256,128]{2,1,0:T(8,128)(2,1)S(1)} %get-tuple-element.75), channel_id=1, source_target_pairs={{0,8},{4,12},{8,0},{12,4},{1,9},{5,13},{9,1},{13,5},{2,10},{6,14},... | collective-permute-start | bytes 393224 | tf_op jit(solution)/shard_map/ppermute | solution.py:440
  95.3 15.2 %collective-permute-start.19 = (bf16[2,256,128]{2,1,0:T(8,128)(2,1)S(1)}, bf16[2,256,128]{2,1,0:T(8,128)(2,1)S(1)}, u32[]{:S(2)}, u32[]{:S(2)}) collective-permute-start(bf16[2,256,128]{2,1,0:T(8,128)(2,1)S(1)} %get-tuple-element.77), channel_id=1, source_target_pairs={{0,12},{4,8},{8,4},{12,0},{1,13},{5,9},{9,5},{13,1},{2,14},{6,10},... | collective-permute-start | bytes 393224 | tf_op jit(solution)/shard_map/ppermute | solution.py:440
  97.0 19.2 %collective-permute-start.13 = (bf16[2,256,128]{2,1,0:T(8,128)(2,1)S(1)}, bf16[2,256,128]{2,1,0:T(8,128)(2,1)S(1)}, u32[]{:S(2)}, u32[]{:S(2)}) collective-permute-start(bf16[2,256,128]{2,1,0:T(8,128)(2,1)S(1)} %get-tuple-element.70), channel_id=1, source_target_pairs={{0,8},{4,12},{8,0},{12,4},{1,9},{5,13},{9,1},{13,5},{2,10},{6,14},... | collective-permute-start | bytes 393224 | tf_op jit(solution)/shard_map/ppermute | solution.py:440
  98.7 17.4 %collective-permute-start.18 = (bf16[2,256,128]{2,1,0:T(8,128)(2,1)S(1)}, bf16[2,256,128]{2,1,0:T(8,128)(2,1)S(1)}, u32[]{:S(2)}, u32[]{:S(2)}) collective-permute-start(bf16[2,256,128]{2,1,0:T(8,128)(2,1)S(1)} %get-tuple-element.76), channel_id=1, source_target_pairs={{0,12},{4,8},{8,4},{12,0},{1,13},{5,9},{9,5},{13,1},{2,14},{6,10},... | collective-permute-start | bytes 393224 | tf_op jit(solution)/shard_map/ppermute | solution.py:440

commit v4 on v3

--- a/solution.py
+++ b/solution.py
@@ -126,19 +126,13 @@
         total_ref[slot, 1] = totals[0][vectors:] - totals[1][:vectors]
 
 
-def last_kernel(normalize, meta_ref, outer_ref, total_ref, last_ref, keep_ref, send_ref):
+def last_kernel(normalize, slot, meta_ref, outer_ref, total_ref, last_ref, out_ref):
     vectors = last_ref.shape[-1]
-    for slot, out in ((1, send_ref), (0, keep_ref)):
-        at = 2 * slot * vectors
-        both = jnp.dot(
-            outer_ref[0, at : at + 2 * vectors, :],
-            last_ref[0],
-            preferred_element_type=jnp.float32,
-        )
-        real = total_ref[slot, 0] + both[vectors:]
-        imag = total_ref[slot, 1] - both[:vectors]
-        out[meta_ref[1]] = (real * normalize).astype(out.dtype)
-        out[1 - meta_ref[1]] = (imag * normalize).astype(out.dtype)
+    both = jnp.dot(outer_ref[0], last_ref[0], preferred_element_type=jnp.float32)
+    real = total_ref[slot, 0] + both[vectors:]
+    imag = total_ref[slot, 1] - both[:vectors]
+    out_ref[meta_ref[1]] = (real * normalize).astype(out_ref.dtype)
+    out_ref[1 - meta_ref[1]] = (imag * normalize).astype(out_ref.dtype)
 
 
 def deal_kernel(share, meta_ref, perams_ref, move_ref, *outs):
@@ -382,24 +376,25 @@
         compiler_params=pltpu.CompilerParams(vmem_limit_bytes=14 << 20),
         name="most",
     )(outer, inner, first, most)
-    keep, send = pl.pallas_call(
-        functools.partial(last_kernel, normalize),
-        grid=(1,),
-        in_specs=[
-            smem(),
-            pl.BlockSpec((1, 4 * vectors, sites), lambda i: (COLORS - 1, 0, 0)),
-            vmem(),
-            vmem(),
-        ],
-        out_specs=[vmem()] * 2,
-        out_shape=[
-            jax.ShapeDtypeStruct((2, vectors, vectors), f32),
-            jax.ShapeDtypeStruct((2, vectors, vectors), bf16),
-        ],
-        compiler_params=pltpu.CompilerParams(vmem_limit_bytes=10 << 20),
-        name="last",
-    )(meta, outer, total, last)
-
+
+    def finish(slot, dtype):
+        return pl.pallas_call(
+            functools.partial(last_kernel, normalize, slot),
+            grid=(1,),
+            in_specs=[
+                smem(),
+                pl.BlockSpec((1, 2 * vectors, sites), lambda i: (COLORS - 1, slot, 0)),
+                vmem(),
+                vmem(),
+            ],
+            out_specs=vmem(),
+            out_shape=jax.ShapeDtypeStruct((2, vectors, vectors), dtype),
+            compiler_params=pltpu.CompilerParams(vmem_limit_bytes=8 << 20),
+            name="last",
+        )(meta, outer, total, last)
+
+    send = finish(1, bf16)
+    keep = finish(0, f32)
     half = keep + swap(send, "spin", 1).astype(f32)
     quarter = half[0] + swap(half[1].astype(bf16), "slab", 1).astype(f32)
     distance = 4

time: 118 us -> 118 us (level)
    unnamed x32 -> x28, local copies, waits for them, and re-layouts: 5.16 us -> 4.53 us
where the time goes in v4:
time: 118 us
  waiting for transfers between devices  40.7 us (34%)
  starting transfers between devices  37.6 us (32%)
  Pallas kernels  29.2 us (25%)
  local copies, waits for them, and re-layouts  7.52 us (6%)
  between operations  1.64 us (1%)
    ppermute x12, waiting for transfers between devices, swap(): return lax.ppermute(x, axis, [(i, i ^ distance) for i in range(count)])  16.7 us
    ppermute x12, starting transfers between devices, swap(): return lax.ppermute(x, axis, [(i, i ^ distance) for i in range(count)])  15 us
    ppermute x6, starting transfers between devices, body(): piece = lax.ppermute(piece, 'slab', route)  15 us
    ppermute x6, waiting for transfers between devices, body(): piece = lax.ppermute(piece, 'slab', route)  14.9 us
    pallas_call x1, Pallas kernels, body(): pl.pallas_call(field_kernel, grid=(sites // block,), in_specs=[smem(), pl...  14.2 us
    ppermute x4, waiting for transfers between devices, shift(): return lax.ppermute(x, axis, [(i, (i + by) % count) for i in range(count)])  9.08 us
    ppermute x4, starting transfers between devices, shift(): return lax.ppermute(x, axis, [(i, (i + by) % count) for i in range(count)])  7.65 us
    unnamed x28, local copies, waits for them, and re-layouts  4.53 us
  transfers between devices with their start and end apart: 22, of which 11 were waited for; matrix products, arithmetic and copies ran while one was open for 3% of the time, Pallas kernels for 21%

profile of v4, /device:TPU:0, one launch (start us, length us, event | category | flops | bytes accessed | tf_op | source)
XLA Modules:
  0.0 117.6 jit_solution(4008015292455546076)
XLA Ops:
  0.0 1.8 %edge.2 = bf16[1,512,256]{2,1,0:T(8,128)(2,1)} custom-call(bf16[2,3,2,512,256]{4,3,2,1,0:T(8,128)(2,1)} %bitcast.21), custom_call_target="tpu_custom_call" | custom-call | tf_op jit(solution)/shard_map/edge/pallas_call | solution.py:267
  1.8 0.0 copy-start.2
  1.8 5.1 %collective-permute-start = (bf16[1,512,256]{2,1,0:T(8,128)(2,1)}, bf16[1,512,256]{2,1,0:T(8,128)(2,1)S(1)}, u32[]{:S(2)}, u32[]{:S(2)}) collective-permute-start(bf16[1,512,256]{2,1,0:T(8,128)(2,1)} %edge.2), channel_id=1, source_target_pairs={{0,12},{4,0},{8,4},{12,8},{1,13},{5,1},{9,5},{13,9},{2,14},{6,2},{... | collective-permute-start | bytes 786440 | tf_op jit(solution)/shard_map/ppermute | solution.py:22
  6.9 2.3 %edge.3 = (bf16[4,512,256]{2,1,0:T(8,128)(2,1)}, bf16[1,512,256]{2,1,0:T(8,128)(2,1)}) custom-call(bf16[2,3,2,512,256]{4,3,2,1,0:T(8,128)(2,1)} %bitcast.22), custom_call_target="tpu_custom_call" | custom-call | tf_op jit(solution)/shard_map/edge/pallas_call | solution.py:267
  9.3 0.5 collective-permute-start.2
  9.8 0.4 collective-permute-start.1
  10.3 0.1 rev.7
  10.4 0.2 slice_reduce_fusion.2
  10.7 0.1 fusion.17
  10.8 0.1 pad_add_fusion.1.place_ref
  10.8 0.7 fusion.20
  11.5 0.1 fusion.8
  11.6 0.2 fusion.5
  11.8 0.1 pad_add_fusion.place_ref
  11.9 0.7 fusion.19
  13.9 1.3 %stack.21.meta_ref = s32[7]{0:T(128)S(1)} concatenate(s32[1]{0:T(128)} %bitcast, s32[1]{0:T(128)} %bitcast.1, s32[1]{0:T(128)} %bitcast.2, s32[1]{0:T(128)} %bitcast.3, s32[1]{0:T(128)} %bitcast.4, s32[2]{0:T(128)S(1)} %copy-done.12), dimensions={0} | concatenate | bytes 56 | tf_op jit(solution)/shard_map/stack | solution.py:312
  15.2 0.1 fusion.2
  15.3 1.2 %deal.1 = (bf16[2,256,128]{2,1,0:T(8,128)(2,1)S(1)}, bf16[2,256,128]{2,1,0:T(8,128)(2,1)S(1)}, bf16[2,256,128]{2,1,0:T(8,128)(2,1)S(1)}, bf16[2,256,128]{2,1,0:T...) custom-call(s32[7]{0:T(128)S(1)} %stack.21.meta_ref, ...), custom_call_target="tpu_custom_call" | custom-call | tf_op jit(solution)/shard_map/deal/pallas_call | solution.py:361
  16.6 0.6 copy-done.3
  17.2 0.6 copy-done.5
  17.9 0.6 copy-done.7
  18.5 0.6 copy-done.9
  19.2 1.9 %copy-done = bf16[1,2,3,2,512,256]{5,4,3,2,1,0:T(8,128)(2,1)S(1)} copy-done((bf16[1,2,3,2,512,256]{5,4,3,2,1,0:T(8,128)(2,1)S(1)}, bf16[1,2,3,2,512,256]{5,4,3,2,1,0:T(8,128)(2,1)}, u32[]{:S(2)}) %copy-start) | copy-done | bytes 3145752
  21.1 14.2 %fields.1 = (f32[1024,512]{1,0:T(8,128)S(1)}, bf16[3,1024,512]{2,1,0:T(8,128)(2,1)S(1)}) custom-call(s32[7]{0:T(128)S(1)} %stack.21.meta_ref, bf16[2,3,2,512,256]{4,3,2,1,0:T(8,128)(2,1)S(1)} %bitcast.23, f32[18,2,512]{2,1,0:T(2,128)S(1)} %bitcast.25, f32[4,2,512]{2,1,0:T(2,128)S(1)} %bitcast.26), custom_call_target="tpu_custom_call" | custom-call | tf_op jit(solution)/shard_map/fields/pallas_call | solution.py:336
  35.3 0.0 collective-permute-done.first_ref
  35.3 5.6 %collective-permute-done.1.most_ref = bf16[4,512,256]{2,1,0:T(8,128)(2,1)S(1)} collective-permute-done((bf16[4,512,256]{2,1,0:T(8,128)(2,1)}, bf16[4,512,256]{2,1,0:T(8,128)(2,1)S(1)}, u32[]{:S(2)}, u32[]{:S(2)}) %collective-permute-start.1) | collective-permute-done | bytes 1048608 | tf_op jit(solution)/shard_map/ppermute | solution.py:22
  40.9 1.5 %most.1.total_ref = f32[2,2,256,256]{3,2,1,0:T(8,128)S(1)} custom-call(bf16[3,1024,512]{2,1,0:T(8,128)(2,1)S(1)} %get-tuple-element.57.outer_ref, f32[1024,512]{1,0:T(8,128)S(1)} %get-tuple-element.58.inner_ref, bf16[1,512,256]{2,1,0:T(8,128)(2,1)S(1)} %collective-permute-done.first_ref, bf16[4,512,256]{2,1,0:T(8,128)(2,1)S(1)} %collective-permute-done.1.most_ref), custom_call_target="tpu_custom_call" | custom-call | tf_op jit(solution)/shard_map/most/pallas_call | solution.py:371
  42.4 0.0 collective-permute-done.2.last_ref
  42.4 0.8 last.3
  43.3 0.1 collective-permute-start.3
  43.4 0.9 last.2
  44.3 0.7 collective-permute-done.3
  44.9 0.1 convert_add_fusion
  45.0 0.4 collective-permute-start.4
  45.4 5.2 %collective-permute-done.4 = bf16[256,256]{1,0:T(8,128)(2,1)S(1)} collective-permute-done((bf16[256,256]{1,0:T(8,128)(2,1)S(1)}, bf16[256,256]{1,0:T(8,128)(2,1)S(1)}, u32[]{:S(2)}, u32[]{:S(2)}) %collective-permute-start.4) | collective-permute-done | bytes 131104 | tf_op jit(solution)/shard_map/ppermute | solution.py:27
  50.7 1.6 %collective-permute-start.5 = (bf16[256,256]{1,0:T(8,128)(2,1)S(1)}, bf16[256,256]{1,0:T(8,128)(2,1)S(1)}, u32[]{:S(2)}, u32[]{:S(2)}) collective-permute-start(bf16[256,256]{1,0:T(8,128)(2,1)S(1)} %fusion.3), channel_id=1, source_target_pairs={{0,2},{2,0},{1,3},{3,1},{4,6},{6,4},{5,7},{7,5},{8,10},{10,8},{9,1... | collective-permute-start | bytes 393224 | tf_op jit(solution)/shard_map/ppermute | solution.py:22
  52.2 3.5 %collective-permute-done.5 = bf16[256,256]{1,0:T(8,128)(2,1)S(1)} collective-permute-done((bf16[256,256]{1,0:T(8,128)(2,1)S(1)}, bf16[256,256]{1,0:T(8,128)(2,1)S(1)}, u32[]{:S(2)}, u32[]{:S(2)}) %collective-permute-start.5) | collective-permute-done | bytes 131104 | tf_op jit(solution)/shard_map/ppermute | solution.py:22
  55.7 3.1 %collective-permute-start.6 = (bf16[256,256]{1,0:T(8,128)(2,1)S(1)}, bf16[256,256]{1,0:T(8,128)(2,1)S(1)}, u32[]{:S(2)}, u32[]{:S(2)}) collective-permute-start(bf16[256,256]{1,0:T(8,128)(2,1)S(1)} %broadcast_select_fusion), channel_id=1, source_target_pairs={{0,8},{4,12},{8,0},{12,4},{1,9},{5,13},{9,1},{13,5},{2,10},{6,14},... | collective-permute-start | bytes 393224 | tf_op jit(solution)/shard_map/ppermute | solution.py:27
  58.8 4.9 %collective-permute-done.6 = bf16[256,256]{1,0:T(8,128)(2,1)S(1)} collective-permute-done((bf16[256,256]{1,0:T(8,128)(2,1)S(1)}, bf16[256,256]{1,0:T(8,128)(2,1)S(1)}, u32[]{:S(2)}, u32[]{:S(2)}) %collective-permute-start.6) | collective-permute-done | bytes 131104 | tf_op jit(solution)/shard_map/ppermute | solution.py:27
  63.7 0.1 add_convert_fusion.refs_0_
  63.7 0.8 collective-permute-start.7
  64.5 1.3 %collective-permute-start.14 = (bf16[2,256,128]{2,1,0:T(8,128)(2,1)S(1)}, bf16[2,256,128]{2,1,0:T(8,128)(2,1)S(1)}, u32[]{:S(2)}, u32[]{:S(2)}) collective-permute-start(bf16[2,256,128]{2,1,0:T(8,128)(2,1)S(1)} %copy-done.10), channel_id=1, source_target_pairs={{0,4},{4,0},{8,12},{12,8},{1,5},{5,1},{9,13},{13,9},{2,6},{6,2},{1... | collective-permute-start | bytes 393224 | tf_op jit(solution)/shard_map/ppermute | solution.py:27
  65.8 2.2 %collective-permute-start.15 = (bf16[2,256,128]{2,1,0:T(8,128)(2,1)S(1)}, bf16[2,256,128]{2,1,0:T(8,128)(2,1)S(1)}, u32[]{:S(2)}, u32[]{:S(2)}) collective-permute-start(bf16[2,256,128]{2,1,0:T(8,128)(2,1)S(1)} %copy-done.8), channel_id=1, source_target_pairs={{0,8},{4,12},{8,0},{12,4},{1,9},{5,13},{9,1},{13,5},{2,10},{6,14},... | collective-permute-start | bytes 393224 | tf_op jit(solution)/shard_map/ppermute | solution.py:27
  68.0 1.4 %collective-permute-start.16 = (bf16[2,256,128]{2,1,0:T(8,128)(2,1)S(1)}, bf16[2,256,128]{2,1,0:T(8,128)(2,1)S(1)}, u32[]{:S(2)}, u32[]{:S(2)}) collective-permute-start(bf16[2,256,128]{2,1,0:T(8,128)(2,1)S(1)} %copy-done.6), channel_id=1, source_target_pairs={{0,12},{4,8},{8,4},{12,0},{1,13},{5,9},{9,5},{13,1},{2,14},{6,10},... | collective-permute-start | bytes 393224 | tf_op jit(solution)/shard_map/ppermute | solution.py:27
  69.4 0.0 collective-permute-start.8
  69.4 0.7 collective-permute-done.7.refs_1_
  70.2 2.0 %collective-permute-done.14.refs_5_ = bf16[2,256,128]{2,1,0:T(8,128)(2,1)S(1)} collective-permute-done((bf16[2,256,128]{2,1,0:T(8,128)(2,1)S(1)}, bf16[2,256,128]{2,1,0:T(8,128)(2,1)S(1)}, u32[]{:S(2)}, u32[]{:S(2)}) %collective-permute-start.14) | collective-permute-done | bytes 131104 | tf_op jit(solution)/shard_map/ppermute | solution.py:27
  72.2 0.4 collective-permute-start.10
  72.6 2.0 %collective-permute-done.15.refs_6_ = bf16[2,256,128]{2,1,0:T(8,128)(2,1)S(1)} collective-permute-done((bf16[2,256,128]{2,1,0:T(8,128)(2,1)S(1)}, bf16[2,256,128]{2,1,0:T(8,128)(2,1)S(1)}, u32[]{:S(2)}, u32[]{:S(2)}) %collective-permute-start.15) | collective-permute-done | bytes 131104 | tf_op jit(solution)/shard_map/ppermute | solution.py:27
  74.6 4.3 %collective-permute-start.11 = (bf16[2,256,128]{2,1,0:T(8,128)(2,1)S(1)}, bf16[2,256,128]{2,1,0:T(8,128)(2,1)S(1)}, u32[]{:S(2)}, u32[]{:S(2)}) collective-permute-start(bf16[2,256,128]{2,1,0:T(8,128)(2,1)S(1)} %get-tuple-element.64), channel_id=1, source_target_pairs={{0,8},{4,12},{8,0},{12,4},{1,9},{5,13},{9,1},{13,5},{2,10},{6,14},... | collective-permute-start | bytes 393224 | tf_op jit(solution)/shard_map/ppermute | solution.py:27
  78.9 1.2 collective-permute-done.16.refs_7_
  80.1 1.0 collective-permute-start.12
  81.1 1.7 %blocks.3 = (bf16[2,256,128]{2,1,0:T(8,128)(2,1)S(1)}, bf16[2,256,128]{2,1,0:T(8,128)(2,1)S(1)}, bf16[2,256,128]{2,1,0:T(8,128)(2,1)S(1)}, bf16[2,256,128]{2,1,0:T(8,128)(2,1)S(1)}) custom-call(s32[7]{0:T(128)S(1)} %stack.21.meta_ref, bf16[256,256]{1,0:T(8,128)(2,1)S(1)} %add_convert_fusion.refs_0_, bf16[256,256]{1,0:T(8,128)(2,1)S(1)} %collective-permute-done.7.refs_1_, ...), custom_call_target="tpu_custom_call" | custom-call | tf_op jit(solution)/shard_map/blocks/pallas_call | solution.py:419
  82.8 7.9 %collective-permute-start.21 = (bf16[2,256,128]{2,1,0:T(8,128)(2,1)S(1)}, bf16[2,256,128]{2,1,0:T(8,128)(2,1)S(1)}, u32[]{:S(2)}, u32[]{:S(2)}) collective-permute-start(bf16[2,256,128]{2,1,0:T(8,128)(2,1)S(1)} %get-tuple-element.78), channel_id=1, source_target_pairs={{0,4},{4,0},{8,12},{12,8},{1,5},{5,1},{9,13},{13,9},{2,6},{6,2},{1... | collective-permute-start | bytes 393224 | tf_op jit(solution)/shard_map/ppermute | solution.py:435
  90.7 1.7 %blocks.2 = (bf16[2,256,128]{2,1,0:T(8,128)(2,1)S(1)}, bf16[2,256,128]{2,1,0:T(8,128)(2,1)S(1)}, bf16[2,256,128]{2,1,0:T(8,128)(2,1)S(1)}, bf16[2,256,128]{2,1,0:T(8,128)(2,1)S(1)}) custom-call(s32[7]{0:T(128)S(1)} %stack.21.meta_ref, bf16[256,256]{1,0:T(8,128)(2,1)S(1)} %add_convert_fusion.refs_0_, bf16[256,256]{1,0:T(8,128)(2,1)S(1)} %collective-permute-done.7.refs_1_, ...), custom_call_target="tpu_custom_call" | custom-call | tf_op jit(solution)/shard_map/blocks/pallas_call | solution.py:419
  92.4 1.2 %collective-permute-start.20 = (bf16[2,256,128]{2,1,0:T(8,128)(2,1)S(1)}, bf16[2,256,128]{2,1,0:T(8,128)(2,1)S(1)}, u32[]{:S(2)}, u32[]{:S(2)}) collective-permute-start(bf16[2,256,128]{2,1,0:T(8,128)(2,1)S(1)} %get-tuple-element.77), channel_id=1, source_target_pairs={{0,4},{4,0},{8,12},{12,8},{1,5},{5,1},{9,13},{13,9},{2,6},{6,2},{1... | collective-permute-start | bytes 393224 | tf_op jit(solution)/shard_map/ppermute | solution.py:435
  93.6 1.5 %collective-permute-start.17 = (bf16[2,256,128]{2,1,0:T(8,128)(2,1)S(1)}, bf16[2,256,128]{2,1,0:T(8,128)(2,1)S(1)}, u32[]{:S(2)}, u32[]{:S(2)}) collective-permute-start(bf16[2,256,128]{2,1,0:T(8,128)(2,1)S(1)} %get-tuple-element.71), channel_id=1, source_target_pairs={{0,8},{4,12},{8,0},{12,4},{1,9},{5,13},{9,1},{13,5},{2,10},{6,14},... | collective-permute-start | bytes 393224 | tf_op jit(solution)/shard_map/ppermute | solution.py:435
  95.2 1.7 %collective-permute-start.19 = (bf16[2,256,128]{2,1,0:T(8,128)(2,1)S(1)}, bf16[2,256,128]{2,1,0:T(8,128)(2,1)S(1)}, u32[]{:S(2)}, u32[]{:S(2)}) collective-permute-start(bf16[2,256,128]{2,1,0:T(8,128)(2,1)S(1)} %get-tuple-element.73), channel_id=1, source_target_pairs={{0,12},{4,8},{8,4},{12,0},{1,13},{5,9},{9,5},{13,1},{2,14},{6,10},... | collective-permute-start | bytes 393224 | tf_op jit(solution)/shard_map/ppermute | solution.py:435
  96.8 1.7 %collective-permute-start.13 = (bf16[2,256,128]{2,1,0:T(8,128)(2,1)S(1)}, bf16[2,256,128]{2,1,0:T(8,128)(2,1)S(1)}, u32[]{:S(2)}, u32[]{:S(2)}) collective-permute-start(bf16[2,256,128]{2,1,0:T(8,128)(2,1)S(1)} %get-tuple-element.66), channel_id=1, source_target_pairs={{0,8},{4,12},{8,0},{12,4},{1,9},{5,13},{9,1},{13,5},{2,10},{6,14},... | collective-permute-start | bytes 393224 | tf_op jit(solution)/shard_map/ppermute | solution.py:435
  98.6 0.9 collective-permute-start.18
  99.5 1.6 %join.2.refs_4_ = bf16[2,2,512,256]{3,2,1,0:T(8,128)(2,1)} custom-call(s32[4]{0:T(128)S(1)} %pad_add_fusion.place_ref, bf16[256,256]{1,0:T(8,128)(2,1)S(1)} %get-tuple-element.43.move_ref, bf16[2,256,128]{2,1,0:T(8,128)(2,1)S(1)} %get-tuple-element.75.refs_0_, bf16[2,256,128]{2,1,0:T(8,128)(2,1)S(1)} %get-tuple-element.76.refs_1_, ...), custom_call_target="tpu_custom_call" | custom-call | tf_op jit(solution)/shard_map/join/pallas_call | solution.py:443
  101.1 9.3 %collective-permute-done.17.refs_1_ = bf16[2,256,128]{2,1,0:T(8,128)(2,1)S(1)} collective-permute-done((bf16[2,256,128]{2,1,0:T(8,128)(2,1)S(1)}, bf16[2,256,128]{2,1,0:T(8,128)(2,1)S(1)}, u32[]{:S(2)}, u32[]{:S(2)}) %collective-permute-start.17) | collective-permute-done | bytes 131104 | tf_op jit(solution)/shard_map/ppermute | solution.py:435
  110.4 5.6 %collective-permute-done.13.refs_0_ = bf16[2,256,128]{2,1,0:T(8,128)(2,1)S(1)} collective-permute-done((bf16[2,256,128]{2,1,0:T(8,128)(2,1)S(1)}, bf16[2,256,128]{2,1,0:T(8,128)(2,1)S(1)}, u32[]{:S(2)}, u32[]{:S(2)}) %collective-permute-start.13) | collective-permute-done | bytes 131104 | tf_op jit(solution)/shard_map/ppermute | solution.py:435
  116.0 1.6 %join.3 = bf16[2,2,512,256]{3,2,1,0:T(8,128)(2,1)} custom-call(s32[4]{0:T(128)S(1)} %pad_add_fusion.1.place_ref, bf16[256,256]{1,0:T(8,128)(2,1)S(1)} %get-tuple-element.43.move_ref, bf16[2,256,128]{2,1,0:T(8,128)(2,1)S(1)} %collective-permute-done.13.refs_0_, ...), custom_call_target="tpu_custom_call", output_to_operand_aliasing={{}: (6, {})} | custom-call | tf_op jit(solution)/shard_map/join/pallas_call | solution.py:443
  (45 shorter events, 0.2 us)
Async XLA Ops:
  0.0 10.3 %copy-start.12 = (s32[2]{0:T(128)S(1)}, s32[2]{0:T(128)}, u32[]{:S(2)}) copy-start(s32[2]{0:T(128)} %param.9) | copy-start | bytes 28
  0.0 10.4 %copy-start.11 = (s32[2,3]{1,0:T(2,128)S(1)}, s32[2,3]{1,0:T(2,128)}, u32[]{:S(2)}) copy-start(s32[2,3]{1,0:T(2,128)} %param.8) | copy-start | bytes 76
  0.0 10.6 %copy-start.13 = (s32[2,2]{1,0:T(2,128)S(1)}, s32[2,2]{1,0:T(2,128)}, u32[]{:S(2)}) copy-start(s32[2,2]{1,0:T(2,128)} %param.10) | copy-start | bytes 52
  0.0 15.3 %copy-start.1 = (bf16[2,2,512,256]{3,2,1,0:T(8,128)(2,1)S(1)}, bf16[2,2,512,256]{3,2,1,0:T(8,128)(2,1)}, u32[]{:S(2)}) copy-start(bf16[2,2,512,256]{3,2,1,0:T(8,128)(2,1)} %param.11) | copy-start | bytes 3145732
  1.8 17.4 %copy-start.2 = (f32[1,2,3,3,2,512]{5,4,3,2,1,0:T(2,128)S(1)}, f32[1,2,3,3,2,512]{5,4,3,2,1,0:T(2,128)}, u32[]{:S(2)}) copy-start(f32[1,2,3,3,2,512]{5,4,3,2,1,0:T(2,128)} %param.7) | copy-start | bytes 221188
  1.8 33.5 %collective-permute-start = (bf16[1,512,256]{2,1,0:T(8,128)(2,1)}, bf16[1,512,256]{2,1,0:T(8,128)(2,1)S(1)}, u32[]{:S(2)}, u32[]{:S(2)}) collective-permute-start(bf16[1,512,256]{2,1,0:T(8,128)(2,1)} %edge.2), channel_id=1, source_target_pairs={{0,12},{4,0},{8,4},{12,8},{1,13},{5,1},{9,5},{13,9},{2,14},{6,2},{... | collective-permute-start | bytes 786440 | tf_op jit(solution)/shard_map/ppermute | solution.py:22
  9.3 33.1 %collective-permute-start.2 = (bf16[1,512,256]{2,1,0:T(8,128)(2,1)}, bf16[1,512,256]{2,1,0:T(8,128)(2,1)S(1)}, u32[]{:S(2)}, u32[]{:S(2)}) collective-permute-start(bf16[1,512,256]{2,1,0:T(8,128)(2,1)} %get-tuple-element.60), channel_id=1, source_target_pairs={{0,12},{4,0},{8,4},{12,8},{1,13},{5,1},{9,5},{13,9},{2,14},{6,2},{... | collective-permute-start | bytes 786440 | tf_op jit(solution)/shard_map/ppermute | solution.py:22
  9.8 31.1 %collective-permute-start.1 = (bf16[4,512,256]{2,1,0:T(8,128)(2,1)}, bf16[4,512,256]{2,1,0:T(8,128)(2,1)S(1)}, u32[]{:S(2)}, u32[]{:S(2)}) collective-permute-start(bf16[4,512,256]{2,1,0:T(8,128)(2,1)} %get-tuple-element.59), channel_id=1, source_target_pairs={{0,12},{4,0},{8,4},{12,8},{1,13},{5,1},{9,5},{13,9},{2,14},{6,2},{... | collective-permute-start | bytes 3145736 | tf_op jit(solution)/shard_map/ppermute | solution.py:22
  16.6 0.7 copy-start.3
  17.2 0.7 copy-start.5
  17.9 0.6 copy-start.7
  18.5 0.7 copy-start.9
  19.2 1.9 %copy-start = (bf16[1,2,3,2,512,256]{5,4,3,2,1,0:T(8,128)(2,1)S(1)}, bf16[1,2,3,2,512,256]{5,4,3,2,1,0:T(8,128)(2,1)}, u32[]{:S(2)}) copy-start(bf16[1,2,3,2,512,256]{5,4,3,2,1,0:T(8,128)(2,1)} %param.6) | copy-start | bytes 9437188
  43.3 21.2 %copy-start.10 = (bf16[2,256,128]{2,1,0:T(8,128)(2,1)S(1)}, bf16[2,256,128]{2,1,0:T(8,128)(2,1)}, u32[]{:S(2)}) copy-start(bf16[2,256,128]{2,1,0:T(8,128)(2,1)} %copy-done.9) | copy-start | bytes 393220
  43.3 22.5 %copy-start.8 = (bf16[2,256,128]{2,1,0:T(8,128)(2,1)S(1)}, bf16[2,256,128]{2,1,0:T(8,128)(2,1)}, u32[]{:S(2)}) copy-start(bf16[2,256,128]{2,1,0:T(8,128)(2,1)} %copy-done.7) | copy-start | bytes 393220
  43.3 24.7 %copy-start.6 = (bf16[2,256,128]{2,1,0:T(8,128)(2,1)S(1)}, bf16[2,256,128]{2,1,0:T(8,128)(2,1)}, u32[]{:S(2)}) copy-start(bf16[2,256,128]{2,1,0:T(8,128)(2,1)} %copy-done.5) | copy-start | bytes 393220
  43.3 28.9 %copy-start.4 = (bf16[2,256,128]{2,1,0:T(8,128)(2,1)S(1)}, bf16[2,256,128]{2,1,0:T(8,128)(2,1)}, u32[]{:S(2)}) copy-start(bf16[2,256,128]{2,1,0:T(8,128)(2,1)} %copy-done.3) | copy-start | bytes 393220
  43.3 1.6 %collective-permute-start.3 = (bf16[2,256,256]{2,1,0:T(8,128)(2,1)S(1)}, bf16[2,256,256]{2,1,0:T(8,128)(2,1)S(1)}, u32[]{:S(2)}, u32[]{:S(2)}) collective-permute-start(bf16[2,256,256]{2,1,0:T(8,128)(2,1)S(1)} %last.3), channel_id=1, source_target_pairs={{0,1},{1,0},{2,3},{3,2},{4,5},{5,4},{6,7},{7,6},{8,9},{9,8},{10,11... | collective-permute-start | bytes 786440 | tf_op jit(solution)/shard_map/ppermute | solution.py:27
  45.0 5.6 %collective-permute-start.4 = (bf16[256,256]{1,0:T(8,128)(2,1)S(1)}, bf16[256,256]{1,0:T(8,128)(2,1)S(1)}, u32[]{:S(2)}, u32[]{:S(2)}) collective-permute-start(bf16[256,256]{1,0:T(8,128)(2,1)S(1)} %fusion.4), channel_id=1, source_target_pairs={{0,4},{4,0},{8,12},{12,8},{1,5},{5,1},{9,13},{13,9},{2,6},{6,2},{1... | collective-permute-start | bytes 393224 | tf_op jit(solution)/shard_map/ppermute | solution.py:27
  50.7 5.0 %collective-permute-start.5 = (bf16[256,256]{1,0:T(8,128)(2,1)S(1)}, bf16[256,256]{1,0:T(8,128)(2,1)S(1)}, u32[]{:S(2)}, u32[]{:S(2)}) collective-permute-start(bf16[256,256]{1,0:T(8,128)(2,1)S(1)} %fusion.3), channel_id=1, source_target_pairs={{0,2},{2,0},{1,3},{3,1},{4,6},{6,4},{5,7},{7,5},{8,10},{10,8},{9,1... | collective-permute-start | bytes 393224 | tf_op jit(solution)/shard_map/ppermute | solution.py:22
  55.7 7.9 %collective-permute-start.6 = (bf16[256,256]{1,0:T(8,128)(2,1)S(1)}, bf16[256,256]{1,0:T(8,128)(2,1)S(1)}, u32[]{:S(2)}, u32[]{:S(2)}) collective-permute-start(bf16[256,256]{1,0:T(8,128)(2,1)S(1)} %broadcast_select_fusion), channel_id=1, source_target_pairs={{0,8},{4,12},{8,0},{12,4},{1,9},{5,13},{9,1},{13,5},{2,10},{6,14},... | collective-permute-start | bytes 393224 | tf_op jit(solution)/shard_map/ppermute | solution.py:27
  63.7 6.4 %collective-permute-start.7 = (bf16[256,256]{1,0:T(8,128)(2,1)S(1)}, bf16[256,256]{1,0:T(8,128)(2,1)S(1)}, u32[]{:S(2)}, u32[]{:S(2)}) collective-permute-start(bf16[256,256]{1,0:T(8,128)(2,1)S(1)} %add_convert_fusion.refs_0_), channel_id=1, source_target_pairs={{0,4},{4,0},{8,12},{12,8},{1,5},{5,1},{9,13},{13,9},{2,6},{6,2},{1... | collective-permute-start | bytes 393224 | tf_op jit(solution)/shard_map/ppermute | solution.py:27
  64.5 7.7 %collective-permute-start.14 = (bf16[2,256,128]{2,1,0:T(8,128)(2,1)S(1)}, bf16[2,256,128]{2,1,0:T(8,128)(2,1)S(1)}, u32[]{:S(2)}, u32[]{:S(2)}) collective-permute-start(bf16[2,256,128]{2,1,0:T(8,128)(2,1)S(1)} %copy-done.10), channel_id=1, source_target_pairs={{0,4},{4,0},{8,12},{12,8},{1,5},{5,1},{9,13},{13,9},{2,6},{6,2},{1... | collective-permute-start | bytes 393224 | tf_op jit(solution)/shard_map/ppermute | solution.py:27
  65.8 8.8 %collective-permute-start.15 = (bf16[2,256,128]{2,1,0:T(8,128)(2,1)S(1)}, bf16[2,256,128]{2,1,0:T(8,128)(2,1)S(1)}, u32[]{:S(2)}, u32[]{:S(2)}) collective-permute-start(bf16[2,256,128]{2,1,0:T(8,128)(2,1)S(1)} %copy-done.8), channel_id=1, source_target_pairs={{0,8},{4,12},{8,0},{12,4},{1,9},{5,13},{9,1},{13,5},{2,10},{6,14},... | collective-permute-start | bytes 393224 | tf_op jit(solution)/shard_map/ppermute | solution.py:27
  68.0 12.1 %collective-permute-start.16 = (bf16[2,256,128]{2,1,0:T(8,128)(2,1)S(1)}, bf16[2,256,128]{2,1,0:T(8,128)(2,1)S(1)}, u32[]{:S(2)}, u32[]{:S(2)}) collective-permute-start(bf16[2,256,128]{2,1,0:T(8,128)(2,1)S(1)} %copy-done.6), channel_id=1, source_target_pairs={{0,12},{4,8},{8,4},{12,0},{1,13},{5,9},{9,5},{13,1},{2,14},{6,10},... | collective-permute-start | bytes 393224 | tf_op jit(solution)/shard_map/ppermute | solution.py:27
  69.4 11.7 %collective-permute-start.8 = (bf16[256,256]{1,0:T(8,128)(2,1)S(1)}, bf16[256,256]{1,0:T(8,128)(2,1)S(1)}, u32[]{:S(2)}, u32[]{:S(2)}) collective-permute-start(bf16[256,256]{1,0:T(8,128)(2,1)S(1)} %add_convert_fusion.refs_0_), channel_id=1, source_target_pairs={{0,1},{1,0},{2,3},{3,2},{4,5},{5,4},{6,7},{7,6},{8,9},{9,8},{10,11... | collective-permute-start | bytes 393224 | tf_op jit(solution)/shard_map/ppermute | solution.py:27
  70.2 11.0 %collective-permute-start.9 = (bf16[256,256]{1,0:T(8,128)(2,1)S(1)}, bf16[256,256]{1,0:T(8,128)(2,1)S(1)}, u32[]{:S(2)}, u32[]{:S(2)}) collective-permute-start(bf16[256,256]{1,0:T(8,128)(2,1)S(1)} %collective-permute-done.7.refs_1_), channel_id=1, source_target_pairs={{0,1},{1,0},{2,3},{3,2},{4,5},{5,4},{6,7},{7,6},{8,9},{9,8},{10,11... | collective-permute-start | bytes 393224 | tf_op jit(solution)/shard_map/ppermute | solution.py:27
  72.2 18.5 %collective-permute-start.10 = (bf16[2,256,128]{2,1,0:T(8,128)(2,1)S(1)}, bf16[2,256,128]{2,1,0:T(8,128)(2,1)S(1)}, u32[]{:S(2)}, u32[]{:S(2)}) collective-permute-start(bf16[2,256,128]{2,1,0:T(8,128)(2,1)S(1)} %copy-done.4), channel_id=1, source_target_pairs={{0,4},{4,0},{8,12},{12,8},{1,5},{5,1},{9,13},{13,9},{2,6},{6,2},{1... | collective-permute-start | bytes 393224 | tf_op jit(solution)/shard_map/ppermute | solution.py:27
  74.6 16.1 %collective-permute-start.11 = (bf16[2,256,128]{2,1,0:T(8,128)(2,1)S(1)}, bf16[2,256,128]{2,1,0:T(8,128)(2,1)S(1)}, u32[]{:S(2)}, u32[]{:S(2)}) collective-permute-start(bf16[2,256,128]{2,1,0:T(8,128)(2,1)S(1)} %get-tuple-element.64), channel_id=1, source_target_pairs={{0,8},{4,12},{8,0},{12,4},{1,9},{5,13},{9,1},{13,5},{2,10},{6,14},... | collective-permute-start | bytes 393224 | tf_op jit(solution)/shard_map/ppermute | solution.py:27
  80.1 10.6 %collective-permute-start.12 = (bf16[2,256,128]{2,1,0:T(8,128)(2,1)S(1)}, bf16[2,256,128]{2,1,0:T(8,128)(2,1)S(1)}, u32[]{:S(2)}, u32[]{:S(2)}) collective-permute-start(bf16[2,256,128]{2,1,0:T(8,128)(2,1)S(1)} %get-tuple-element.65), channel_id=1, source_target_pairs={{0,12},{4,8},{8,4},{12,0},{1,13},{5,9},{9,5},{13,1},{2,14},{6,10},... | collective-permute-start | bytes 393224 | tf_op jit(solution)/shard_map/ppermute | solution.py:27
  82.8 15.8 %collective-permute-start.21 = (bf16[2,256,128]{2,1,0:T(8,128)(2,1)S(1)}, bf16[2,256,128]{2,1,0:T(8,128)(2,1)S(1)}, u32[]{:S(2)}, u32[]{:S(2)}) collective-permute-start(bf16[2,256,128]{2,1,0:T(8,128)(2,1)S(1)} %get-tuple-element.78), channel_id=1, source_target_pairs={{0,4},{4,0},{8,12},{12,8},{1,5},{5,1},{9,13},{13,9},{2,6},{6,2},{1... | collective-permute-start | bytes 393224 | tf_op jit(solution)/shard_map/ppermute | solution.py:435
  92.4 7.1 %collective-permute-start.20 = (bf16[2,256,128]{2,1,0:T(8,128)(2,1)S(1)}, bf16[2,256,128]{2,1,0:T(8,128)(2,1)S(1)}, u32[]{:S(2)}, u32[]{:S(2)}) collective-permute-start(bf16[2,256,128]{2,1,0:T(8,128)(2,1)S(1)} %get-tuple-element.77), channel_id=1, source_target_pairs={{0,4},{4,0},{8,12},{12,8},{1,5},{5,1},{9,13},{13,9},{2,6},{6,2},{1... | collective-permute-start | bytes 393224 | tf_op jit(solution)/shard_map/ppermute | solution.py:435
  93.6 16.8 %collective-permute-start.17 = (bf16[2,256,128]{2,1,0:T(8,128)(2,1)S(1)}, bf16[2,256,128]{2,1,0:T(8,128)(2,1)S(1)}, u32[]{:S(2)}, u32[]{:S(2)}) collective-permute-start(bf16[2,256,128]{2,1,0:T(8,128)(2,1)S(1)} %get-tuple-element.71), channel_id=1, source_target_pairs={{0,8},{4,12},{8,0},{12,4},{1,9},{5,13},{9,1},{13,5},{2,10},{6,14},... | collective-permute-start | bytes 393224 | tf_op jit(solution)/shard_map/ppermute | solution.py:435
  95.2 15.2 %collective-permute-start.19 = (bf16[2,256,128]{2,1,0:T(8,128)(2,1)S(1)}, bf16[2,256,128]{2,1,0:T(8,128)(2,1)S(1)}, u32[]{:S(2)}, u32[]{:S(2)}) collective-permute-start(bf16[2,256,128]{2,1,0:T(8,128)(2,1)S(1)} %get-tuple-element.73), channel_id=1, source_target_pairs={{0,12},{4,8},{8,4},{12,0},{1,13},{5,9},{9,5},{13,1},{2,14},{6,10},... | collective-permute-start | bytes 393224 | tf_op jit(solution)/shard_map/ppermute | solution.py:435
  96.8 19.2 %collective-permute-start.13 = (bf16[2,256,128]{2,1,0:T(8,128)(2,1)S(1)}, bf16[2,256,128]{2,1,0:T(8,128)(2,1)S(1)}, u32[]{:S(2)}, u32[]{:S(2)}) collective-permute-start(bf16[2,256,128]{2,1,0:T(8,128)(2,1)S(1)} %get-tuple-element.66), channel_id=1, source_target_pairs={{0,8},{4,12},{8,0},{12,4},{1,9},{5,13},{9,1},{13,5},{2,10},{6,14},... | collective-permute-start | bytes 393224 | tf_op jit(solution)/shard_map/ppermute | solution.py:435
  98.6 17.4 %collective-permute-start.18 = (bf16[2,256,128]{2,1,0:T(8,128)(2,1)S(1)}, bf16[2,256,128]{2,1,0:T(8,128)(2,1)S(1)}, u32[]{:S(2)}, u32[]{:S(2)}) collective-permute-start(bf16[2,256,128]{2,1,0:T(8,128)(2,1)S(1)} %get-tuple-element.72), channel_id=1, source_target_pairs={{0,12},{4,8},{8,4},{12,0},{1,13},{5,9},{9,5},{13,1},{2,14},{6,10},... | collective-permute-start | bytes 393224 | tf_op jit(solution)/shard_map/ppermute | solution.py:435
